TPU v7x, 768 devices: a whole 4x8x12 slice. The times are simulated.
768 devices in a mesh: seq: 32 (over x, y), head: 24 (over z, core).
Axes of the slice: x: 4, y: 8, z: 12, core: 2. Of those that a mesh axis runs over, the one named last changes fastest.
Arguments:
- queries: bfloat16 [16384, 3072], P('seq', 'head'), may hold values from -6 to 6
- key_rows: bfloat16 [16384, 3072], P('seq', 'head'), may hold values from -6 to 6
- value_rows: bfloat16 [16384, 3072], P('seq', 'head'), may hold values from -6 to 6
- upstream: bfloat16 [16384, 3072], P('seq', 'head'), may hold values from -6 to 6
- exit_weight: bfloat16 [3072], P('head'), may hold values from -4 to 4
- labels: int32 [16384], P('seq'), may hold values 0 or 1
- rand_blocks: int32 [256, 3], replicated, may hold values from 0 to 255, as said below
- glob_blocks: int32 [2], replicated, may hold values from 0 to 255, as said below
Outputs:
- attended: bfloat16 [16384, 3072], P('seq', 'head')
- token_loss: float32 [16384], P('seq')
- grad_query: float32 [16384, 3072], P('seq', 'head')
- grad_key: float32 [16384, 3072], P('seq', 'head')
- grad_value: float32 [16384, 3072], P('seq', 'head')
Inputs may be any that keep to these rules, and one draw needn't show every extreme that they name: `rand_blocks`: among the 24 entries of the rows of one device (aligned groups of 8 rows), at most 1 lie in any one aligned range of 8 key blocks, and some range holds exactly 1. `glob_blocks`: 2 distinct blocks, the same for every query block; the document's last block is always among them.
All inputs are finite; a program needn't handle non-finite values. No bound on the sum of `labels` on one device may be relied on, other than what follows from the above.
Results may differ from a plain program's by a relative error of at most 0.018.
Values may be sent and summed in bfloat16 or wider, within the bound.
No kernel may reach another device: no remote copies, remote signals or barrier semaphores. Data moves between devices by JAX's collectives and lax.ppermute only.
A program may use at most 64 MiB of HBM per device.

v0:
```python
import math

import jax
import jax.numpy as jnp
from jax import lax
from jax.sharding import PartitionSpec as P

BLOCK = 64
RAND = 3
GLOBAL = 2


def spread(x, axis, root):
    mine = lax.axis_index(axis) == root
    return lax.psum(jnp.where(mine, x, jnp.zeros_like(x)), axis)


def slot_tables(rand_blocks, blocks, shards):
    requests = rand_blocks.reshape(shards, blocks * RAND)
    starts = jnp.arange(shards, dtype=jnp.int32) * blocks
    total_blocks = blocks * shards
    behind = (starts - 1) % total_blocks
    beyond = (starts + blocks) % total_blocks
    requests = jnp.concatenate([requests, behind[:, None], beyond[:, None]], axis=1)
    owners = requests // blocks
    offsets = requests % blocks
    onehot = (owners[:, :, None] == jnp.arange(shards, dtype=jnp.int32)[None, None, :]).astype(
        jnp.int32
    )
    ranking = jnp.sum(onehot * jnp.cumsum(onehot, axis=1), axis=2) - 1
    return (owners, offsets, ranking)


def body(queries, key_rows, value_rows, upstream, exit_weight, labels, rand_blocks, glob_blocks):
    tokens, head_dim = queries.shape
    blocks = tokens // BLOCK
    shards = lax.axis_size("seq")
    myself = lax.axis_index("seq")
    total_blocks = blocks * shards
    kv_width = 2 * head_dim
    slot_count = 3 + RAND + GLOBAL
    inv_sqrt = 1.0 / math.sqrt(head_dim)
    rand_dev = blocks * RAND
    packed = jnp.concatenate([key_rows, value_rows], axis=1)
    local_kv = packed.reshape(blocks, BLOCK, kv_width)
    cap_rand = max(1, (rand_dev + shards - 1) // shards)
    capacity = cap_rand + 1
    owners, offsets, ranking = slot_tables(rand_blocks, blocks, shards)
    picked = (owners == myself)[:, :, None] & (
        ranking[:, :, None] == jnp.arange(capacity, dtype=jnp.int32)[None, None, :]
    )
    send_index = jnp.sum(jnp.where(picked, offsets[:, :, None], 0), axis=1)
    slot_used = jnp.any(picked, axis=1)
    outgoing = local_kv[send_index]
    incoming = lax.all_to_all(outgoing, "seq", split_axis=0, concat_axis=0, tiled=True)
    my_owner = lax.dynamic_index_in_dim(owners, myself, 0, keepdims=False)
    my_rank = lax.dynamic_index_in_dim(ranking, myself, 0, keepdims=False)
    slot_row = my_owner * capacity + my_rank
    fetched = incoming.reshape(shards * capacity, BLOCK, kv_width)[slot_row]
    randoms = fetched[:rand_dev].reshape(blocks, RAND, BLOCK, kv_width)
    extended = jnp.concatenate(
        [fetched[rand_dev][None], local_kv, fetched[rand_dev + 1][None]], axis=0
    )
    owner_glob = glob_blocks // blocks
    offset_glob = glob_blocks % blocks
    pieces = []
    for glob_no in range(GLOBAL):
        glob_piece = lax.dynamic_index_in_dim(local_kv, offset_glob[glob_no], 0, keepdims=False)
        pieces.append(spread(glob_piece, "seq", owner_glob[glob_no]))
    shared = jnp.stack(pieces)
    window = jnp.stack([extended[:blocks], extended[1 : blocks + 1], extended[2:]], axis=1)
    gathered_keys = jnp.concatenate(
        [window, randoms, jnp.broadcast_to(shared[None], (blocks, GLOBAL, BLOCK, kv_width))], axis=1
    )
    gathered_keys = gathered_keys.reshape(blocks, slot_count * BLOCK, kv_width)
    key_portion = gathered_keys[..., :head_dim]
    value_portion = gathered_keys[..., head_dim:]
    blocked_queries = queries.reshape(blocks, BLOCK, head_dim)
    block_ids = myself * blocks + jnp.arange(blocks, dtype=jnp.int32)
    slot_ok = jnp.concatenate(
        [
            (block_ids > 0)[:, None],
            jnp.ones((blocks, 1), bool),
            (block_ids < total_blocks - 1)[:, None],
            jnp.ones((blocks, RAND + GLOBAL), bool),
        ],
        axis=1,
    )
    key_ok = jnp.repeat(slot_ok, BLOCK, axis=1)
    attention_scores = (
        jnp.einsum("afs,ans->afn", blocked_queries, key_portion, preferred_element_type=jnp.float32)
        * inv_sqrt
    )
    attention_scores = jnp.where(key_ok[:, None, :], attention_scores, -jnp.inf)
    row_peak = jnp.max(attention_scores, axis=-1, keepdims=True)
    exp_terms = jnp.exp(attention_scores - row_peak)
    probs = exp_terms / jnp.sum(exp_terms, axis=-1, keepdims=True)
    reduced_probabilities = probs.astype(jnp.bfloat16)
    attended = (
        jnp.einsum(
            "omc,och->omh", reduced_probabilities, value_portion, preferred_element_type=jnp.float32
        )
        .astype(jnp.bfloat16)
        .reshape(tokens, head_dim)
    )
    partial_logit = jnp.dot(attended, exit_weight, preferred_element_type=jnp.float32)
    logits = lax.psum(partial_logit, "head")
    target = labels.astype(jnp.float32)
    token_loss = jax.nn.softplus(logits) - target * logits
    dlogits = jax.nn.sigmoid(logits) - target
    grad_out = (
        upstream.astype(jnp.float32) + dlogits[:, None] * exit_weight.astype(jnp.float32)[None, :]
    ).astype(jnp.bfloat16)
    block_gradient = grad_out.reshape(blocks, BLOCK, head_dim)
    probability_gradient = jnp.einsum(
        "afs,ans->afn", block_gradient, value_portion, preferred_element_type=jnp.float32
    )
    row_dot = jnp.sum(probs * probability_gradient, axis=-1, keepdims=True)
    score_gradient = (probs * (probability_gradient - row_dot) * inv_sqrt).astype(jnp.bfloat16)
    grad_query = jnp.einsum(
        "omc,och->omh", score_gradient, key_portion, preferred_element_type=jnp.float32
    ).reshape(tokens, head_dim)
    key_gradient = jnp.einsum(
        "tnc,tny->tcy", score_gradient, blocked_queries, preferred_element_type=jnp.float32
    )
    value_gradient = jnp.einsum(
        "tnc,tny->tcy", reduced_probabilities, block_gradient, preferred_element_type=jnp.float32
    )
    slot_grads = jnp.concatenate([key_gradient, value_gradient], axis=-1).reshape(
        blocks, slot_count, BLOCK, kv_width
    )
    to_prev = slot_grads[:, 0].astype(jnp.bfloat16)
    to_next = slot_grads[:, 2].astype(jnp.bfloat16)
    rand_grads = slot_grads[:, 3 : 3 + RAND].astype(jnp.bfloat16).reshape(rand_dev, BLOCK, kv_width)
    zero_block = jnp.zeros((1, BLOCK, kv_width), jnp.float32)
    kv_total = slot_grads[:, 1] + jnp.concatenate(
        [to_prev[1:].astype(jnp.float32), zero_block], axis=0
    )
    kv_total = kv_total + jnp.concatenate([zero_block, to_next[:-1].astype(jnp.float32)], axis=0)
    entries = jnp.concatenate([rand_grads, to_prev[:1], to_next[-1:]], axis=0)
    placing = (slot_row[None, :] == jnp.arange(shards * capacity, dtype=jnp.int32)[:, None]).astype(
        jnp.bfloat16
    )
    outgoing_grads = jnp.einsum(
        "se,exf->sxf", placing, entries, preferred_element_type=jnp.float32
    ).astype(jnp.bfloat16)
    outgoing_grads = outgoing_grads.reshape(shards, capacity, BLOCK, kv_width)
    returned = lax.all_to_all(
        outgoing_grads, "seq", split_axis=0, concat_axis=0, tiled=True
    ).reshape(shards * capacity, BLOCK, kv_width)
    receive_map = (
        (send_index.reshape(-1)[None, :] == jnp.arange(blocks, dtype=jnp.int32)[:, None])
        & slot_used.reshape(-1)[None, :]
    ).astype(jnp.bfloat16)
    kv_total = kv_total + jnp.einsum(
        "bs,sxf->bxf", receive_map, returned, preferred_element_type=jnp.float32
    )
    glob_terms = jnp.sum(slot_grads[:, 3 + RAND :], axis=0)
    glob_total = lax.psum(glob_terms.astype(jnp.bfloat16), "seq").astype(jnp.float32)
    for glob_no in range(GLOBAL):
        is_home = (owner_glob[glob_no] == myself) & (
            jnp.arange(blocks, dtype=jnp.int32) == offset_glob[glob_no]
        )
        kv_total = kv_total + jnp.where(is_home[:, None, None], glob_total[glob_no][None], 0.0)
    grad_key = kv_total[..., :head_dim].reshape(tokens, head_dim)
    grad_value = kv_total[..., head_dim:].reshape(tokens, head_dim)
    return (attended, token_loss, grad_query, grad_key, grad_value)


def solution(mesh):
    placed = (
        P("seq", "head"),
        P("seq", "head"),
        P("seq", "head"),
        P("seq", "head"),
        P("head"),
        P("seq"),
        P(),
        P(),
    )
    return jax.shard_map(
        body,
        mesh=mesh,
        in_specs=placed,
        out_specs=(
            P("seq", "head"),
            P("seq"),
            P("seq", "head"),
            P("seq", "head"),
            P("seq", "head"),
        ),
        check_vma=False,
    )
```

profile of v0, /device:TPU:4, one launch (start us, length us, event | category | flops | bytes accessed | tf_op | source)
XLA Modules:
  0.0 472.9 jit_solution(18062759920414362517)
XLA Ops:
  10.6 0.9 constant_dynamic-update-slice_fusion
  11.5 2.0 gather_fusion
  13.6 13.4 %all-to-all-start = ((bf16[32,2,64,256]{3,2,1,0:T(8,128)(2,1)}), bf16[32,2,64,256]{3,2,1,0:T(8,128)(2,1)S(1)}, u32[]{:S(2)}, u32[]{:S(2)}) async-start(bf16[32,2,64,256]{3,2,1,0:T(8,128)(2,1)} %bitcast.2), calls=%async_computation | async-start | bytes 4194304 | tf_op jit(solution)/shard_map/all_to_all | solution.py:55
  34.9 165.9 %all-reduce.8.cloned.1.call-done = (bf16[1,64,256]{2,1,0:T(8,128)(2,1)}, bf16[1,64,256]{2,1,0:T(8,128)(2,1)}) async-done(((bf16[1,64,256]{2,1,0:T(8,128)(2,1)}, bf16[1,64,256]{2,1,0:T(8,128)(2,1)}), (bf16[1,64,256]{2,1,0:T(8,128)(2,1)}, bf16[1,64,256]{2,1,0:T(8,128)(2,1)})) %all-reduce.8.cloned.1.call-update) | async-done | bytes 65552 | tf_op jit(solution)/shard_map/psum | solution.py:15
  203.1 1.5 fusion.70
  204.6 2.3 convolution_convert_fusion.1
  207.1 36.0 %psum.30 = f32[512]{0:T(512)S(1)} all-reduce(f32[512]{0:T(512)S(1)} %bitcast.109), channel_id=1, replica_groups=mesh['seq'=32,'head'=24] {'head'}, use_global_device_ids=true, to_apply=%region_7.8 | all-reduce | flops 512 | bytes 4096 | tf_op jit(solution)/shard_map/psum | solution.py:107
  243.9 2.7 fusion.23
  246.6 2.7 fusion.37
  249.3 5.6 %fusion.17 = f32[8,512,128]{1,2,0:T(8,128)} fusion(bf16[8,64,128]{2,1,0:T(8,128)(2,1)S(1)} %bitcast.87, f32[8,64,512]{2,1,0:T(8,128)} %fusion.23, f32[8,64,512]{2,1,0:T(8,128)S(1)} %get-tuple-element.30, f32[8,64]{1,0:T(8,128)} %copy-done.10), kind=kOutput, calls=%fused_computation.26 | convolution fusion | flops 68944896 | bytes 4327424 | tf_op jit(solution)/shard_map/tnc,tny->tcy/dot_general | solution.py:123
  254.9 4.2 pad_maximum_fusion
  259.1 5.4 %copy.125 = f32[8,512,256]{2,0,1:T(8,128)} copy(f32[8,512,256]{1,2,0:T(8,128)} %pad_maximum_fusion) | data formatting | bytes 8388608 | tf_op jit(solution)/shard_map/reshape | solution.py:129
  264.6 2.4 convert.11
  269.2 2.3 reshape.419
  271.4 5.1 %copy.121 = bf16[32,2,64,256]{3,1,2,0:T(2,128)(2,1)} copy(bf16[32,2,64,256]{3,1,0,2:T(2,128)(2,1)} %reshape.419) | data formatting | bytes 4194304 | tf_op jit(solution)/shard_map/reshape | solution.py:147
  276.6 7.8 %all-to-all-start.1 = ((bf16[32,2,64,256]{3,1,2,0:T(2,128)(2,1)}), bf16[32,2,64,256]{3,1,2,0:T(2,128)(2,1)S(1)}, u32[]{:S(2)}, u32[]{:S(2)}) async-start(bf16[32,2,64,256]{3,1,2,0:T(2,128)(2,1)} %copy.121), calls=%async_computation.1 | async-start | bytes 4194304 | tf_op jit(solution)/shard_map/all_to_all | solution.py:148
  287.7 5.3 %copy.112 = f32[8,512,256]{2,1,0:T(8,128)} copy(f32[8,512,256]{1,2,0:T(8,128)} %pad_maximum_fusion) | data formatting | bytes 8388608 | tf_op jit(solution)/shard_map/concatenate | solution.py:129
  293.0 1.9 slice_reduce_fusion
  295.0 5.1 %fusion.18 = f32[8,64,128]{2,1,0:T(8,128)} fusion(f32[8,64,512]{2,1,0:T(8,128)} %fusion.23, bf16[8,512,256]{2,1,0:T(8,128)(2,1)} %bitcast.102, f32[8,64,512]{2,1,0:T(8,128)S(1)} %get-tuple-element.30, f32[8,64]{1,0:T(8,128)S(1)} %copy-done.11), kind=kOutput, calls=%fused_computation.27 | convolution fusion | flops 68944896 | bytes 5513216 | tf_op jit(solution)/shard_map/omc,och->omh/dot_general | solution.py:120
  300.1 1.1 slice_bitcast_fusion.2
  301.2 154.6 %all-reduce.6.cloned.1.call-done = bf16[2,64,256]{2,1,0:T(8,128)(2,1)} async-done(((bf16[2,64,256]{2,1,0:T(8,128)(2,1)}), bf16[2,64,256]{2,1,0:T(8,128)(2,1)}) %all-reduce.6.cloned.1.call-update) | async-done | bytes 65552 | tf_op jit(solution)/shard_map/psum | solution.py:159
  456.7 3.7 copy.122
  460.4 2.7 reshape.420
  463.1 1.4 fusion.11
  (105 shorter events, 15.9 us)
Async XLA Ops:
  7.2 195.4 %copy-start = (bf16[512,128]{1,0:T(8,128)(2,1)S(1)}, bf16[512,128]{1,0:T(8,128)(2,1)}, u32[]{:S(2)}) copy-start(bf16[512,128]{1,0:T(8,128)(2,1)} %param.8) | copy-start | bytes 393220
  8.5 5.1 %copy-start.6 = (pred[32,26]{1,0:T(8,128)(4,1)}, pred[32,26]{1,0:T(8,128)(4,1)S(1)}, u32[]{:S(2)}) copy-start(pred[32,26]{1,0:T(8,128)(4,1)S(1)} %copy.105) | copy-start | bytes 2500
  9.4 4.1 copy-start.8
  13.6 13.5 %copy-start.18 = (s32[2]{0:T(128)S(1)}, s32[2]{0:T(128)}, u32[]{:S(2)}) copy-start(s32[2]{0:T(128)} %param.15) | copy-start | bytes 28
  13.6 19.7 %copy-start.15 = (bf16[128]{0:T(256)(128)(2,1)S(1)}, bf16[128]{0:T(256)(128)(2,1)}, u32[]{:S(2)}) copy-start(bf16[128]{0:T(256)(128)(2,1)} %param.12) | copy-start | bytes 772
  13.6 188.1 %all-to-all-start = ((bf16[32,2,64,256]{3,2,1,0:T(8,128)(2,1)}), bf16[32,2,64,256]{3,2,1,0:T(8,128)(2,1)S(1)}, u32[]{:S(2)}, u32[]{:S(2)}) async-start(bf16[32,2,64,256]{3,2,1,0:T(8,128)(2,1)} %bitcast.2), calls=%async_computation | async-start | bytes 4194304 | tf_op jit(solution)/shard_map/all_to_all | solution.py:55
  27.0 173.9 %all-reduce.8.cloned.1.call-start = ((), (), s32[]{:S(2)}) async-start(), calls=%async_computation.3 | async-start | bytes 131072 | tf_op jit(solution)/shard_map/psum | solution.py:15
  34.4 0.5 copy-start.12
  202.6 2.0 copy-start.3
  203.1 3.8 copy-start.2
  204.6 2.4 copy-start.10
  204.6 2.4 copy-start.16
  204.6 38.5 %copy-start.14 = (s32[512]{0:T(512)S(1)}, s32[512]{0:T(512)}, u32[]{:S(2)}) copy-start(s32[512]{0:T(512)} %param.13) | copy-start | bytes 6148
  204.6 39.1 %copy-start.4 = (bf16[512,128]{1,0:T(8,128)(2,1)S(1)}, bf16[512,128]{1,0:T(8,128)(2,1)}, u32[]{:S(2)}) copy-start(bf16[512,128]{1,0:T(8,128)(2,1)} %param.11) | copy-start | bytes 393220
  204.6 39.1 %copy-start.17 = (f32[128]{0:T(128)S(1)}, f32[128]{0:T(128)}, u32[]{:S(2)}) copy-start(f32[128]{0:T(128)} %convert_element_type.53) | copy-start | bytes 1540
  206.9 42.3 %copy-start.5 = (bf16[8,64,128]{2,1,0:T(8,128)(2,1)}, bf16[8,64,128]{2,1,0:T(8,128)(2,1)S(1)}, u32[]{:S(2)}) copy-start(bf16[8,64,128]{2,1,0:T(8,128)(2,1)S(1)} %convolution_convert_fusion.1) | copy-start | bytes 393220
  267.0 1.3 copy-start.1
  267.1 1.2 copy-start.13
  276.6 9.3 %copy-start.9 = (s32[32,2]{0,1:T(2,128)S(1)}, s32[32,2]{0,1:T(2,128)}, u32[]{:S(2)}) copy-start(s32[32,2]{0,1:T(2,128)} %copy-done.8) | copy-start | bytes 772
  276.6 9.4 %copy-start.7 = (pred[32,26]{1,0:T(8,128)(4,1)S(1)}, pred[32,26]{1,0:T(8,128)(4,1)}, u32[]{:S(2)}) copy-start(pred[32,26]{1,0:T(8,128)(4,1)} %copy-done.6) | copy-start | bytes 2500
  276.6 180.1 %all-to-all-start.1 = ((bf16[32,2,64,256]{3,1,2,0:T(2,128)(2,1)}), bf16[32,2,64,256]{3,1,2,0:T(2,128)(2,1)S(1)}, u32[]{:S(2)}, u32[]{:S(2)}) async-start(bf16[32,2,64,256]{3,1,2,0:T(2,128)(2,1)} %copy.121), calls=%async_computation.1 | async-start | bytes 4194304 | tf_op jit(solution)/shard_map/all_to_all | solution.py:148
  284.4 171.4 %all-reduce.6.cloned.1.call-start = ((), (), s32[]{:S(2)}) async-start(), calls=%async_computation.2 | async-start | bytes 131072 | tf_op jit(solution)/shard_map/psum | solution.py:159
  287.7 7.3 %copy-start.11 = (f32[8,64]{1,0:T(8,128)S(1)}, f32[8,64]{1,0:T(8,128)}, u32[]{:S(2)}) copy-start(f32[8,64]{1,0:T(8,128)} %copy-done.10) | copy-start | bytes 6148
Sparse Core Ops, SparseCore 0:
  33.4 167.4 all-reduce.7
  295.1 160.6 all-reduce.5
where the time goes:
time: 474 us; the launch traced here: 473 us
  waiting for transfers between devices  321 us (68%)
  local copies, waits for them, and re-layouts  36.7 us (8%)
  blocking collectives  36 us (8%)
  starting transfers between devices  21.5 us (5%)
  matrix products  21.3 us (4%)
  between operations  20.7 us (4%)
  other arithmetic  16.2 us (3%)
    psum x1, waiting for transfers between devices, spread(): return lax.psum(jnp.where(mine, x, jnp.zeros_like(x)), axis)  166 us
    psum x1, waiting for transfers between devices, body(): lax.psum(glob_terms.astype(jnp.bfloat16), 'seq').astype(jnp.float32)  155 us
    psum x1, blocking collectives, body(): logits = lax.psum(partial_logit, 'head')  36 us
    all_to_all x1, starting transfers between devices, body(): lax.all_to_all(outgoing, 'seq', split_axis=0, concat_axis=0, tiled=True)  13.4 us
  transfers between devices with their start and end apart: 4, of which 2 were waited for; matrix products, arithmetic and copies ran while one was open for 4% of the time, Pallas kernels for 0%

commit v1 on v0

v1 whole, which is shorter than its diff:
```python
import math

import jax
import jax.numpy as jnp
from jax import lax
from jax.experimental import pallas as pl
from jax.experimental.pallas import tpu as pltpu
from jax.sharding import PartitionSpec as P

BLOCK = 64
RAND = 3
GLOBAL = 2
CHUNK = 8

NT = (((1,), (1,)), ((), ()))
NN = (((1,), (0,)), ((), ()))
TN = (((0,), (0,)), ((), ()))


def mm(a, b, dims):
    return lax.dot_general(a, b, dims, preferred_element_type=jnp.float32)


def smem(count):
    return [pl.BlockSpec(memory_space=pltpu.SMEM) for _ in range(count)]


def vmem(count):
    return [pl.BlockSpec(memory_space=pltpu.VMEM) for _ in range(count)]


def call(kernel, name, n_smem, n_vmem, outs, **kw):
    return pl.pallas_call(
        kernel,
        name=name,
        in_specs=smem(n_smem) + vmem(n_vmem),
        out_specs=tuple(vmem(len(outs))),
        out_shape=tuple(jax.ShapeDtypeStruct(s, d) for s, d in outs),
        compiler_params=pltpu.CompilerParams(vmem_limit_bytes=40 * 1024 * 1024),
        **kw,
    )


def pack_kernel(pick, glob, k, v, send, gsend, first, last):
    blocks = k.shape[0]
    shards = send.shape[0]
    for r in range(shards):
        at = jnp.maximum(pick[r], 0)
        send[r, :BLOCK] = k[at]
        send[r, BLOCK:] = v[at]
    per_block = 2 * BLOCK // CHUNK
    for g in range(GLOBAL):
        at = glob[g] % blocks
        kg = k[at]
        vg = v[at]
        for c in range(per_block):
            src = kg if c < per_block // 2 else vg
            lo = (c * CHUNK) % BLOCK
            gsend[g * per_block + c] = src[lo : lo + CHUNK]
    first[:BLOCK] = k[0]
    first[BLOCK:] = v[0]
    last[:BLOCK] = k[blocks - 1]
    last[BLOCK:] = v[blocks - 1]


def slots_of(i, base, local, prev, after, incoming, shared, rand, blocks):
    parts = [
        local[i - 1] if i > 0 else prev[base : base + BLOCK],
        local[i],
        local[i + 1] if i < blocks - 1 else after[base : base + BLOCK],
    ]
    for j in range(RAND):
        parts.append(incoming[rand[i, j] // blocks, base : base + BLOCK])
    for g in range(GLOBAL):
        lo = g * 2 * BLOCK + base
        parts.append(shared[lo : lo + BLOCK])
    return jnp.concatenate(parts, axis=0)


def forward_kernel(rand, me, q, k, v, prev, after, incoming, shared, weight, attended, probs, part):
    blocks = k.shape[0]
    head_dim = k.shape[2]
    keys = (3 + RAND + GLOBAL) * BLOCK
    inv_sqrt = 1.0 / math.sqrt(head_dim)
    w8 = jnp.broadcast_to(weight[...], (8, head_dim))
    lane = lax.broadcasted_iota(jnp.int32, (BLOCK, keys), 1)
    rows = []
    for i in range(blocks):
        kk = slots_of(i, 0, k, prev, after, incoming, shared, rand, blocks)
        vv = slots_of(i, BLOCK, v, prev, after, incoming, shared, rand, blocks)
        s = mm(q[i], kk, NT) * inv_sqrt
        if i == 0:
            s = jnp.where((lane < BLOCK) & (me[0] == 0), -jnp.inf, s)
        if i == blocks - 1:
            void = (lane >= 2 * BLOCK) & (lane < 3 * BLOCK)
            s = jnp.where(void & (me[0] == me[1] - 1), -jnp.inf, s)
        e = jnp.exp(s - jnp.max(s, axis=1, keepdims=True))
        p = e / jnp.sum(e, axis=1, keepdims=True)
        probs[i] = p
        a = mm(p.astype(jnp.bfloat16), vv, NN).astype(jnp.bfloat16)
        attended[i] = a
        rows.append(mm(w8, a, NT)[:1])
    row = jnp.concatenate(rows, axis=1)
    for r in range(part.shape[0]):
        part[r] = row


def backward_kernel(
    rand, me, parts, labels, q, k, v, prev, after, incoming, shared, weight, upstream, probs,
    grad_q, acc_k, acc_v, outgoing, gparts, to_prev, to_next,
):
    blocks = k.shape[0]
    head_dim = k.shape[2]
    inv_sqrt = 1.0 / math.sqrt(head_dim)
    bf16 = jnp.bfloat16
    logits = jnp.sum(parts[...], axis=0)
    slope = lax.logistic(logits) - labels[...].astype(jnp.float32)
    column = jnp.transpose(jnp.broadcast_to(slope, (8, slope.shape[1])))[:, :1]
    w = weight[...].astype(jnp.float32)
    glob = [jnp.zeros((BLOCK, head_dim), jnp.float32) for _ in range(2 * GLOBAL)]
    own = []
    for i in range(blocks):
        kk = slots_of(i, 0, k, prev, after, incoming, shared, rand, blocks)
        vv = slots_of(i, BLOCK, v, prev, after, incoming, shared, rand, blocks)
        p = probs[i]
        g = (upstream[i].astype(jnp.float32) + column[i * BLOCK : (i + 1) * BLOCK] * w).astype(bf16)
        dp = mm(g, vv, NT)
        dot = jnp.sum(p * dp, axis=1, keepdims=True)
        ds = (p * (dp - dot) * inv_sqrt).astype(bf16)
        grad_q[i] = mm(ds, kk, NN)
        dk = mm(ds, q[i], TN)
        dv = mm(p.astype(bf16), g, TN)
        for j in range(RAND):
            lo = (3 + j) * BLOCK
            at = rand[i, j] // blocks
            outgoing[at, :BLOCK] = dk[lo : lo + BLOCK].astype(bf16)
            outgoing[at, BLOCK:] = dv[lo : lo + BLOCK].astype(bf16)
        for n in range(GLOBAL):
            lo = (3 + RAND + n) * BLOCK
            glob[2 * n] = glob[2 * n] + dk[lo : lo + BLOCK]
            glob[2 * n + 1] = glob[2 * n + 1] + dv[lo : lo + BLOCK]
        own.append((dk[: 3 * BLOCK], dv[: 3 * BLOCK]))
    for which, acc in enumerate((acc_k, acc_v)):
        lo = which * BLOCK
        for i in range(blocks):
            total = own[i][which][BLOCK : 2 * BLOCK]
            if i < blocks - 1:
                total = total + own[i + 1][which][:BLOCK].astype(bf16).astype(jnp.float32)
            if i > 0:
                total = total + own[i - 1][which][2 * BLOCK :].astype(bf16).astype(jnp.float32)
            acc[i] = total
        to_prev[lo : lo + BLOCK] = own[0][which][:BLOCK].astype(bf16)
        to_next[lo : lo + BLOCK] = own[blocks - 1][which][2 * BLOCK :].astype(bf16)
    for n in range(2 * GLOBAL):
        gparts[n * BLOCK : (n + 1) * BLOCK] = glob[n].astype(bf16)


def final_kernel(pick, glob, me, acc_k, acc_v, back, from_prev, from_next, shared, out_k, out_v):
    blocks = acc_k.shape[0]
    shards = back.shape[0]
    f32 = jnp.float32
    out_k[...] = acc_k[...]
    out_v[...] = acc_v[...]
    out_k[0] = out_k[0] + from_prev[:BLOCK].astype(f32)
    out_v[0] = out_v[0] + from_prev[BLOCK:].astype(f32)
    out_k[blocks - 1] = out_k[blocks - 1] + from_next[:BLOCK].astype(f32)
    out_v[blocks - 1] = out_v[blocks - 1] + from_next[BLOCK:].astype(f32)
    for r in range(shards):
        at = pick[r]

        @pl.when(at >= 0)
        def _():
            out_k[at] = out_k[at] + back[r, :BLOCK].astype(f32)
            out_v[at] = out_v[at] + back[r, BLOCK:].astype(f32)

    for g in range(GLOBAL):

        @pl.when(glob[g] // blocks == me[0])
        def _():
            at = glob[g] % blocks
            lo = g * 2 * BLOCK
            out_k[at] = out_k[at] + shared[lo : lo + BLOCK].astype(f32)
            out_v[at] = out_v[at] + shared[lo + BLOCK : lo + 2 * BLOCK].astype(f32)


def exchange(x, axis):
    return lax.all_to_all(x, axis, split_axis=0, concat_axis=0, tiled=True)


def body(queries, key_rows, value_rows, upstream, exit_weight, labels, rand_blocks, glob_blocks):
    tokens, head_dim = queries.shape
    blocks = tokens // BLOCK
    shards = lax.axis_size("seq")
    heads = lax.axis_size("head")
    myself = lax.axis_index("seq")
    bf16 = jnp.bfloat16
    f32 = jnp.float32
    keys = (3 + RAND + GLOBAL) * BLOCK
    wide = 2 * BLOCK
    chunks = GLOBAL * wide // CHUNK
    ups = [(n, n + 1) for n in range(shards - 1)]
    downs = [(n + 1, n) for n in range(shards - 1)]

    me = jnp.stack([myself, jnp.full_like(myself, shards)]).astype(jnp.int32)
    rand = lax.dynamic_slice_in_dim(rand_blocks, myself * blocks, blocks, 0)
    mine = jnp.where(rand_blocks // blocks == myself, rand_blocks % blocks, -1)
    pick = jnp.max(jnp.max(mine, axis=1).reshape(shards, blocks), axis=1)

    q = queries.reshape(blocks, BLOCK, head_dim)
    k = key_rows.reshape(blocks, BLOCK, head_dim)
    v = value_rows.reshape(blocks, BLOCK, head_dim)
    up = upstream.reshape(blocks, BLOCK, head_dim)
    weight = exit_weight.reshape(1, head_dim)

    send, gsend, first, last = call(
        pack_kernel, "pack", 2, 2,
        [((shards, wide, head_dim), bf16), ((chunks, CHUNK, head_dim), bf16),
         ((wide, head_dim), bf16), ((wide, head_dim), bf16)],
    )(pick, glob_blocks, k, v)
    incoming = exchange(send, "seq")
    glob_got = exchange(gsend, "seq")
    prev = lax.ppermute(last, "seq", ups)
    after = lax.ppermute(first, "seq", downs)
    owner = glob_blocks[myself // (shards // GLOBAL)] // blocks
    piece = lax.dynamic_index_in_dim(glob_got, owner, 0, keepdims=True)
    shared = exchange(jnp.broadcast_to(piece, (shards, CHUNK, head_dim)), "seq")
    shared = shared.reshape(GLOBAL * wide, head_dim)

    attended, probs, part = call(
        forward_kernel, "forward", 2, 8,
        [((blocks, BLOCK, head_dim), bf16), ((blocks, BLOCK, keys), f32), ((heads, 1, tokens), f32)],
    )(rand, me, q, k, v, prev, after, incoming, shared, weight)
    parts = exchange(part, "head")

    acc3 = (blocks, BLOCK, head_dim)
    grad_q, acc_k, acc_v, outgoing, gparts, to_prev, to_next = call(
        backward_kernel, "backward", 2, 12,
        [(acc3, f32), (acc3, f32), (acc3, f32), ((shards, wide, head_dim), bf16),
         ((GLOBAL * wide, head_dim), bf16), ((wide, head_dim), bf16), ((wide, head_dim), bf16)],
    )(rand, me, parts, labels.reshape(1, tokens), q, k, v, prev, after, incoming, shared, weight, up, probs)
    back = exchange(outgoing, "seq")
    gback = exchange(gparts.reshape(chunks, CHUNK, head_dim), "seq")
    from_prev = lax.ppermute(to_next, "seq", ups)
    from_next = lax.ppermute(to_prev, "seq", downs)
    gsum = jnp.sum(gback.astype(f32), axis=0, keepdims=True).astype(bf16)
    gtotal = exchange(jnp.broadcast_to(gsum, (shards, CHUNK, head_dim)), "seq")
    gtotal = gtotal.reshape(GLOBAL * wide, head_dim)

    logits = jnp.sum(parts, axis=(0, 1))
    token_loss = jax.nn.softplus(logits) - labels.astype(f32) * logits

    out_k, out_v = call(
        final_kernel, "final", 3, 6, [(acc3, f32), (acc3, f32)],
        input_output_aliases={3: 0, 4: 1},
    )(pick, glob_blocks, me, acc_k, acc_v, back, from_prev, from_next, gtotal)
    flat = (tokens, head_dim)
    return (
        attended.reshape(flat),
        token_loss,
        grad_q.reshape(flat),
        out_k.reshape(flat),
        out_v.reshape(flat),
    )


def solution(mesh):
    placed = (
        P("seq", "head"),
        P("seq", "head"),
        P("seq", "head"),
        P("seq", "head"),
        P("head"),
        P("seq"),
        P(),
        P(),
    )
    return jax.shard_map(
        body,
        mesh=mesh,
        in_specs=placed,
        out_specs=(
            P("seq", "head"),
            P("seq"),
            P("seq", "head"),
            P("seq", "head"),
            P("seq", "head"),
        ),
        check_vma=False,
    )
```

time: 474 us -> 169 us (0.36)
  the two profiles are of different devices: /device:TPU:4 before, /device:TPU:8 now
where the time goes in v1:
time: 169 us
  blocking collectives  66 us (39%)
  waiting for transfers between devices  44.6 us (26%)
  starting transfers between devices  34.3 us (20%)
  Pallas kernels  14.2 us (8%)
  local copies, waits for them, and re-layouts  5.32 us (3%)
  between operations  3.37 us (2%)
    all_to_all x4, blocking collectives, exchange(): return lax.all_to_all(x, axis, split_axis=0, concat_axis=0, tiled=True)  66 us
    all_to_all x3, starting transfers between devices, exchange(): return lax.all_to_all(x, axis, split_axis=0, concat_axis=0, tiled=True)  22.6 us
    all_to_all x3, waiting for transfers between devices, exchange(): return lax.all_to_all(x, axis, split_axis=0, concat_axis=0, tiled=True)  16.5 us
    ppermute x1, waiting for transfers between devices, body(): from_prev = lax.ppermute(to_next, 'seq', ups)  14.1 us
    ppermute x1, waiting for transfers between devices, body(): prev = lax.ppermute(last, 'seq', ups)  12.3 us
    pallas_call x1, Pallas kernels, body(): call(backward_kernel, 'backward', 2, 12, [(acc3, f32), (acc3, f32), (acc3...  5.35 us
    pallas_call x1, Pallas kernels, body(): call(forward_kernel, 'forward', 2, 8, [((blocks, BLOCK, head_dim), bf16),...  5.01 us
    unnamed x21, local copies, waits for them, and re-layouts  4.55 us
  transfers between devices with their start and end apart: 7, of which 7 were waited for; matrix products, arithmetic and copies ran while one was open for 1% of the time, Pallas kernels for 0%

profile of v1, /device:TPU:8, one launch (start us, length us, event | category | flops | bytes accessed | tf_op | source)
XLA Modules:
  0.0 168.7 jit_solution(15951252491909837750)
XLA Ops:
  2.2 0.9 copy-done
  3.1 0.9 copy-done.2
  4.0 1.6 pack.1
  5.6 13.0 %all-to-all-start.1 = ((bf16[32,8,128]{2,1,0:T(8,128)(2,1)}), bf16[32,8,128]{2,1,0:T(8,128)(2,1)S(1)}, u32[]{:S(2)}, u32[]{:S(2)}) async-start(bf16[32,8,128]{2,1,0:T(8,128)(2,1)} %get-tuple-element.24), calls=%async_computation.1 | async-start | bytes 131072 | tf_op jit(solution)/shard_map/all_to_all | solution.py:187
  21.8 6.0 %all-to-all-done.1 = bf16[32,8,128]{2,1,0:T(8,128)(2,1)S(1)} async-done(((bf16[32,8,128]{2,1,0:T(8,128)(2,1)}), bf16[32,8,128]{2,1,0:T(8,128)(2,1)S(1)}, u32[]{:S(2)}, u32[]{:S(2)}) %all-to-all-start.1) | async-done | bytes 65568 | tf_op jit(solution)/shard_map/all_to_all | solution.py:187
  27.8 13.2 %all_to_all.35 = bf16[32,8,128]{2,1,0:T(8,128)(2,1)S(1)} all-to-all(bf16[32,8,128]{2,1,0:T(8,128)(2,1)S(1)} %broadcast_in_dim.16), channel_id=1, replica_groups=mesh['seq'=32,'head'=24] {'seq'}, dimensions={0} | all-to-all | bytes 131072 | tf_op jit(solution)/shard_map/all_to_all | solution.py:187
  41.0 4.9 %all-to-all-start = ((bf16[32,128,128]{2,1,0:T(8,128)(2,1)}), bf16[32,128,128]{2,1,0:T(8,128)(2,1)S(1)}, u32[]{:S(2)}, u32[]{:S(2)}) async-start(bf16[32,128,128]{2,1,0:T(8,128)(2,1)} %get-tuple-element.23), calls=%async_computation | async-start | bytes 2097152 | tf_op jit(solution)/shard_map/all_to_all | solution.py:187
  45.8 3.4 %collective-permute-start = (bf16[128,128]{1,0:T(8,128)(2,1)S(1)}, bf16[128,128]{1,0:T(8,128)(2,1)S(1)}, u32[]{:S(2)}, u32[]{:S(2)}) collective-permute-start(bf16[128,128]{1,0:T(8,128)(2,1)S(1)} %get-tuple-element.21), channel_id=1, source_target_pairs={{0,24},{24,48},{48,72},{72,96},{96,120},{120,144},{144,168},{168,1... | collective-permute-start | bytes 98312 | tf_op jit(solution)/shard_map/ppermute | solution.py:222
  49.2 2.5 %collective-permute-start.1 = (bf16[128,128]{1,0:T(8,128)(2,1)S(1)}, bf16[128,128]{1,0:T(8,128)(2,1)S(1)}, u32[]{:S(2)}, u32[]{:S(2)}) collective-permute-start(bf16[128,128]{1,0:T(8,128)(2,1)S(1)} %get-tuple-element.22), channel_id=1, source_target_pairs={{24,0},{48,24},{72,48},{96,72},{120,96},{144,120},{168,144},{192,1... | collective-permute-start | bytes 98312 | tf_op jit(solution)/shard_map/ppermute | solution.py:223
  51.9 12.3 %collective-permute-done.prev = bf16[128,128]{1,0:T(8,128)(2,1)S(1)} collective-permute-done((bf16[128,128]{1,0:T(8,128)(2,1)S(1)}, bf16[128,128]{1,0:T(8,128)(2,1)S(1)}, u32[]{:S(2)}, u32[]{:S(2)}) %collective-permute-start) | collective-permute-done | bytes 32800 | tf_op jit(solution)/shard_map/ppermute | solution.py:222
  64.8 5.2 %all-to-all-done.incoming = bf16[32,128,128]{2,1,0:T(8,128)(2,1)S(1)} async-done(((bf16[32,128,128]{2,1,0:T(8,128)(2,1)}), bf16[32,128,128]{2,1,0:T(8,128)(2,1)S(1)}, u32[]{:S(2)}, u32[]{:S(2)}) %all-to-all-start) | async-done | bytes 1048608 | tf_op jit(solution)/shard_map/all_to_all | solution.py:187
  70.6 5.0 %forward.1 = (bf16[8,64,128]{2,1,0:T(8,128)(2,1)}, f32[8,64,512]{2,1,0:T(8,128)S(1)}, f32[24,1,512]{2,1,0:T(1,128)S(1)}) custom-call(s32[8,3]{1,0:T(8,128)S(1)} %copy.17.rand, s32[2]{0:T(128)S(1)} %pad_add_fusion.me, bf16[8,64,128]{2,1,0:T(8,128)(2,1)S(1)} %bitcast.25, bf16[8,64,128]{2,1,0:T(8,128)(2,1)S(1)} %bitcast.18, bf16[8,64,128]{2,1,0:T(8,128)(2,1)S(1)} %bitcast.21, ...), custom_call_target="tpu_custom_call" | custom-call | tf_op jit(solution)/shard_map/forward/pallas_call | solution.py:229
  75.7 25.6 %all_to_all.36.parts = f32[24,1,512]{2,1,0:T(1,128)S(1)} all-to-all(f32[24,1,512]{2,1,0:T(1,128)S(1)} %get-tuple-element.26), channel_id=1, replica_groups=mesh['seq'=32,'head'=24] {'head'}, dimensions={0} | all-to-all | bytes 98304 | tf_op jit(solution)/shard_map/all_to_all | solution.py:187
  101.3 0.7 copy-done.6
  102.0 5.4 %backward.1 = (f32[8,64,128]{2,1,0:T(8,128)}, f32[8,64,128]{2,1,0:T(8,128)}, f32[8,64,128]{2,1,0:T(8,128)}, bf16[32,128,128]{2,1,0:T(8,128)(2,1)}, bf16[256,128]...) custom-call(s32[8,3]{1,0:T(8,128)S(1)} %copy.17.rand, s32[2]{0:T(128)S(1)} %pad_add_fusion.me, ...), custom_call_target="tpu_custom_call" | custom-call | tf_op jit(solution)/shard_map/backward/pallas_call | solution.py:236
  107.3 14.0 %all_to_all.37 = bf16[32,8,128]{2,1,0:T(8,128)(2,1)S(1)} all-to-all(bf16[32,8,128]{2,1,0:T(8,128)(2,1)S(1)} %bitcast.29), channel_id=1, replica_groups=mesh['seq'=32,'head'=24] {'seq'}, dimensions={0} | all-to-all | bytes 131072 | tf_op jit(solution)/shard_map/all_to_all | solution.py:187
  121.4 13.2 %all_to_all.38 = bf16[32,8,128]{2,1,0:T(8,128)(2,1)S(1)} all-to-all(bf16[32,8,128]{2,1,0:T(8,128)(2,1)S(1)} %broadcast_in_dim.17), channel_id=1, replica_groups=mesh['seq'=32,'head'=24] {'seq'}, dimensions={0} | all-to-all | bytes 131072 | tf_op jit(solution)/shard_map/all_to_all | solution.py:187
  134.6 4.8 %all-to-all-start.4 = ((bf16[32,128,128]{2,1,0:T(8,128)(2,1)}), bf16[32,128,128]{2,1,0:T(8,128)(2,1)S(1)}, u32[]{:S(2)}, u32[]{:S(2)}) async-start(bf16[32,128,128]{2,1,0:T(8,128)(2,1)} %get-tuple-element.31), calls=%async_computation.4 | async-start | bytes 2097152 | tf_op jit(solution)/shard_map/all_to_all | solution.py:187
  139.4 3.4 %collective-permute-start.2 = (bf16[128,128]{1,0:T(8,128)(2,1)S(1)}, bf16[128,128]{1,0:T(8,128)(2,1)S(1)}, u32[]{:S(2)}, u32[]{:S(2)}) collective-permute-start(bf16[128,128]{1,0:T(8,128)(2,1)S(1)} %get-tuple-element.32), channel_id=1, source_target_pairs={{0,24},{24,48},{48,72},{72,96},{96,120},{120,144},{144,168},{168,1... | collective-permute-start | bytes 98312 | tf_op jit(solution)/shard_map/ppermute | solution.py:243
  142.7 2.5 %collective-permute-start.3 = (bf16[128,128]{1,0:T(8,128)(2,1)S(1)}, bf16[128,128]{1,0:T(8,128)(2,1)S(1)}, u32[]{:S(2)}, u32[]{:S(2)}) collective-permute-start(bf16[128,128]{1,0:T(8,128)(2,1)S(1)} %get-tuple-element.33), channel_id=1, source_target_pairs={{24,0},{48,24},{72,48},{96,72},{120,96},{144,120},{168,144},{192,1... | collective-permute-start | bytes 98312 | tf_op jit(solution)/shard_map/ppermute | solution.py:244
  145.9 14.1 %collective-permute-done.2.from_prev = bf16[128,128]{1,0:T(8,128)(2,1)S(1)} collective-permute-done((bf16[128,128]{1,0:T(8,128)(2,1)S(1)}, bf16[128,128]{1,0:T(8,128)(2,1)S(1)}, u32[]{:S(2)}, u32[]{:S(2)}) %collective-permute-start.2) | collective-permute-done | bytes 32800 | tf_op jit(solution)/shard_map/ppermute | solution.py:243
  159.9 1.2 collective-permute-done.3.from_next
  161.1 5.3 %all-to-all-done.4.back = bf16[32,128,128]{2,1,0:T(8,128)(2,1)S(1)} async-done(((bf16[32,128,128]{2,1,0:T(8,128)(2,1)}), bf16[32,128,128]{2,1,0:T(8,128)(2,1)S(1)}, u32[]{:S(2)}, u32[]{:S(2)}) %all-to-all-start.4) | async-done | bytes 1048608 | tf_op jit(solution)/shard_map/all_to_all | solution.py:187
  166.4 2.2 %final.1 = (f32[8,64,128]{2,1,0:T(8,128)}, f32[8,64,128]{2,1,0:T(8,128)}) custom-call(s32[32]{0:T(128)S(1)} %reduce_max.19.pick, s32[2]{0:T(128)S(1)} %copy-done.8, s32[2]{0:T(128)S(1)} %pad_add_fusion.me, f32[8,64,128]{2,1,0:T(8,128)} %get-tuple-element.29.acc_k, ...), custom_call_target="tpu_custom_call", output_to_operand_aliasing={{0}: (3, {}), {1}: (4, {})} | custom-call | tf_op jit(solution)/shard_map/final/pallas_call | solution.py:252
  (31 shorter events, 4.3 us)
Async XLA Ops:
  0.6 0.7 copy-start.9
  1.6 0.7 copy-start.8
  2.2 0.9 copy-start
  3.1 0.9 copy-start.2
  5.6 22.2 %all-to-all-start.1 = ((bf16[32,8,128]{2,1,0:T(8,128)(2,1)}), bf16[32,8,128]{2,1,0:T(8,128)(2,1)S(1)}, u32[]{:S(2)}, u32[]{:S(2)}) async-start(bf16[32,8,128]{2,1,0:T(8,128)(2,1)} %get-tuple-element.24), calls=%async_computation.1 | async-start | bytes 131072 | tf_op jit(solution)/shard_map/all_to_all | solution.py:187
  41.0 29.0 %copy-start.1 = (bf16[512,128]{1,0:T(8,128)(2,1)S(1)}, bf16[512,128]{1,0:T(8,128)(2,1)}, u32[]{:S(2)}) copy-start(bf16[512,128]{1,0:T(8,128)(2,1)} %param.9) | copy-start | bytes 393220
  41.0 29.0 %copy-start.3 = (bf16[512,128]{1,0:T(8,128)(2,1)S(1)}, bf16[512,128]{1,0:T(8,128)(2,1)}, u32[]{:S(2)}) copy-start(bf16[512,128]{1,0:T(8,128)(2,1)} %param.10) | copy-start | bytes 393220
  41.0 29.0 %copy-start.4 = (bf16[512,128]{1,0:T(8,128)(2,1)S(1)}, bf16[512,128]{1,0:T(8,128)(2,1)}, u32[]{:S(2)}) copy-start(bf16[512,128]{1,0:T(8,128)(2,1)} %param.8) | copy-start | bytes 393220
  41.0 29.0 %all-to-all-start = ((bf16[32,128,128]{2,1,0:T(8,128)(2,1)}), bf16[32,128,128]{2,1,0:T(8,128)(2,1)S(1)}, u32[]{:S(2)}, u32[]{:S(2)}) async-start(bf16[32,128,128]{2,1,0:T(8,128)(2,1)} %get-tuple-element.23), calls=%async_computation | async-start | bytes 2097152 | tf_op jit(solution)/shard_map/all_to_all | solution.py:187
  45.8 18.4 %collective-permute-start = (bf16[128,128]{1,0:T(8,128)(2,1)S(1)}, bf16[128,128]{1,0:T(8,128)(2,1)S(1)}, u32[]{:S(2)}, u32[]{:S(2)}) collective-permute-start(bf16[128,128]{1,0:T(8,128)(2,1)S(1)} %get-tuple-element.21), channel_id=1, source_target_pairs={{0,24},{24,48},{48,72},{72,96},{96,120},{120,144},{144,168},{168,1... | collective-permute-start | bytes 98312 | tf_op jit(solution)/shard_map/ppermute | solution.py:222
  49.2 15.6 %collective-permute-start.1 = (bf16[128,128]{1,0:T(8,128)(2,1)S(1)}, bf16[128,128]{1,0:T(8,128)(2,1)S(1)}, u32[]{:S(2)}, u32[]{:S(2)}) collective-permute-start(bf16[128,128]{1,0:T(8,128)(2,1)S(1)} %get-tuple-element.22), channel_id=1, source_target_pairs={{24,0},{48,24},{72,48},{96,72},{120,96},{144,120},{168,144},{192,1... | collective-permute-start | bytes 98312 | tf_op jit(solution)/shard_map/ppermute | solution.py:223
  70.0 0.7 copy-start.7
  70.6 30.7 %copy-start.5 = (bf16[512,128]{1,0:T(8,128)(2,1)S(1)}, bf16[512,128]{1,0:T(8,128)(2,1)}, u32[]{:S(2)}) copy-start(bf16[512,128]{1,0:T(8,128)(2,1)} %param.11) | copy-start | bytes 393220
  101.3 0.7 copy-start.6
  134.6 31.9 %all-to-all-start.4 = ((bf16[32,128,128]{2,1,0:T(8,128)(2,1)}), bf16[32,128,128]{2,1,0:T(8,128)(2,1)S(1)}, u32[]{:S(2)}, u32[]{:S(2)}) async-start(bf16[32,128,128]{2,1,0:T(8,128)(2,1)} %get-tuple-element.31), calls=%async_computation.4 | async-start | bytes 2097152 | tf_op jit(solution)/shard_map/all_to_all | solution.py:187
  139.4 20.6 %collective-permute-start.2 = (bf16[128,128]{1,0:T(8,128)(2,1)S(1)}, bf16[128,128]{1,0:T(8,128)(2,1)S(1)}, u32[]{:S(2)}, u32[]{:S(2)}) collective-permute-start(bf16[128,128]{1,0:T(8,128)(2,1)S(1)} %get-tuple-element.32), channel_id=1, source_target_pairs={{0,24},{24,48},{48,72},{72,96},{96,120},{120,144},{144,168},{168,1... | collective-permute-start | bytes 98312 | tf_op jit(solution)/shard_map/ppermute | solution.py:243
  142.7 18.4 %collective-permute-start.3 = (bf16[128,128]{1,0:T(8,128)(2,1)S(1)}, bf16[128,128]{1,0:T(8,128)(2,1)S(1)}, u32[]{:S(2)}, u32[]{:S(2)}) collective-permute-start(bf16[128,128]{1,0:T(8,128)(2,1)S(1)} %get-tuple-element.33), channel_id=1, source_target_pairs={{24,0},{48,24},{72,48},{96,72},{120,96},{144,120},{168,144},{192,1... | collective-permute-start | bytes 98312 | tf_op jit(solution)/shard_map/ppermute | solution.py:244

commit v2 on v1

--- a/solution.py
+++ b/solution.py
@@ -41,26 +41,57 @@
     )
 
 
-def pack_kernel(pick, glob, k, v, send, gsend, first, last):
+def scatter_kernel(glob, k, v, gsend, staged, sems):
     blocks = k.shape[0]
-    shards = send.shape[0]
-    for r in range(shards):
+    copies = []
+    for g in range(GLOBAL):
+        at = glob[g] % blocks
+        for n, src in enumerate((k, v)):
+            slot = 2 * g + n
+            copies.append(pltpu.make_async_copy(src.at[at], staged.at[slot], sems.at[slot]))
+    for copy in copies:
+        copy.start()
+    per_block = BLOCK // CHUNK
+    for slot, copy in enumerate(copies):
+        copy.wait()
+        for c in range(per_block):
+            gsend[slot * per_block + c] = staged[slot, c * CHUNK : (c + 1) * CHUNK]
+
+
+def pack_kernel(pick, k, v, weight, labels, send, first, last, weight_out, labels_out):
+    blocks = k.shape[0]
+    for r in range(send.shape[0]):
         at = jnp.maximum(pick[r], 0)
         send[r, :BLOCK] = k[at]
-        send[r, BLOCK:] = v[at]
-    per_block = 2 * BLOCK // CHUNK
-    for g in range(GLOBAL):
-        at = glob[g] % blocks
-        kg = k[at]
-        vg = v[at]
-        for c in range(per_block):
-            src = kg if c < per_block // 2 else vg
-            lo = (c * CHUNK) % BLOCK
-            gsend[g * per_block + c] = src[lo : lo + CHUNK]
+        send[r, BLOCK : 2 * BLOCK] = v[at]
+        send[r, 2 * BLOCK :] = jnp.zeros((CHUNK, k.shape[2]), k.dtype)
     first[:BLOCK] = k[0]
     first[BLOCK:] = v[0]
     last[:BLOCK] = k[blocks - 1]
     last[BLOCK:] = v[blocks - 1]
+    weight_out[...] = weight[...].astype(jnp.float32)
+    labels_out[...] = labels[...].astype(jnp.float32)
+
+
+def fill_kernel(glob, me, got, send, out, sems):
+    del send
+    shards = got.shape[0]
+    owner = glob[me[0] // (shards // GLOBAL)] // me[2]
+    copies = [
+        pltpu.make_async_copy(got.at[owner], out.at[r, 2 * BLOCK :], sems.at[r])
+        for r in range(shards)
+    ]
+    for copy in copies:
+        copy.start()
+    for copy in copies:
+        copy.wait()
+
+
+def shared_rows(incoming, slot):
+    per_block = BLOCK // CHUNK
+    lo = slot * per_block
+    rows = incoming[lo : lo + per_block, 2 * BLOCK :]
+    return rows.reshape(BLOCK, rows.shape[2])
 
 
 def slots_of(i, base, local, prev, after, incoming, shared, rand, blocks):
@@ -71,23 +102,23 @@
     ]
     for j in range(RAND):
         parts.append(incoming[rand[i, j] // blocks, base : base + BLOCK])
-    for g in range(GLOBAL):
-        lo = g * 2 * BLOCK + base
-        parts.append(shared[lo : lo + BLOCK])
+    parts.extend(shared)
     return jnp.concatenate(parts, axis=0)
 
 
-def forward_kernel(rand, me, q, k, v, prev, after, incoming, shared, weight, attended, probs, part):
+def forward_kernel(rand, me, q, k, v, prev, after, incoming, weight, attended, probs, part):
     blocks = k.shape[0]
     head_dim = k.shape[2]
     keys = (3 + RAND + GLOBAL) * BLOCK
     inv_sqrt = 1.0 / math.sqrt(head_dim)
-    w8 = jnp.broadcast_to(weight[...], (8, head_dim))
+    w8 = jnp.broadcast_to(weight[...], (8, head_dim)).astype(jnp.bfloat16)
+    gk = [shared_rows(incoming, 2 * g) for g in range(GLOBAL)]
+    gv = [shared_rows(incoming, 2 * g + 1) for g in range(GLOBAL)]
     lane = lax.broadcasted_iota(jnp.int32, (BLOCK, keys), 1)
     rows = []
     for i in range(blocks):
-        kk = slots_of(i, 0, k, prev, after, incoming, shared, rand, blocks)
-        vv = slots_of(i, BLOCK, v, prev, after, incoming, shared, rand, blocks)
+        kk = slots_of(i, 0, k, prev, after, incoming, gk, rand, blocks)
+        vv = slots_of(i, BLOCK, v, prev, after, incoming, gv, rand, blocks)
         s = mm(q[i], kk, NT) * inv_sqrt
         if i == 0:
             s = jnp.where((lane < BLOCK) & (me[0] == 0), -jnp.inf, s)
@@ -106,22 +137,24 @@
 
 
 def backward_kernel(
-    rand, me, parts, labels, q, k, v, prev, after, incoming, shared, weight, upstream, probs,
-    grad_q, acc_k, acc_v, outgoing, gparts, to_prev, to_next,
+    rand, parts, labels, q, k, v, prev, after, incoming, weight, upstream, probs,
+    grad_q, acc_k, acc_v, outgoing, to_prev, to_next,
 ):
     blocks = k.shape[0]
     head_dim = k.shape[2]
     inv_sqrt = 1.0 / math.sqrt(head_dim)
     bf16 = jnp.bfloat16
     logits = jnp.sum(parts[...], axis=0)
-    slope = lax.logistic(logits) - labels[...].astype(jnp.float32)
+    slope = lax.logistic(logits) - labels[...]
     column = jnp.transpose(jnp.broadcast_to(slope, (8, slope.shape[1])))[:, :1]
-    w = weight[...].astype(jnp.float32)
+    w = weight[...]
+    gk = [shared_rows(incoming, 2 * g) for g in range(GLOBAL)]
+    gv = [shared_rows(incoming, 2 * g + 1) for g in range(GLOBAL)]
     glob = [jnp.zeros((BLOCK, head_dim), jnp.float32) for _ in range(2 * GLOBAL)]
     own = []
     for i in range(blocks):
-        kk = slots_of(i, 0, k, prev, after, incoming, shared, rand, blocks)
-        vv = slots_of(i, BLOCK, v, prev, after, incoming, shared, rand, blocks)
+        kk = slots_of(i, 0, k, prev, after, incoming, gk, rand, blocks)
+        vv = slots_of(i, BLOCK, v, prev, after, incoming, gv, rand, blocks)
         p = probs[i]
         g = (upstream[i].astype(jnp.float32) + column[i * BLOCK : (i + 1) * BLOCK] * w).astype(bf16)
         dp = mm(g, vv, NT)
@@ -134,7 +167,7 @@
             lo = (3 + j) * BLOCK
             at = rand[i, j] // blocks
             outgoing[at, :BLOCK] = dk[lo : lo + BLOCK].astype(bf16)
-            outgoing[at, BLOCK:] = dv[lo : lo + BLOCK].astype(bf16)
+            outgoing[at, BLOCK : 2 * BLOCK] = dv[lo : lo + BLOCK].astype(bf16)
         for n in range(GLOBAL):
             lo = (3 + RAND + n) * BLOCK
             glob[2 * n] = glob[2 * n] + dk[lo : lo + BLOCK]
@@ -151,8 +184,10 @@
             acc[i] = total
         to_prev[lo : lo + BLOCK] = own[0][which][:BLOCK].astype(bf16)
         to_next[lo : lo + BLOCK] = own[blocks - 1][which][2 * BLOCK :].astype(bf16)
+    per_block = BLOCK // CHUNK
     for n in range(2 * GLOBAL):
-        gparts[n * BLOCK : (n + 1) * BLOCK] = glob[n].astype(bf16)
+        rows = glob[n].astype(bf16).reshape(per_block, CHUNK, head_dim)
+        outgoing[n * per_block : (n + 1) * per_block, 2 * BLOCK :] = rows
 
 
 def final_kernel(pick, glob, me, acc_k, acc_v, back, from_prev, from_next, shared, out_k, out_v):
@@ -171,7 +206,7 @@
         @pl.when(at >= 0)
         def _():
             out_k[at] = out_k[at] + back[r, :BLOCK].astype(f32)
-            out_v[at] = out_v[at] + back[r, BLOCK:].astype(f32)
+            out_v[at] = out_v[at] + back[r, BLOCK : 2 * BLOCK].astype(f32)
 
     for g in range(GLOBAL):
 
@@ -201,7 +236,7 @@
     ups = [(n, n + 1) for n in range(shards - 1)]
     downs = [(n + 1, n) for n in range(shards - 1)]
 
-    me = jnp.stack([myself, jnp.full_like(myself, shards)]).astype(jnp.int32)
+    me = jnp.stack([myself, jnp.full_like(myself, shards), jnp.full_like(myself, blocks)])
     rand = lax.dynamic_slice_in_dim(rand_blocks, myself * blocks, blocks, 0)
     mine = jnp.where(rand_blocks // blocks == myself, rand_blocks % blocks, -1)
     pick = jnp.max(jnp.max(mine, axis=1).reshape(shards, blocks), axis=1)
@@ -212,37 +247,54 @@
     up = upstream.reshape(blocks, BLOCK, head_dim)
     weight = exit_weight.reshape(1, head_dim)
 
-    send, gsend, first, last = call(
-        pack_kernel, "pack", 2, 2,
-        [((shards, wide, head_dim), bf16), ((chunks, CHUNK, head_dim), bf16),
-         ((wide, head_dim), bf16), ((wide, head_dim), bf16)],
-    )(pick, glob_blocks, k, v)
-    incoming = exchange(send, "seq")
+    slot_rows = wide + CHUNK
+    gsend = pl.pallas_call(
+        scatter_kernel,
+        name="scatter",
+        in_specs=smem(1) + [pl.BlockSpec(memory_space=pl.ANY)] * 2,
+        out_specs=pl.BlockSpec(memory_space=pltpu.VMEM),
+        out_shape=jax.ShapeDtypeStruct((chunks, CHUNK, head_dim), bf16),
+        scratch_shapes=[
+            pltpu.VMEM((2 * GLOBAL, BLOCK, head_dim), bf16),
+            pltpu.SemaphoreType.DMA((2 * GLOBAL,)),
+        ],
+    )(glob_blocks, k, v)
     glob_got = exchange(gsend, "seq")
+    send, first, last, w32, target = call(
+        pack_kernel, "pack", 1, 4,
+        [((shards, slot_rows, head_dim), bf16), ((wide, head_dim), bf16), ((wide, head_dim), bf16),
+         ((1, head_dim), f32), ((1, tokens), f32)],
+    )(pick, k, v, weight, labels.reshape(1, tokens))
     prev = lax.ppermute(last, "seq", ups)
     after = lax.ppermute(first, "seq", downs)
-    owner = glob_blocks[myself // (shards // GLOBAL)] // blocks
-    piece = lax.dynamic_index_in_dim(glob_got, owner, 0, keepdims=True)
-    shared = exchange(jnp.broadcast_to(piece, (shards, CHUNK, head_dim)), "seq")
-    shared = shared.reshape(GLOBAL * wide, head_dim)
+    anywhere = pl.BlockSpec(memory_space=pl.ANY)
+    send = pl.pallas_call(
+        fill_kernel,
+        name="fill",
+        in_specs=smem(2) + [anywhere] * 2,
+        out_specs=anywhere,
+        out_shape=jax.ShapeDtypeStruct(send.shape, send.dtype),
+        scratch_shapes=[pltpu.SemaphoreType.DMA((shards,))],
+        input_output_aliases={3: 0},
+    )(glob_blocks, me, glob_got, send)
+    incoming = exchange(send, "seq")
 
     attended, probs, part = call(
-        forward_kernel, "forward", 2, 8,
+        forward_kernel, "forward", 2, 7,
         [((blocks, BLOCK, head_dim), bf16), ((blocks, BLOCK, keys), f32), ((heads, 1, tokens), f32)],
-    )(rand, me, q, k, v, prev, after, incoming, shared, weight)
+    )(rand, me, q, k, v, prev, after, incoming, w32)
     parts = exchange(part, "head")
 
     acc3 = (blocks, BLOCK, head_dim)
-    grad_q, acc_k, acc_v, outgoing, gparts, to_prev, to_next = call(
-        backward_kernel, "backward", 2, 12,
-        [(acc3, f32), (acc3, f32), (acc3, f32), ((shards, wide, head_dim), bf16),
-         ((GLOBAL * wide, head_dim), bf16), ((wide, head_dim), bf16), ((wide, head_dim), bf16)],
-    )(rand, me, parts, labels.reshape(1, tokens), q, k, v, prev, after, incoming, shared, weight, up, probs)
+    grad_q, acc_k, acc_v, outgoing, to_prev, to_next = call(
+        backward_kernel, "backward", 1, 11,
+        [(acc3, f32), (acc3, f32), (acc3, f32), ((shards, slot_rows, head_dim), bf16),
+         ((wide, head_dim), bf16), ((wide, head_dim), bf16)],
+    )(rand, parts, target, q, k, v, prev, after, incoming, w32, up, probs)
     back = exchange(outgoing, "seq")
-    gback = exchange(gparts.reshape(chunks, CHUNK, head_dim), "seq")
     from_prev = lax.ppermute(to_next, "seq", ups)
     from_next = lax.ppermute(to_prev, "seq", downs)
-    gsum = jnp.sum(gback.astype(f32), axis=0, keepdims=True).astype(bf16)
+    gsum = jnp.sum(back[:, wide:].astype(f32), axis=0, keepdims=True).astype(bf16)
     gtotal = exchange(jnp.broadcast_to(gsum, (shards, CHUNK, head_dim)), "seq")
     gtotal = gtotal.reshape(GLOBAL * wide, head_dim)
 

time: 169 us -> 154 us (0.911)
  blocking collectives: 66 us -> 25.5 us
  waiting for transfers between devices: 44.6 us -> 55.8 us
  starting transfers between devices: 34.3 us -> 43.4 us
  Pallas kernels: 14.2 us -> 19.5 us
  between operations: 3.37 us -> 0.84 us
    all_to_all x4 -> x1, blocking collectives: 66 us -> 25.5 us  [exchange(): return lax.all_to_all(x, axis, split_axis=0, concat_axis=0, tiled=True)]
    all_to_all x3 -> x4, waiting for transfers between devices: 16.5 us -> 40.2 us  [exchange(): return lax.all_to_all(x, axis, split_axis=0, concat_axis=0, tiled=True)]
    ppermute x1, waiting for transfers between devices: 14.1 us -> 0.01 us  [body(): from_prev = lax.ppermute(to_next, 'seq', ups)]
    all_to_all x3 -> x4, starting transfers between devices: 22.6 us -> 31.6 us  [exchange(): return lax.all_to_all(x, axis, split_axis=0, concat_axis=0, tiled=True)]
    pallas_call x3 -> x5, Pallas kernels: 12 us -> 17.2 us  [the longest x1 5.4 us: body(): call(backward_kernel, 'backward', 1, 11, [(acc3, f32), (acc3, f32), (acc3...]
    ppermute x1, waiting for transfers between devices: 12.3 us -> 14.7 us  [body(): prev = lax.ppermute(last, 'seq', ups)]
    unnamed x21 -> x29, local copies, waits for them, and re-layouts: 4.55 us -> 4.91 us
  transfers between devices with their start and end apart: 7 -> 8, of which waited for: 7 -> 6; matrix products, arithmetic and copies ran while one was open for 1% -> 2% of each run, Pallas kernels for 0% -> 0%
where the time goes in v2:
time: 154 us; the launch traced here: 153 us
  waiting for transfers between devices  55.8 us (36%)
  starting transfers between devices  43.4 us (28%)
  blocking collectives  25.5 us (17%)
  Pallas kernels  19.5 us (13%)
  local copies, waits for them, and re-layouts  5.72 us (4%)
  other arithmetic  2.11 us (1%)
    all_to_all x4, waiting for transfers between devices, exchange(): return lax.all_to_all(x, axis, split_axis=0, concat_axis=0, tiled=True)  40.2 us
    all_to_all x4, starting transfers between devices, exchange(): return lax.all_to_all(x, axis, split_axis=0, concat_axis=0, tiled=True)  31.6 us
    all_to_all x1, blocking collectives, exchange(): return lax.all_to_all(x, axis, split_axis=0, concat_axis=0, tiled=True)  25.5 us
    ppermute x1, waiting for transfers between devices, body(): prev = lax.ppermute(last, 'seq', ups)  14.7 us
    pallas_call x1, Pallas kernels, body(): call(backward_kernel, 'backward', 1, 11, [(acc3, f32), (acc3, f32), (acc3...  5.4 us
    pallas_call x1, Pallas kernels, body(): call(forward_kernel, 'forward', 2, 7, [((blocks, BLOCK, head_dim), bf16),...  5.03 us
    unnamed x29, local copies, waits for them, and re-layouts  4.91 us
    pallas_call x1, Pallas kernels, body(): pl.pallas_call(fill_kernel, name='fill', in_specs=smem(2) + [anywhere] *...  4.07 us
  transfers between devices with their start and end apart: 8, of which 6 were waited for; matrix products, arithmetic and copies ran while one was open for 2% of the time, Pallas kernels for 0%

profile of v2, /device:TPU:8, one launch (start us, length us, event | category | flops | bytes accessed | tf_op | source)
XLA Modules:
  0.0 152.9 jit_solution(12806814719985262135)
XLA Ops:
  0.6 2.1 %scatter.1 = bf16[32,8,128]{2,1,0:T(8,128)(2,1)} custom-call(s32[2]{0:T(128)} %glob.5, bf16[8,64,128]{2,1,0:T(8,128)(2,1)} %bitcast.12, bf16[8,64,128]{2,1,0:T(8,128)(2,1)} %bitcast.16), custom_call_target="tpu_custom_call" | custom-call | tf_op jit(solution)/shard_map/scatter/pallas_call | solution.py:251
  2.7 13.0 %all-to-all-start = ((bf16[32,8,128]{2,1,0:T(8,128)(2,1)}), bf16[32,8,128]{2,1,0:T(8,128)(2,1)S(1)}, u32[]{:S(2)}, u32[]{:S(2)}) async-start(bf16[32,8,128]{2,1,0:T(8,128)(2,1)} %scatter.1), calls=%async_computation | async-start | bytes 131072 | tf_op jit(solution)/shard_map/all_to_all | solution.py:222
  15.7 0.7 fusion.2
  16.7 0.9 copy-done.1
  17.6 0.9 copy-done.3
  20.4 1.0 copy-done
  22.0 2.9 %all-to-all-done.got = bf16[32,8,128]{2,1,0:T(8,128)(2,1)S(1)} async-done(((bf16[32,8,128]{2,1,0:T(8,128)(2,1)}), bf16[32,8,128]{2,1,0:T(8,128)(2,1)S(1)}, u32[]{:S(2)}, u32[]{:S(2)}) %all-to-all-start) | async-done | bytes 65568 | tf_op jit(solution)/shard_map/all_to_all | solution.py:222
  25.6 4.1 %fill.1 = bf16[32,136,128]{2,1,0:T(8,128)(2,1)} custom-call(s32[2]{0:T(128)} %glob.5, s32[3]{0:T(128)} %pad_add_fusion.me, bf16[32,8,128]{2,1,0:T(8,128)(2,1)} %copy-done.12, bf16[32,136,128]{2,1,0:T(8,128)(2,1)} %copy-done), custom_call_target="tpu_custom_call", output_to_operand_aliasing={{}: (3, {})} | custom-call | tf_op jit(solution)/shard_map/fill/pallas_call | solution.py:271
  29.7 7.2 %all-to-all-start.1 = ((bf16[32,136,128]{2,1,0:T(8,128)(2,1)}), bf16[32,136,128]{2,1,0:T(8,128)(2,1)S(1)}, u32[]{:S(2)}, u32[]{:S(2)}) async-start(bf16[32,136,128]{2,1,0:T(8,128)(2,1)} %fill.1), calls=%async_computation.1 | async-start | bytes 2228224 | tf_op jit(solution)/shard_map/all_to_all | solution.py:222
  36.9 3.5 %collective-permute-start = (bf16[128,128]{1,0:T(8,128)(2,1)S(1)}, bf16[128,128]{1,0:T(8,128)(2,1)S(1)}, u32[]{:S(2)}, u32[]{:S(2)}) collective-permute-start(bf16[128,128]{1,0:T(8,128)(2,1)S(1)} %get-tuple-element.21), channel_id=1, source_target_pairs={{0,24},{24,48},{48,72},{72,96},{96,120},{120,144},{144,168},{168,1... | collective-permute-start | bytes 98312 | tf_op jit(solution)/shard_map/ppermute | solution.py:268
  40.4 2.5 %collective-permute-start.1 = (bf16[128,128]{1,0:T(8,128)(2,1)S(1)}, bf16[128,128]{1,0:T(8,128)(2,1)S(1)}, u32[]{:S(2)}, u32[]{:S(2)}) collective-permute-start(bf16[128,128]{1,0:T(8,128)(2,1)S(1)} %get-tuple-element.22), channel_id=1, source_target_pairs={{24,0},{48,24},{72,48},{96,72},{120,96},{144,120},{168,144},{192,1... | collective-permute-start | bytes 98312 | tf_op jit(solution)/shard_map/ppermute | solution.py:269
  43.0 14.7 %collective-permute-done.prev = bf16[128,128]{1,0:T(8,128)(2,1)S(1)} collective-permute-done((bf16[128,128]{1,0:T(8,128)(2,1)S(1)}, bf16[128,128]{1,0:T(8,128)(2,1)S(1)}, u32[]{:S(2)}, u32[]{:S(2)}) %collective-permute-start) | collective-permute-done | bytes 32800 | tf_op jit(solution)/shard_map/ppermute | solution.py:268
  57.8 0.8 collective-permute-done.1.after
  58.6 5.0 %all-to-all-done.1.incoming = bf16[32,136,128]{2,1,0:T(8,128)(2,1)S(1)} async-done(((bf16[32,136,128]{2,1,0:T(8,128)(2,1)}), bf16[32,136,128]{2,1,0:T(8,128)(2,1)S(1)}, u32[]{:S(2)}, u32[]{:S(2)}) %all-to-all-start.1) | async-done | bytes 1114144 | tf_op jit(solution)/shard_map/all_to_all | solution.py:222
  63.7 5.0 %forward.1 = (bf16[8,64,128]{2,1,0:T(8,128)(2,1)}, f32[8,64,512]{2,1,0:T(8,128)S(1)}, f32[24,1,512]{2,1,0:T(1,128)S(1)}) custom-call(s32[8,3]{1,0:T(8,128)S(1)} %copy.18.rand, s32[3]{0:T(128)S(1)} %copy-done.9, bf16[8,64,128]{2,1,0:T(8,128)(2,1)S(1)} %bitcast.20, bf16[8,64,128]{2,1,0:T(8,128)(2,1)S(1)} %bitcast.14, bf16[8,64,128]{2,1,0:T(8,128)(2,1)S(1)} %bitcast.18, ...), custom_call_target="tpu_custom_call" | custom-call | tf_op jit(solution)/shard_map/forward/pallas_call | solution.py:282
  68.7 25.5 %all_to_all.25.parts = f32[24,1,512]{2,1,0:T(1,128)S(1)} all-to-all(f32[24,1,512]{2,1,0:T(1,128)S(1)} %get-tuple-element.26), channel_id=1, replica_groups=mesh['seq'=32,'head'=24] {'head'}, dimensions={0} | all-to-all | bytes 98304 | tf_op jit(solution)/shard_map/all_to_all | solution.py:222
  94.2 5.4 %backward.1 = (f32[8,64,128]{2,1,0:T(8,128)}, f32[8,64,128]{2,1,0:T(8,128)}, f32[8,64,128]{2,1,0:T(8,128)}, bf16[32,136,128]{2,1,0:T(8,128)(2,1)}, bf16[128,128]...) custom-call(s32[8,3]{1,0:T(8,128)S(1)} %copy.18.rand, f32[24,1,512]{2,1,0:T(1,128)S(1)} %all_to_all.25.parts, ...), custom_call_target="tpu_custom_call" | custom-call | tf_op jit(solution)/shard_map/backward/pallas_call | solution.py:289
  99.6 5.5 %all-to-all-start.3 = ((bf16[32,136,128]{2,1,0:T(8,128)(2,1)}), bf16[32,136,128]{2,1,0:T(8,128)(2,1)S(1)}, u32[]{:S(2)}, u32[]{:S(2)}) async-start(bf16[32,136,128]{2,1,0:T(8,128)(2,1)} %get-tuple-element.32), calls=%async_computation.3 | async-start | bytes 2228224 | tf_op jit(solution)/shard_map/all_to_all | solution.py:222
  105.1 3.4 %collective-permute-start.2 = (bf16[128,128]{1,0:T(8,128)(2,1)S(1)}, bf16[128,128]{1,0:T(8,128)(2,1)S(1)}, u32[]{:S(2)}, u32[]{:S(2)}) collective-permute-start(bf16[128,128]{1,0:T(8,128)(2,1)S(1)} %get-tuple-element.33), channel_id=1, source_target_pairs={{0,24},{24,48},{48,72},{72,96},{96,120},{120,144},{144,168},{168,1... | collective-permute-start | bytes 98312 | tf_op jit(solution)/shard_map/ppermute | solution.py:295
  108.5 2.5 %collective-permute-start.3 = (bf16[128,128]{1,0:T(8,128)(2,1)S(1)}, bf16[128,128]{1,0:T(8,128)(2,1)S(1)}, u32[]{:S(2)}, u32[]{:S(2)}) collective-permute-start(bf16[128,128]{1,0:T(8,128)(2,1)S(1)} %get-tuple-element.34), channel_id=1, source_target_pairs={{24,0},{48,24},{72,48},{96,72},{120,96},{144,120},{168,144},{192,1... | collective-permute-start | bytes 98312 | tf_op jit(solution)/shard_map/ppermute | solution.py:296
  111.0 23.8 %all-to-all-done.3.back = bf16[32,136,128]{2,1,0:T(8,128)(2,1)S(1)} async-done(((bf16[32,136,128]{2,1,0:T(8,128)(2,1)}), bf16[32,136,128]{2,1,0:T(8,128)(2,1)S(1)}, u32[]{:S(2)}, u32[]{:S(2)}) %all-to-all-start.3) | async-done | bytes 1114144 | tf_op jit(solution)/shard_map/all_to_all | solution.py:222
  135.5 6.0 %all-to-all-start.4 = ((bf16[32,8,128]{2,1,0:T(8,128)(2,1)}), bf16[32,8,128]{2,1,0:T(8,128)(2,1)S(1)}, u32[]{:S(2)}, u32[]{:S(2)}) async-start(bf16[32,8,128]{2,1,0:T(8,128)(2,1)} %broadcast_in_dim.4), calls=%async_computation.4 | async-start | bytes 131072 | tf_op jit(solution)/shard_map/all_to_all | solution.py:222
  142.2 8.5 %all-to-all-done.4 = bf16[32,8,128]{2,1,0:T(8,128)(2,1)S(1)} async-done(((bf16[32,8,128]{2,1,0:T(8,128)(2,1)}), bf16[32,8,128]{2,1,0:T(8,128)(2,1)S(1)}, u32[]{:S(2)}, u32[]{:S(2)}) %all-to-all-start.4) | async-done | bytes 65568 | tf_op jit(solution)/shard_map/all_to_all | solution.py:222
  150.6 2.2 %final.1 = (f32[8,64,128]{2,1,0:T(8,128)}, f32[8,64,128]{2,1,0:T(8,128)}) custom-call(s32[32]{0:T(128)S(1)} %reduce_max.19.pick, s32[2]{0:T(128)S(1)} %copy-done.10, s32[3]{0:T(128)S(1)} %copy-done.9, f32[8,64,128]{2,1,0:T(8,128)} %get-tuple-element.30.acc_k, f32[8,64,128]{2,1,0:T(8,128)} %get-tuple-element.31.acc_v, ...), custom_call_target="tpu_custom_call", output_to_operand_aliasing={{0}: (3, {}), {1}: (4, {})} | custom-call | tf_op jit(solution)/shard_map/final/pallas_call | solution.py:304
  (37 shorter events, 4.9 us)
Async XLA Ops:
  2.7 22.2 %all-to-all-start = ((bf16[32,8,128]{2,1,0:T(8,128)(2,1)}), bf16[32,8,128]{2,1,0:T(8,128)(2,1)S(1)}, u32[]{:S(2)}, u32[]{:S(2)}) async-start(bf16[32,8,128]{2,1,0:T(8,128)(2,1)} %scatter.1), calls=%async_computation | async-start | bytes 131072 | tf_op jit(solution)/shard_map/all_to_all | solution.py:222
  16.7 0.9 copy-start.1
  17.6 0.9 copy-start.3
  18.5 0.7 copy-start.7
  19.2 0.7 copy-start.11
  20.4 1.0 copy-start
  24.9 0.6 copy-start.12
  29.6 13.2 %copy-start.13 = (s32[256,3]{0,1:T(4,128)S(1)}, s32[256,3]{0,1:T(4,128)}, u32[]{:S(2)}) copy-start(s32[256,3]{0,1:T(4,128)} %param.14) | copy-start | bytes 9220
  29.7 34.0 %copy-start.2 = (bf16[512,128]{1,0:T(8,128)(2,1)S(1)}, bf16[512,128]{1,0:T(8,128)(2,1)}, u32[]{:S(2)}) copy-start(bf16[512,128]{1,0:T(8,128)(2,1)} %param.9) | copy-start | bytes 393220
  29.7 34.0 %copy-start.4 = (bf16[512,128]{1,0:T(8,128)(2,1)S(1)}, bf16[512,128]{1,0:T(8,128)(2,1)}, u32[]{:S(2)}) copy-start(bf16[512,128]{1,0:T(8,128)(2,1)} %param.10) | copy-start | bytes 393220
  29.7 34.0 %copy-start.5 = (bf16[512,128]{1,0:T(8,128)(2,1)S(1)}, bf16[512,128]{1,0:T(8,128)(2,1)}, u32[]{:S(2)}) copy-start(bf16[512,128]{1,0:T(8,128)(2,1)} %param.8) | copy-start | bytes 393220
  29.7 34.0 %copy-start.9 = (s32[3]{0:T(128)S(1)}, s32[3]{0:T(128)}, u32[]{:S(2)}) copy-start(s32[3]{0:T(128)} %pad_add_fusion.me) | copy-start | bytes 40
  29.7 34.0 %all-to-all-start.1 = ((bf16[32,136,128]{2,1,0:T(8,128)(2,1)}), bf16[32,136,128]{2,1,0:T(8,128)(2,1)S(1)}, u32[]{:S(2)}, u32[]{:S(2)}) async-start(bf16[32,136,128]{2,1,0:T(8,128)(2,1)} %fill.1), calls=%async_computation.1 | async-start | bytes 2228224 | tf_op jit(solution)/shard_map/all_to_all | solution.py:222
  36.9 57.4 %copy-start.6 = (bf16[512,128]{1,0:T(8,128)(2,1)S(1)}, bf16[512,128]{1,0:T(8,128)(2,1)}, u32[]{:S(2)}) copy-start(bf16[512,128]{1,0:T(8,128)(2,1)} %param.11) | copy-start | bytes 393220
  36.9 20.9 %collective-permute-start = (bf16[128,128]{1,0:T(8,128)(2,1)S(1)}, bf16[128,128]{1,0:T(8,128)(2,1)S(1)}, u32[]{:S(2)}, u32[]{:S(2)}) collective-permute-start(bf16[128,128]{1,0:T(8,128)(2,1)S(1)} %get-tuple-element.21), channel_id=1, source_target_pairs={{0,24},{24,48},{48,72},{72,96},{96,120},{120,144},{144,168},{168,1... | collective-permute-start | bytes 98312 | tf_op jit(solution)/shard_map/ppermute | solution.py:268
  40.4 18.2 %collective-permute-start.1 = (bf16[128,128]{1,0:T(8,128)(2,1)S(1)}, bf16[128,128]{1,0:T(8,128)(2,1)S(1)}, u32[]{:S(2)}, u32[]{:S(2)}) collective-permute-start(bf16[128,128]{1,0:T(8,128)(2,1)S(1)} %get-tuple-element.22), channel_id=1, source_target_pairs={{24,0},{48,24},{72,48},{96,72},{120,96},{144,120},{168,144},{192,1... | collective-permute-start | bytes 98312 | tf_op jit(solution)/shard_map/ppermute | solution.py:269
  99.6 41.9 %copy-start.8 = (s32[512]{0:T(512)S(1)}, s32[512]{0:T(512)}, u32[]{:S(2)}) copy-start(s32[512]{0:T(512)} %param.13) | copy-start | bytes 6148
  99.6 51.0 %copy-start.10 = (s32[2]{0:T(128)S(1)}, s32[2]{0:T(128)}, u32[]{:S(2)}) copy-start(s32[2]{0:T(128)} %glob.5) | copy-start | bytes 28
  99.6 35.2 %all-to-all-start.3 = ((bf16[32,136,128]{2,1,0:T(8,128)(2,1)}), bf16[32,136,128]{2,1,0:T(8,128)(2,1)S(1)}, u32[]{:S(2)}, u32[]{:S(2)}) async-start(bf16[32,136,128]{2,1,0:T(8,128)(2,1)} %get-tuple-element.32), calls=%async_computation.3 | async-start | bytes 2228224 | tf_op jit(solution)/shard_map/all_to_all | solution.py:222
  105.1 37.0 %collective-permute-start.2 = (bf16[128,128]{1,0:T(8,128)(2,1)S(1)}, bf16[128,128]{1,0:T(8,128)(2,1)S(1)}, u32[]{:S(2)}, u32[]{:S(2)}) collective-permute-start(bf16[128,128]{1,0:T(8,128)(2,1)S(1)} %get-tuple-element.33), channel_id=1, source_target_pairs={{0,24},{24,48},{48,72},{72,96},{96,120},{120,144},{144,168},{168,1... | collective-permute-start | bytes 98312 | tf_op jit(solution)/shard_map/ppermute | solution.py:295
  108.5 33.6 %collective-permute-start.3 = (bf16[128,128]{1,0:T(8,128)(2,1)S(1)}, bf16[128,128]{1,0:T(8,128)(2,1)S(1)}, u32[]{:S(2)}, u32[]{:S(2)}) collective-permute-start(bf16[128,128]{1,0:T(8,128)(2,1)S(1)} %get-tuple-element.34), channel_id=1, source_target_pairs={{24,0},{48,24},{72,48},{96,72},{120,96},{144,120},{168,144},{192,1... | collective-permute-start | bytes 98312 | tf_op jit(solution)/shard_map/ppermute | solution.py:296
  135.5 15.1 %all-to-all-start.4 = ((bf16[32,8,128]{2,1,0:T(8,128)(2,1)}), bf16[32,8,128]{2,1,0:T(8,128)(2,1)S(1)}, u32[]{:S(2)}, u32[]{:S(2)}) async-start(bf16[32,8,128]{2,1,0:T(8,128)(2,1)} %broadcast_in_dim.4), calls=%async_computation.4 | async-start | bytes 131072 | tf_op jit(solution)/shard_map/all_to_all | solution.py:222

commit v3 on v2

--- a/solution.py
+++ b/solution.py
@@ -29,33 +29,34 @@
     return [pl.BlockSpec(memory_space=pltpu.VMEM) for _ in range(count)]
 
 
-def call(kernel, name, n_smem, n_vmem, outs, **kw):
+def params(mib):
+    return pltpu.CompilerParams(vmem_limit_bytes=mib * 1024 * 1024)
+
+
+def call(kernel, name, n_smem, n_vmem, outs, mib, **kw):
     return pl.pallas_call(
         kernel,
         name=name,
         in_specs=smem(n_smem) + vmem(n_vmem),
         out_specs=tuple(vmem(len(outs))),
         out_shape=tuple(jax.ShapeDtypeStruct(s, d) for s, d in outs),
-        compiler_params=pltpu.CompilerParams(vmem_limit_bytes=40 * 1024 * 1024),
+        compiler_params=params(mib),
         **kw,
     )
 
 
-def scatter_kernel(glob, k, v, gsend, staged, sems):
+def scatter_kernel(glob, k, v, out, sems):
     blocks = k.shape[0]
     copies = []
     for g in range(GLOBAL):
         at = glob[g] % blocks
         for n, src in enumerate((k, v)):
             slot = 2 * g + n
-            copies.append(pltpu.make_async_copy(src.at[at], staged.at[slot], sems.at[slot]))
+            copies.append(pltpu.make_async_copy(src.at[at], out.at[slot], sems.at[slot]))
     for copy in copies:
         copy.start()
-    per_block = BLOCK // CHUNK
-    for slot, copy in enumerate(copies):
+    for copy in copies:
         copy.wait()
-        for c in range(per_block):
-            gsend[slot * per_block + c] = staged[slot, c * CHUNK : (c + 1) * CHUNK]
 
 
 def pack_kernel(pick, k, v, weight, labels, send, first, last, weight_out, labels_out):
@@ -73,18 +74,15 @@
     labels_out[...] = labels[...].astype(jnp.float32)
 
 
-def fill_kernel(glob, me, got, send, out, sems):
+def fill_kernel(glob, me, got, send, out, wide, sem):
     del send
     shards = got.shape[0]
-    owner = glob[me[0] // (shards // GLOBAL)] // me[2]
-    copies = [
-        pltpu.make_async_copy(got.at[owner], out.at[r, 2 * BLOCK :], sems.at[r])
-        for r in range(shards)
-    ]
-    for copy in copies:
-        copy.start()
-    for copy in copies:
-        copy.wait()
+    piece = got[glob[me[0] // (shards // GLOBAL)] // me[2]]
+    for r in range(shards):
+        wide[r] = piece
+    copy = pltpu.make_async_copy(wide, out.at[:, 2 * BLOCK :], sem)
+    copy.start()
+    copy.wait()
 
 
 def shared_rows(incoming, slot):
@@ -138,7 +136,7 @@
 
 def backward_kernel(
     rand, parts, labels, q, k, v, prev, after, incoming, weight, upstream, probs,
-    grad_q, acc_k, acc_v, outgoing, to_prev, to_next,
+    grad_s, grad_o, outgoing, to_prev, to_next,
 ):
     blocks = k.shape[0]
     head_dim = k.shape[2]
@@ -148,33 +146,55 @@
     slope = lax.logistic(logits) - labels[...]
     column = jnp.transpose(jnp.broadcast_to(slope, (8, slope.shape[1])))[:, :1]
     w = weight[...]
-    gk = [shared_rows(incoming, 2 * g) for g in range(GLOBAL)]
     gv = [shared_rows(incoming, 2 * g + 1) for g in range(GLOBAL)]
-    glob = [jnp.zeros((BLOCK, head_dim), jnp.float32) for _ in range(2 * GLOBAL)]
-    own = []
+    far = 3 * BLOCK
+    glob = jnp.zeros((GLOBAL * BLOCK, 2 * head_dim), jnp.float32)
     for i in range(blocks):
-        kk = slots_of(i, 0, k, prev, after, incoming, gk, rand, blocks)
         vv = slots_of(i, BLOCK, v, prev, after, incoming, gv, rand, blocks)
         p = probs[i]
         g = (upstream[i].astype(jnp.float32) + column[i * BLOCK : (i + 1) * BLOCK] * w).astype(bf16)
         dp = mm(g, vv, NT)
         dot = jnp.sum(p * dp, axis=1, keepdims=True)
         ds = (p * (dp - dot) * inv_sqrt).astype(bf16)
-        grad_q[i] = mm(ds, kk, NN)
-        dk = mm(ds, q[i], TN)
-        dv = mm(p.astype(bf16), g, TN)
+        pb = p.astype(bf16)
+        grad_s[i] = ds
+        grad_o[i] = g
+        dk = mm(ds[:, far:], q[i], TN)
+        dv = mm(pb[:, far:], g, TN)
         for j in range(RAND):
-            lo = (3 + j) * BLOCK
+            lo = j * BLOCK
             at = rand[i, j] // blocks
             outgoing[at, :BLOCK] = dk[lo : lo + BLOCK].astype(bf16)
             outgoing[at, BLOCK : 2 * BLOCK] = dv[lo : lo + BLOCK].astype(bf16)
-        for n in range(GLOBAL):
-            lo = (3 + RAND + n) * BLOCK
-            glob[2 * n] = glob[2 * n] + dk[lo : lo + BLOCK]
-            glob[2 * n + 1] = glob[2 * n + 1] + dv[lo : lo + BLOCK]
-        own.append((dk[: 3 * BLOCK], dv[: 3 * BLOCK]))
+        glob = glob + jnp.concatenate([dk[RAND * BLOCK :], dv[RAND * BLOCK :]], axis=1)
+        if i == 0:
+            to_prev[:BLOCK] = mm(ds[:, :BLOCK], q[i], TN).astype(bf16)
+            to_prev[BLOCK:] = mm(pb[:, :BLOCK], g, TN).astype(bf16)
+        if i == blocks - 1:
+            to_next[:BLOCK] = mm(ds[:, 2 * BLOCK : far], q[i], TN).astype(bf16)
+            to_next[BLOCK:] = mm(pb[:, 2 * BLOCK : far], g, TN).astype(bf16)
+    per_block = BLOCK // CHUNK
+    for n in range(2 * GLOBAL):
+        lo = (n // 2) * BLOCK
+        col = (n % 2) * head_dim
+        rows = glob[lo : lo + BLOCK, col : col + head_dim].astype(bf16)
+        outgoing[n * per_block : (n + 1) * per_block, 2 * BLOCK :] = rows.reshape(per_block, CHUNK, head_dim)
+
+
+def local_kernel(rand, q, k, prev, after, incoming, probs, grad_s, grad_o, grad_q, acc_k, acc_v):
+    blocks = k.shape[0]
+    bf16 = jnp.bfloat16
+    gk = [shared_rows(incoming, 2 * g) for g in range(GLOBAL)]
+    own = []
+    for i in range(blocks):
+        kk = slots_of(i, 0, k, prev, after, incoming, gk, rand, blocks)
+        ds = grad_s[i]
+        grad_q[i] = mm(ds, kk, NN)
+        near = 3 * BLOCK
+        dk = mm(ds[:, :near], q[i], TN)
+        dv = mm(probs[i, :, :near].astype(bf16), grad_o[i], TN)
+        own.append((dk, dv))
     for which, acc in enumerate((acc_k, acc_v)):
-        lo = which * BLOCK
         for i in range(blocks):
             total = own[i][which][BLOCK : 2 * BLOCK]
             if i < blocks - 1:
@@ -182,17 +202,10 @@
             if i > 0:
                 total = total + own[i - 1][which][2 * BLOCK :].astype(bf16).astype(jnp.float32)
             acc[i] = total
-        to_prev[lo : lo + BLOCK] = own[0][which][:BLOCK].astype(bf16)
-        to_next[lo : lo + BLOCK] = own[blocks - 1][which][2 * BLOCK :].astype(bf16)
-    per_block = BLOCK // CHUNK
-    for n in range(2 * GLOBAL):
-        rows = glob[n].astype(bf16).reshape(per_block, CHUNK, head_dim)
-        outgoing[n * per_block : (n + 1) * per_block, 2 * BLOCK :] = rows
-
-
-def final_kernel(pick, glob, me, acc_k, acc_v, back, from_prev, from_next, shared, out_k, out_v):
+
+
+def gather_kernel(pick, acc_k, acc_v, back, from_prev, from_next, out_k, out_v):
     blocks = acc_k.shape[0]
-    shards = back.shape[0]
     f32 = jnp.float32
     out_k[...] = acc_k[...]
     out_v[...] = acc_v[...]
@@ -200,7 +213,7 @@
     out_v[0] = out_v[0] + from_prev[BLOCK:].astype(f32)
     out_k[blocks - 1] = out_k[blocks - 1] + from_next[:BLOCK].astype(f32)
     out_v[blocks - 1] = out_v[blocks - 1] + from_next[BLOCK:].astype(f32)
-    for r in range(shards):
+    for r in range(back.shape[0]):
         at = pick[r]
 
         @pl.when(at >= 0)
@@ -208,6 +221,12 @@
             out_k[at] = out_k[at] + back[r, :BLOCK].astype(f32)
             out_v[at] = out_v[at] + back[r, BLOCK : 2 * BLOCK].astype(f32)
 
+
+def final_kernel(glob, me, acc_k, acc_v, shared, out_k, out_v):
+    blocks = acc_k.shape[0]
+    f32 = jnp.float32
+    out_k[...] = acc_k[...]
+    out_v[...] = acc_v[...]
     for g in range(GLOBAL):
 
         @pl.when(glob[g] // blocks == me[0])
@@ -248,50 +267,52 @@
     weight = exit_weight.reshape(1, head_dim)
 
     slot_rows = wide + CHUNK
+    anywhere = pl.BlockSpec(memory_space=pl.ANY)
     gsend = pl.pallas_call(
         scatter_kernel,
         name="scatter",
-        in_specs=smem(1) + [pl.BlockSpec(memory_space=pl.ANY)] * 2,
-        out_specs=pl.BlockSpec(memory_space=pltpu.VMEM),
-        out_shape=jax.ShapeDtypeStruct((chunks, CHUNK, head_dim), bf16),
-        scratch_shapes=[
-            pltpu.VMEM((2 * GLOBAL, BLOCK, head_dim), bf16),
-            pltpu.SemaphoreType.DMA((2 * GLOBAL,)),
-        ],
-    )(glob_blocks, k, v)
+        in_specs=smem(1) + [anywhere] * 2,
+        out_specs=anywhere,
+        out_shape=jax.ShapeDtypeStruct((2 * GLOBAL, BLOCK, head_dim), bf16),
+        scratch_shapes=[pltpu.SemaphoreType.DMA((2 * GLOBAL,))],
+    )(glob_blocks, k, v).reshape(chunks, CHUNK, head_dim)
     glob_got = exchange(gsend, "seq")
     send, first, last, w32, target = call(
         pack_kernel, "pack", 1, 4,
         [((shards, slot_rows, head_dim), bf16), ((wide, head_dim), bf16), ((wide, head_dim), bf16),
-         ((1, head_dim), f32), ((1, tokens), f32)],
+         ((1, head_dim), f32), ((1, tokens), f32)], 6,
     )(pick, k, v, weight, labels.reshape(1, tokens))
     prev = lax.ppermute(last, "seq", ups)
     after = lax.ppermute(first, "seq", downs)
-    anywhere = pl.BlockSpec(memory_space=pl.ANY)
     send = pl.pallas_call(
         fill_kernel,
         name="fill",
-        in_specs=smem(2) + [anywhere] * 2,
+        in_specs=smem(2) + vmem(1) + [anywhere],
         out_specs=anywhere,
         out_shape=jax.ShapeDtypeStruct(send.shape, send.dtype),
-        scratch_shapes=[pltpu.SemaphoreType.DMA((shards,))],
+        scratch_shapes=[pltpu.VMEM((shards, CHUNK, head_dim), bf16), pltpu.SemaphoreType.DMA(())],
         input_output_aliases={3: 0},
+        compiler_params=params(2),
     )(glob_blocks, me, glob_got, send)
     incoming = exchange(send, "seq")
 
     attended, probs, part = call(
         forward_kernel, "forward", 2, 7,
-        [((blocks, BLOCK, head_dim), bf16), ((blocks, BLOCK, keys), f32), ((heads, 1, tokens), f32)],
+        [((blocks, BLOCK, head_dim), bf16), ((blocks, BLOCK, keys), f32), ((heads, 1, tokens), f32)], 16,
     )(rand, me, q, k, v, prev, after, incoming, w32)
     parts = exchange(part, "head")
 
     acc3 = (blocks, BLOCK, head_dim)
-    grad_q, acc_k, acc_v, outgoing, to_prev, to_next = call(
+    grad_s, grad_o, outgoing, to_prev, to_next = call(
         backward_kernel, "backward", 1, 11,
-        [(acc3, f32), (acc3, f32), (acc3, f32), ((shards, slot_rows, head_dim), bf16),
-         ((wide, head_dim), bf16), ((wide, head_dim), bf16)],
+        [((blocks, BLOCK, keys), bf16), (acc3, bf16), ((shards, slot_rows, head_dim), bf16),
+         ((wide, head_dim), bf16), ((wide, head_dim), bf16)], 16,
     )(rand, parts, target, q, k, v, prev, after, incoming, w32, up, probs)
+    grad_q, acc_k, acc_v = call(local_kernel, "local", 1, 8, [(acc3, f32)] * 3, 16)(
+        rand, q, k, prev, after, incoming, probs, grad_s, grad_o
+    )
     back = exchange(outgoing, "seq")
+    back, acc_k, acc_v = lax.optimization_barrier((back, acc_k, acc_v))
     from_prev = lax.ppermute(to_next, "seq", ups)
     from_next = lax.ppermute(to_prev, "seq", downs)
     gsum = jnp.sum(back[:, wide:].astype(f32), axis=0, keepdims=True).astype(bf16)
@@ -301,10 +322,12 @@
     logits = jnp.sum(parts, axis=(0, 1))
     token_loss = jax.nn.softplus(logits) - labels.astype(f32) * logits
 
-    out_k, out_v = call(
-        final_kernel, "final", 3, 6, [(acc3, f32), (acc3, f32)],
-        input_output_aliases={3: 0, 4: 1},
-    )(pick, glob_blocks, me, acc_k, acc_v, back, from_prev, from_next, gtotal)
+    acc_k, acc_v = call(gather_kernel, "gather", 1, 5, [(acc3, f32)] * 2, 8)(
+        pick, acc_k, acc_v, back, from_prev, from_next
+    )
+    out_k, out_v = call(final_kernel, "final", 2, 3, [(acc3, f32)] * 2, 6)(
+        glob_blocks, me, acc_k, acc_v, gtotal
+    )
     flat = (tokens, head_dim)
     return (
         attended.reshape(flat),

time: 154 us -> 155 us (level)
  waiting for transfers between devices: 55.8 us -> 43.9 us
  local copies, waits for them, and re-layouts: 5.72 us -> 16.1 us
  other arithmetic: 2.11 us -> 3.66 us
    all_to_all x4, waiting for transfers between devices: 40.2 us -> 28.3 us  [exchange(): return lax.all_to_all(x, axis, split_axis=0, concat_axis=0, tiled=True)]
    unnamed x29 -> x61, local copies, waits for them, and re-layouts: 4.91 us -> 15.3 us
    pallas_call x4 -> x6, Pallas kernels: 13.8 us -> 13.8 us  [the longest x1 4.42 us: body(): call(backward_kernel, 'backward', 1, 11, [((blocks, BLOCK, keys), bf16),...]
  transfers between devices with their start and end apart: 8 -> 8, of which waited for: 6 -> 6; matrix products, arithmetic and copies ran while one was open for 2% -> 3% of each run, Pallas kernels for 0% -> 3%
where the time goes in v3:
time: 155 us; the launch traced here: 154 us
  waiting for transfers between devices  43.9 us (28%)
  starting transfers between devices  43.3 us (28%)
  blocking collectives  25.5 us (16%)
  Pallas kernels  20.5 us (13%)
  local copies, waits for them, and re-layouts  16.1 us (10%)
  other arithmetic  3.66 us (2%)
    all_to_all x4, starting transfers between devices, exchange(): return lax.all_to_all(x, axis, split_axis=0, concat_axis=0, tiled=True)  30.9 us
    all_to_all x4, waiting for transfers between devices, exchange(): return lax.all_to_all(x, axis, split_axis=0, concat_axis=0, tiled=True)  28.3 us
    all_to_all x1, blocking collectives, exchange(): return lax.all_to_all(x, axis, split_axis=0, concat_axis=0, tiled=True)  25.5 us
    unnamed x61, local copies, waits for them, and re-layouts  15.3 us
    ppermute x1, waiting for transfers between devices, body(): prev = lax.ppermute(last, 'seq', ups)  14.7 us
    pallas_call x1, Pallas kernels, body(): call(forward_kernel, 'forward', 2, 7, [((blocks, BLOCK, head_dim), bf16),...  5.03 us
    pallas_call x1, Pallas kernels, body(): call(backward_kernel, 'backward', 1, 11, [((blocks, BLOCK, keys), bf16),...  4.42 us
    pallas_call x1, Pallas kernels, body(): pl.pallas_call(scatter_kernel, name='scatter', in_specs=smem(1) + [anywhe...  3.79 us
  transfers between devices with their start and end apart: 8, of which 6 were waited for; matrix products, arithmetic and copies ran while one was open for 3% of the time, Pallas kernels for 3%

profile of v3, /device:TPU:8, one launch (start us, length us, event | category | flops | bytes accessed | tf_op | source)
XLA Modules:
  0.0 153.9 jit_solution(16211547083212023571)
XLA Ops:
  0.6 3.8 %scatter.1 = bf16[4,64,128]{2,1,0:T(8,128)(2,1)} custom-call(s32[2]{0:T(128)} %glob.5, bf16[8,64,128]{2,1,0:T(8,128)(2,1)} %bitcast.13, bf16[8,64,128]{2,1,0:T(8,128)(2,1)} %bitcast.18), custom_call_target="tpu_custom_call" | custom-call | tf_op jit(solution)/shard_map/scatter/pallas_call | solution.py:271
  4.4 13.0 %all-to-all-start = ((bf16[32,8,128]{2,1,0:T(8,128)(2,1)}), bf16[32,8,128]{2,1,0:T(8,128)(2,1)S(1)}, u32[]{:S(2)}, u32[]{:S(2)}) async-start(bf16[32,8,128]{2,1,0:T(8,128)(2,1)} %bitcast.29), calls=%async_computation | async-start | bytes 131072 | tf_op jit(solution)/shard_map/all_to_all | solution.py:241
  21.5 1.6 %pack.1 = (bf16[32,136,128]{2,1,0:T(8,128)(2,1)}, bf16[128,128]{1,0:T(8,128)(2,1)S(1)}, bf16[128,128]{1,0:T(8,128)(2,1)S(1)}, f32[1,128]{1,0:T(1,128)S(1)}, f32[1,512]{1,0:T(1,128)S(1)}) custom-call(s32[32]{0:T(128)S(1)} %reduce_max.19.pick, bf16[8,64,128]{2,1,0:T(8,128)(2,1)S(1)} %bitcast.14, bf16[8,64,128]{2,1,0:T(8,128)(2,1)S(1)} %bitcast.19, ...), custom_call_target="tpu_custom_call" | custom-call | tf_op jit(solution)/shard_map/pack/pallas_call | solution.py:280
  23.2 3.4 %all-to-all-done.got = bf16[32,8,128]{2,1,0:T(8,128)(2,1)S(1)} async-done(((bf16[32,8,128]{2,1,0:T(8,128)(2,1)}), bf16[32,8,128]{2,1,0:T(8,128)(2,1)S(1)}, u32[]{:S(2)}, u32[]{:S(2)}) %all-to-all-start) | async-done | bytes 65568 | tf_op jit(solution)/shard_map/all_to_all | solution.py:241
  27.3 1.3 fill.1
  28.6 6.6 %all-to-all-start.1 = ((bf16[32,136,128]{2,1,0:T(8,128)(2,1)}), bf16[32,136,128]{2,1,0:T(8,128)(2,1)S(1)}, u32[]{:S(2)}, u32[]{:S(2)}) async-start(bf16[32,136,128]{2,1,0:T(8,128)(2,1)} %fill.1), calls=%async_computation.1 | async-start | bytes 2228224 | tf_op jit(solution)/shard_map/all_to_all | solution.py:241
  35.2 3.5 %collective-permute-start = (bf16[128,128]{1,0:T(8,128)(2,1)S(1)}, bf16[128,128]{1,0:T(8,128)(2,1)S(1)}, u32[]{:S(2)}, u32[]{:S(2)}) collective-permute-start(bf16[128,128]{1,0:T(8,128)(2,1)S(1)} %get-tuple-element.28), channel_id=1, source_target_pairs={{0,24},{24,48},{48,72},{72,96},{96,120},{120,144},{144,168},{168,1... | collective-permute-start | bytes 98312 | tf_op jit(solution)/shard_map/ppermute | solution.py:285
  38.7 2.5 %collective-permute-start.1 = (bf16[128,128]{1,0:T(8,128)(2,1)S(1)}, bf16[128,128]{1,0:T(8,128)(2,1)S(1)}, u32[]{:S(2)}, u32[]{:S(2)}) collective-permute-start(bf16[128,128]{1,0:T(8,128)(2,1)S(1)} %get-tuple-element.29), channel_id=1, source_target_pairs={{24,0},{48,24},{72,48},{96,72},{120,96},{144,120},{168,144},{192,1... | collective-permute-start | bytes 98312 | tf_op jit(solution)/shard_map/ppermute | solution.py:286
  41.4 14.7 %collective-permute-done.prev = bf16[128,128]{1,0:T(8,128)(2,1)S(1)} collective-permute-done((bf16[128,128]{1,0:T(8,128)(2,1)S(1)}, bf16[128,128]{1,0:T(8,128)(2,1)S(1)}, u32[]{:S(2)}, u32[]{:S(2)}) %collective-permute-start) | collective-permute-done | bytes 32800 | tf_op jit(solution)/shard_map/ppermute | solution.py:285
  57.0 5.0 %all-to-all-done.1.incoming = bf16[32,136,128]{2,1,0:T(8,128)(2,1)S(1)} async-done(((bf16[32,136,128]{2,1,0:T(8,128)(2,1)}), bf16[32,136,128]{2,1,0:T(8,128)(2,1)S(1)}, u32[]{:S(2)}, u32[]{:S(2)}) %all-to-all-start.1) | async-done | bytes 1114144 | tf_op jit(solution)/shard_map/all_to_all | solution.py:241
  62.0 5.0 %forward.1 = (bf16[8,64,128]{2,1,0:T(8,128)(2,1)}, f32[8,64,512]{2,1,0:T(8,128)S(1)}, f32[24,1,512]{2,1,0:T(1,128)S(1)}) custom-call(s32[8,3]{1,0:T(8,128)S(1)} %copy.16.rand, s32[3]{0:T(128)S(1)} %pad_add_fusion.me, bf16[8,64,128]{2,1,0:T(8,128)(2,1)S(1)} %bitcast.22, bf16[8,64,128]{2,1,0:T(8,128)(2,1)S(1)} %bitcast.15, bf16[8,64,128]{2,1,0:T(8,128)(2,1)S(1)} %bitcast.20, ...), custom_call_target="tpu_custom_call" | custom-call | tf_op jit(solution)/shard_map/forward/pallas_call | solution.py:299
  67.0 25.5 %all_to_all.25.parts = f32[24,1,512]{2,1,0:T(1,128)S(1)} all-to-all(f32[24,1,512]{2,1,0:T(1,128)S(1)} %get-tuple-element.33), channel_id=1, replica_groups=mesh['seq'=32,'head'=24] {'head'}, dimensions={0} | all-to-all | bytes 98304 | tf_op jit(solution)/shard_map/all_to_all | solution.py:241
  94.1 4.4 %backward.1 = (bf16[8,64,512]{2,1,0:T(8,128)(2,1)S(1)}, bf16[8,64,128]{2,1,0:T(8,128)(2,1)S(1)}, bf16[32,136,128]{2,1,0:T(8,128)(2,1)S(1)}, bf16[128,128]{1,0:T(8,128)(2,1)S(1)}, bf16[128,128]{1,0:T(8,128)(2,1)S(1)}) custom-call(s32[8,3]{1,0:T(8,128)S(1)} %copy.16.rand, f32[24,1,512]{2,1,0:T(1,128)S(1)} %all_to_all.25.parts, ...), custom_call_target="tpu_custom_call" | custom-call | tf_op jit(solution)/shard_map/backward/pallas_call | solution.py:306
  101.6 5.4 %all-to-all-start.3 = ((bf16[32,136,128]{2,1,0:T(8,128)(2,1)}), bf16[32,136,128]{2,1,0:T(8,128)(2,1)S(1)}, u32[]{:S(2)}, u32[]{:S(2)}) async-start(bf16[32,136,128]{2,1,0:T(8,128)(2,1)} %copy-done.5), calls=%async_computation.3 | async-start | bytes 2228224 | tf_op jit(solution)/shard_map/all_to_all | solution.py:241
  107.0 3.4 %collective-permute-start.2 = (bf16[128,128]{1,0:T(8,128)(2,1)}, bf16[128,128]{1,0:T(8,128)(2,1)}, u32[]{:S(2)}, u32[]{:S(2)}) collective-permute-start(bf16[128,128]{1,0:T(8,128)(2,1)} %copy-done.28), channel_id=1, source_target_pairs={{0,24},{24,48},{48,72},{72,96},{96,120},{120,144},{144,168},{168,1... | collective-permute-start | bytes 98312 | tf_op jit(solution)/shard_map/ppermute | solution.py:316
  110.4 3.1 %collective-permute-start.3 = (bf16[128,128]{1,0:T(8,128)(2,1)}, bf16[128,128]{1,0:T(8,128)(2,1)}, u32[]{:S(2)}, u32[]{:S(2)}) collective-permute-start(bf16[128,128]{1,0:T(8,128)(2,1)} %copy-done.27), channel_id=1, source_target_pairs={{24,0},{48,24},{72,48},{96,72},{120,96},{144,120},{168,144},{192,1... | collective-permute-start | bytes 98312 | tf_op jit(solution)/shard_map/ppermute | solution.py:317
  113.5 1.4 reduce_sum.21
  118.3 1.8 %local.1 = (f32[8,64,128]{2,1,0:T(8,128)}, f32[8,64,128]{2,1,0:T(8,128)S(1)}, f32[8,64,128]{2,1,0:T(8,128)S(1)}) custom-call(s32[8,3]{1,0:T(8,128)S(1)} %copy.16.rand, bf16[8,64,128]{2,1,0:T(8,128)(2,1)S(1)} %bitcast.24, bf16[8,64,128]{2,1,0:T(8,128)(2,1)S(1)} %bitcast.17, bf16[128,128]{1,0:T(8,128)(2,1)S(1)} %copy-done.11, bf16[128,128]{1,0:T(8,128)(2,1)S(1)} %copy-done.14, ...), custom_call_target="tpu_custom_call" | custom-call | tf_op jit(solution)/shard_map/local/pallas_call | solution.py:311
  121.6 15.1 %all-to-all-done.3.back = bf16[32,136,128]{2,1,0:T(8,128)(2,1)S(1)} async-done(((bf16[32,136,128]{2,1,0:T(8,128)(2,1)}), bf16[32,136,128]{2,1,0:T(8,128)(2,1)S(1)}, u32[]{:S(2)}, u32[]{:S(2)}) %all-to-all-start.3) | async-done | bytes 1114144 | tf_op jit(solution)/shard_map/all_to_all | solution.py:241
  137.4 6.0 %all-to-all-start.4 = ((bf16[32,8,128]{2,1,0:T(8,128)(2,1)}), bf16[32,8,128]{2,1,0:T(8,128)(2,1)S(1)}, u32[]{:S(2)}, u32[]{:S(2)}) async-start(bf16[32,8,128]{2,1,0:T(8,128)(2,1)} %broadcast_in_dim.4), calls=%async_computation.4 | async-start | bytes 131072 | tf_op jit(solution)/shard_map/all_to_all | solution.py:241
  143.4 1.3 fusion.4
  146.6 1.2 gather.1
  147.8 4.7 %all-to-all-done.4 = bf16[32,8,128]{2,1,0:T(8,128)(2,1)S(1)} async-done(((bf16[32,8,128]{2,1,0:T(8,128)(2,1)}), bf16[32,8,128]{2,1,0:T(8,128)(2,1)S(1)}, u32[]{:S(2)}, u32[]{:S(2)}) %all-to-all-start.4) | async-done | bytes 65568 | tf_op jit(solution)/shard_map/all_to_all | solution.py:241
  152.5 1.4 final.1
  (71 shorter events, 17.9 us)
Async XLA Ops:
  4.4 22.2 %all-to-all-start = ((bf16[32,8,128]{2,1,0:T(8,128)(2,1)}), bf16[32,8,128]{2,1,0:T(8,128)(2,1)S(1)}, u32[]{:S(2)}, u32[]{:S(2)}) async-start(bf16[32,8,128]{2,1,0:T(8,128)(2,1)} %bitcast.29), calls=%async_computation | async-start | bytes 131072 | tf_op jit(solution)/shard_map/all_to_all | solution.py:241
  18.3 0.9 copy-start
  28.6 12.7 %copy-start.29 = (s32[256,3]{0,1:T(4,128)S(1)}, s32[256,3]{0,1:T(4,128)}, u32[]{:S(2)}) copy-start(s32[256,3]{0,1:T(4,128)} %param.14) | copy-start | bytes 9220
  28.6 33.4 %copy-start.1 = (bf16[512,128]{1,0:T(8,128)(2,1)S(1)}, bf16[512,128]{1,0:T(8,128)(2,1)}, u32[]{:S(2)}) copy-start(bf16[512,128]{1,0:T(8,128)(2,1)} %param.9) | copy-start | bytes 393220
  28.6 33.4 %copy-start.3 = (bf16[512,128]{1,0:T(8,128)(2,1)S(1)}, bf16[512,128]{1,0:T(8,128)(2,1)}, u32[]{:S(2)}) copy-start(bf16[512,128]{1,0:T(8,128)(2,1)} %param.10) | copy-start | bytes 393220
  28.6 33.4 %copy-start.4 = (bf16[512,128]{1,0:T(8,128)(2,1)S(1)}, bf16[512,128]{1,0:T(8,128)(2,1)}, u32[]{:S(2)}) copy-start(bf16[512,128]{1,0:T(8,128)(2,1)} %param.8) | copy-start | bytes 393220
  28.6 33.4 %all-to-all-start.1 = ((bf16[32,136,128]{2,1,0:T(8,128)(2,1)}), bf16[32,136,128]{2,1,0:T(8,128)(2,1)S(1)}, u32[]{:S(2)}, u32[]{:S(2)}) async-start(bf16[32,136,128]{2,1,0:T(8,128)(2,1)} %fill.1), calls=%async_computation.1 | async-start | bytes 2228224 | tf_op jit(solution)/shard_map/all_to_all | solution.py:241
  35.2 57.4 %copy-start.21 = (bf16[512,128]{1,0:T(8,128)(2,1)S(1)}, bf16[512,128]{1,0:T(8,128)(2,1)}, u32[]{:S(2)}) copy-start(bf16[512,128]{1,0:T(8,128)(2,1)} %param.11) | copy-start | bytes 393220
  35.2 20.9 %collective-permute-start = (bf16[128,128]{1,0:T(8,128)(2,1)S(1)}, bf16[128,128]{1,0:T(8,128)(2,1)S(1)}, u32[]{:S(2)}, u32[]{:S(2)}) collective-permute-start(bf16[128,128]{1,0:T(8,128)(2,1)S(1)} %get-tuple-element.28), channel_id=1, source_target_pairs={{0,24},{24,48},{48,72},{72,96},{96,120},{120,144},{144,168},{168,1... | collective-permute-start | bytes 98312 | tf_op jit(solution)/shard_map/ppermute | solution.py:285
  38.7 18.2 %collective-permute-start.1 = (bf16[128,128]{1,0:T(8,128)(2,1)S(1)}, bf16[128,128]{1,0:T(8,128)(2,1)S(1)}, u32[]{:S(2)}, u32[]{:S(2)}) collective-permute-start(bf16[128,128]{1,0:T(8,128)(2,1)S(1)} %get-tuple-element.29), channel_id=1, source_target_pairs={{24,0},{48,24},{72,48},{96,72},{120,96},{144,120},{168,144},{192,1... | collective-permute-start | bytes 98312 | tf_op jit(solution)/shard_map/ppermute | solution.py:286
  56.1 36.4 %copy-start.9 = (bf16[128,128]{1,0:T(8,128)(2,1)}, bf16[128,128]{1,0:T(8,128)(2,1)S(1)}, u32[]{:S(2)}) copy-start(bf16[128,128]{1,0:T(8,128)(2,1)S(1)} %collective-permute-done.prev) | copy-start | bytes 98308
  57.0 35.6 %copy-start.12 = (bf16[128,128]{1,0:T(8,128)(2,1)}, bf16[128,128]{1,0:T(8,128)(2,1)S(1)}, u32[]{:S(2)}) copy-start(bf16[128,128]{1,0:T(8,128)(2,1)S(1)} %collective-permute-done.1.after) | copy-start | bytes 98308
  92.6 6.0 %copy-start.8 = (f32[24,1,512]{2,1,0:T(1,128)}, f32[24,1,512]{2,1,0:T(1,128)S(1)}, u32[]{:S(2)}) copy-start(f32[24,1,512]{2,1,0:T(1,128)S(1)} %all_to_all.25.parts) | copy-start | bytes 147460
  98.6 1.0 copy-start.5
  101.6 35.1 %all-to-all-start.3 = ((bf16[32,136,128]{2,1,0:T(8,128)(2,1)}), bf16[32,136,128]{2,1,0:T(8,128)(2,1)S(1)}, u32[]{:S(2)}, u32[]{:S(2)}) async-start(bf16[32,136,128]{2,1,0:T(8,128)(2,1)} %copy-done.5), calls=%async_computation.3 | async-start | bytes 2228224 | tf_op jit(solution)/shard_map/all_to_all | solution.py:241
  107.0 37.7 %collective-permute-start.2 = (bf16[128,128]{1,0:T(8,128)(2,1)}, bf16[128,128]{1,0:T(8,128)(2,1)}, u32[]{:S(2)}, u32[]{:S(2)}) collective-permute-start(bf16[128,128]{1,0:T(8,128)(2,1)} %copy-done.28), channel_id=1, source_target_pairs={{0,24},{24,48},{48,72},{72,96},{96,120},{120,144},{144,168},{168,1... | collective-permute-start | bytes 98312 | tf_op jit(solution)/shard_map/ppermute | solution.py:316
  110.4 34.3 %collective-permute-start.3 = (bf16[128,128]{1,0:T(8,128)(2,1)}, bf16[128,128]{1,0:T(8,128)(2,1)}, u32[]{:S(2)}, u32[]{:S(2)}) collective-permute-start(bf16[128,128]{1,0:T(8,128)(2,1)} %copy-done.27), channel_id=1, source_target_pairs={{24,0},{48,24},{72,48},{96,72},{120,96},{144,120},{168,144},{192,1... | collective-permute-start | bytes 98312 | tf_op jit(solution)/shard_map/ppermute | solution.py:317
  114.9 1.0 copy-start.7
  117.4 0.9 copy-start.20
  118.3 25.1 %copy-start.23 = (s32[512]{0:T(512)S(1)}, s32[512]{0:T(512)}, u32[]{:S(2)}) copy-start(s32[512]{0:T(512)} %param.13) | copy-start | bytes 6148
  121.6 30.9 %copy-start.25 = (s32[2]{0:T(128)S(1)}, s32[2]{0:T(128)}, u32[]{:S(2)}) copy-start(s32[2]{0:T(128)} %glob.5) | copy-start | bytes 28
  137.4 15.1 %all-to-all-start.4 = ((bf16[32,8,128]{2,1,0:T(8,128)(2,1)}), bf16[32,8,128]{2,1,0:T(8,128)(2,1)S(1)}, u32[]{:S(2)}, u32[]{:S(2)}) async-start(bf16[32,8,128]{2,1,0:T(8,128)(2,1)} %broadcast_in_dim.4), calls=%async_computation.4 | async-start | bytes 131072 | tf_op jit(solution)/shard_map/all_to_all | solution.py:241
  144.7 1.0 copy-start.16
  145.7 0.9 copy-start.18
  (14 other events, 10.0 us)

commit v4 on v1

v4 whole, which is shorter than its diff:
```python
import math

import jax
import jax.numpy as jnp
from jax import lax
from jax.experimental import pallas as pl
from jax.experimental.pallas import tpu as pltpu
from jax.sharding import PartitionSpec as P

BLOCK = 64
RAND = 3
GLOBAL = 2
CHUNK = 8

NT = (((1,), (1,)), ((), ()))
NN = (((1,), (0,)), ((), ()))
TN = (((0,), (0,)), ((), ()))


def mm(a, b, dims):
    return lax.dot_general(a, b, dims, preferred_element_type=jnp.float32)


def smem(count):
    return [pl.BlockSpec(memory_space=pltpu.SMEM) for _ in range(count)]


def vmem(count):
    return [pl.BlockSpec(memory_space=pltpu.VMEM) for _ in range(count)]


def call(kernel, name, n_smem, n_vmem, outs, mib=40, **kw):
    if mib:
        kw["compiler_params"] = pltpu.CompilerParams(vmem_limit_bytes=mib * 1024 * 1024)
    return pl.pallas_call(
        kernel,
        name=name,
        in_specs=smem(n_smem) + vmem(n_vmem),
        out_specs=tuple(vmem(len(outs))),
        out_shape=tuple(jax.ShapeDtypeStruct(s, d) for s, d in outs),
        **kw,
    )


def pack_kernel(pick, glob, k, v, send, first, last):
    blocks = k.shape[0]
    wide = 2 * BLOCK
    per_block = BLOCK // CHUNK
    for r in range(send.shape[0]):
        at = jnp.maximum(pick[r], 0)
        send[r, :BLOCK] = k[at]
        send[r, BLOCK:wide] = v[at]
    for g in range(GLOBAL):
        at = glob[g] % blocks
        for n, src in enumerate((k, v)):
            rows = src[at].reshape(per_block, CHUNK, src.shape[2])
            lo = (2 * g + n) * per_block
            send[lo : lo + per_block, wide:] = rows
    first[:BLOCK] = k[0]
    first[BLOCK:] = v[0]
    last[:BLOCK] = k[blocks - 1]
    last[BLOCK:] = v[blocks - 1]


def near_slots(i, base, local, prev, after, incoming, rand, blocks):
    parts = [
        local[i - 1] if i > 0 else prev[base : base + BLOCK],
        local[i],
        local[i + 1] if i < blocks - 1 else after[base : base + BLOCK],
    ]
    for j in range(RAND):
        parts.append(incoming[rand[i, j] // blocks, base : base + BLOCK])
    return jnp.concatenate(parts, axis=0)


def global_slots(base, shared):
    lows = [g * 2 * BLOCK + base for g in range(GLOBAL)]
    return jnp.concatenate([shared[lo : lo + BLOCK] for lo in lows], axis=0)


def near_kernel(rand, me, q, k, v, prev, after, incoming, terms, out, peak, total):
    blocks = k.shape[0]
    head_dim = k.shape[2]
    keys = (3 + RAND) * BLOCK
    inv_sqrt = 1.0 / math.sqrt(head_dim)
    lane = lax.broadcasted_iota(jnp.int32, (BLOCK, keys), 1)
    for i in range(blocks):
        kk = near_slots(i, 0, k, prev, after, incoming, rand, blocks)
        vv = near_slots(i, BLOCK, v, prev, after, incoming, rand, blocks)
        s = mm(q[i], kk, NT) * inv_sqrt
        if i == 0:
            s = jnp.where((lane < BLOCK) & (me[0] == 0), -jnp.inf, s)
        if i == blocks - 1:
            void = (lane >= 2 * BLOCK) & (lane < 3 * BLOCK)
            s = jnp.where(void & (me[0] == me[1] - 1), -jnp.inf, s)
        m = jnp.max(s, axis=1, keepdims=True)
        e = jnp.exp(s - m)
        terms[i] = e
        out[i] = mm(e.astype(jnp.bfloat16), vv, NN)
        peak[i] = jnp.broadcast_to(m, (BLOCK, head_dim))
        total[i] = jnp.broadcast_to(jnp.sum(e, axis=1, keepdims=True), (BLOCK, head_dim))


def forward_kernel(q, shared, weight, terms, out, peak, total, attended, probs, part):
    blocks = q.shape[0]
    head_dim = q.shape[2]
    near = (3 + RAND) * BLOCK
    inv_sqrt = 1.0 / math.sqrt(head_dim)
    w8 = jnp.broadcast_to(weight[...], (8, head_dim))
    gk = global_slots(0, shared)
    gv = global_slots(BLOCK, shared)
    rows = []
    for i in range(blocks):
        s = mm(q[i], gk, NT) * inv_sqrt
        old = peak[i][:, :1]
        m = jnp.maximum(old, jnp.max(s, axis=1, keepdims=True))
        e = jnp.exp(s - m)
        shift = jnp.exp(old - m)
        inv = 1.0 / (shift * total[i][:, :1] + jnp.sum(e, axis=1, keepdims=True))
        probs[i, :, :near] = terms[i] * (shift * inv)
        probs[i, :, near:] = e * inv
        a = (out[i] * shift + mm(e.astype(jnp.bfloat16), gv, NN)) * inv
        a = a.astype(jnp.bfloat16)
        attended[i] = a
        rows.append(mm(w8, a, NT)[:1])
    row = jnp.concatenate(rows, axis=1)
    for r in range(part.shape[0]):
        part[r] = row


def backward_kernel(
    rand, parts, labels, q, k, v, prev, after, incoming, shared, weight, upstream, probs,
    grad_q, acc_k, acc_v, outgoing, to_prev, to_next,
):
    blocks = k.shape[0]
    head_dim = k.shape[2]
    inv_sqrt = 1.0 / math.sqrt(head_dim)
    bf16 = jnp.bfloat16
    logits = jnp.sum(parts[...], axis=0)
    slope = lax.logistic(logits) - labels[...].astype(jnp.float32)
    column = jnp.transpose(jnp.broadcast_to(slope, (8, slope.shape[1])))[:, :1]
    w = weight[...].astype(jnp.float32)
    gk = global_slots(0, shared)
    gv = global_slots(BLOCK, shared)
    glob_k = jnp.zeros((GLOBAL * BLOCK, head_dim), jnp.float32)
    glob_v = jnp.zeros((GLOBAL * BLOCK, head_dim), jnp.float32)
    own = []
    for i in range(blocks):
        kk = near_slots(i, 0, k, prev, after, incoming, rand, blocks)
        kk = jnp.concatenate([kk, gk], axis=0)
        d = column[i * BLOCK : (i + 1) * BLOCK]
        g = (upstream[i].astype(jnp.float32) + d * w).astype(bf16)
        vv = near_slots(i, BLOCK, v, prev, after, incoming, rand, blocks)
        vv = jnp.concatenate([vv, gv], axis=0)
        p = probs[i]
        dp = mm(g, vv, NT)
        ds = (p * (dp - jnp.sum(p * dp, axis=1, keepdims=True)) * inv_sqrt).astype(bf16)
        grad_q[i] = mm(ds, kk, NN)
        dk = mm(ds, q[i], TN)
        dv = mm(p.astype(bf16), g, TN)
        for j in range(RAND):
            lo = (3 + j) * BLOCK
            at = rand[i, j] // blocks
            outgoing[at, :BLOCK] = dk[lo : lo + BLOCK].astype(bf16)
            outgoing[at, BLOCK : 2 * BLOCK] = dv[lo : lo + BLOCK].astype(bf16)
        glob_k = glob_k + dk[(3 + RAND) * BLOCK :]
        glob_v = glob_v + dv[(3 + RAND) * BLOCK :]
        own.append((dk[: 3 * BLOCK], dv[: 3 * BLOCK]))
    for which, acc in enumerate((acc_k, acc_v)):
        lo = which * BLOCK
        for i in range(blocks):
            total = own[i][which][BLOCK : 2 * BLOCK]
            if i < blocks - 1:
                total = total + own[i + 1][which][:BLOCK].astype(bf16).astype(jnp.float32)
            if i > 0:
                total = total + own[i - 1][which][2 * BLOCK :].astype(bf16).astype(jnp.float32)
            acc[i] = total
        to_prev[lo : lo + BLOCK] = own[0][which][:BLOCK].astype(bf16)
        to_next[lo : lo + BLOCK] = own[blocks - 1][which][2 * BLOCK :].astype(bf16)
    per_block = BLOCK // CHUNK
    for n in range(2 * GLOBAL):
        lo = (n // 2) * BLOCK
        rows = (glob_v if n % 2 else glob_k)[lo : lo + BLOCK].astype(bf16)
        outgoing[n * per_block : (n + 1) * per_block, 2 * BLOCK :] = rows.reshape(per_block, CHUNK, head_dim)


def gather_kernel(pick, acc_k, acc_v, back, from_prev, from_next, out_k, out_v):
    blocks = acc_k.shape[0]
    f32 = jnp.float32
    out_k[...] = acc_k[...]
    out_v[...] = acc_v[...]
    out_k[0] = out_k[0] + from_prev[:BLOCK].astype(f32)
    out_v[0] = out_v[0] + from_prev[BLOCK:].astype(f32)
    out_k[blocks - 1] = out_k[blocks - 1] + from_next[:BLOCK].astype(f32)
    out_v[blocks - 1] = out_v[blocks - 1] + from_next[BLOCK:].astype(f32)
    for r in range(back.shape[0]):
        at = pick[r]

        @pl.when(at >= 0)
        def _():
            out_k[at] = out_k[at] + back[r, :BLOCK].astype(f32)
            out_v[at] = out_v[at] + back[r, BLOCK : 2 * BLOCK].astype(f32)


def final_kernel(glob, me, acc_k, acc_v, shared, out_k, out_v):
    blocks = acc_k.shape[0]
    f32 = jnp.float32
    out_k[...] = acc_k[...]
    out_v[...] = acc_v[...]
    for g in range(GLOBAL):

        @pl.when(glob[g] // blocks == me[0])
        def _():
            at = glob[g] % blocks
            lo = g * 2 * BLOCK
            out_k[at] = out_k[at] + shared[lo : lo + BLOCK].astype(f32)
            out_v[at] = out_v[at] + shared[lo + BLOCK : lo + 2 * BLOCK].astype(f32)


def exchange(x, axis):
    return lax.all_to_all(x, axis, split_axis=0, concat_axis=0, tiled=True)


def body(queries, key_rows, value_rows, upstream, exit_weight, labels, rand_blocks, glob_blocks):
    tokens, head_dim = queries.shape
    blocks = tokens // BLOCK
    shards = lax.axis_size("seq")
    heads = lax.axis_size("head")
    myself = lax.axis_index("seq")
    bf16 = jnp.bfloat16
    f32 = jnp.float32
    keys = (3 + RAND + GLOBAL) * BLOCK
    wide = 2 * BLOCK
    ups = [(n, n + 1) for n in range(shards - 1)]
    downs = [(n + 1, n) for n in range(shards - 1)]

    me = jnp.stack([myself, jnp.full_like(myself, shards)])
    rand = lax.dynamic_slice_in_dim(rand_blocks, myself * blocks, blocks, 0)
    mine = jnp.where(rand_blocks // blocks == myself, rand_blocks % blocks, -1)
    pick = jnp.max(jnp.max(mine, axis=1).reshape(shards, blocks), axis=1)

    q = queries.reshape(blocks, BLOCK, head_dim)
    k = key_rows.reshape(blocks, BLOCK, head_dim)
    v = value_rows.reshape(blocks, BLOCK, head_dim)
    up = upstream.reshape(blocks, BLOCK, head_dim)
    weight = exit_weight.reshape(1, head_dim)
    slot_rows = wide + CHUNK
    acc3 = (blocks, BLOCK, head_dim)

    send, first, last = call(
        pack_kernel, "pack", 2, 2,
        [((shards, slot_rows, head_dim), bf16), ((wide, head_dim), bf16), ((wide, head_dim), bf16)],
        mib=None,
    )(pick, glob_blocks, k, v)
    incoming = exchange(send, "seq")
    prev = lax.ppermute(last, "seq", ups)
    after = lax.ppermute(first, "seq", downs)
    owner = glob_blocks[myself // (shards // GLOBAL)] // blocks
    piece = lax.dynamic_slice(incoming, (owner, wide, 0), (1, CHUNK, head_dim))
    shared = exchange(jnp.broadcast_to(piece, (shards, CHUNK, head_dim)), "seq")
    shared = shared.reshape(GLOBAL * wide, head_dim)

    near = (blocks, BLOCK, (3 + RAND) * BLOCK)
    terms, out, peak, total = call(
        near_kernel, "near", 2, 6, [(near, f32), (acc3, f32), (acc3, f32), (acc3, f32)]
    )(rand, me, q, k, v, prev, after, incoming)
    full = (blocks, BLOCK, keys)
    attended, probs, part = call(
        forward_kernel, "forward", 0, 7, [(acc3, bf16), (full, f32), ((heads, 1, tokens), f32)]
    )(q, shared, weight, terms, out, peak, total)
    parts = exchange(part, "head")

    grad_q, acc_k, acc_v, outgoing, to_prev, to_next = call(
        backward_kernel, "backward", 1, 12,
        [(acc3, f32), (acc3, f32), (acc3, f32), ((shards, slot_rows, head_dim), bf16),
         ((wide, head_dim), bf16), ((wide, head_dim), bf16)],
    )(
        rand, parts, labels.reshape(1, tokens), q, k, v, prev, after, incoming, shared, weight, up, probs
    )
    back = exchange(outgoing, "seq")
    from_prev = lax.ppermute(to_next, "seq", ups)
    from_next = lax.ppermute(to_prev, "seq", downs)
    gsum = jnp.sum(back[:, wide:].astype(f32), axis=0, keepdims=True).astype(bf16)
    gtotal = exchange(jnp.broadcast_to(gsum, (shards, CHUNK, head_dim)), "seq")
    gtotal = gtotal.reshape(GLOBAL * wide, head_dim)

    logits = jnp.sum(parts, axis=(0, 1))
    token_loss = jax.nn.softplus(logits) - labels.astype(f32) * logits

    acc_k, acc_v = call(gather_kernel, "gather", 1, 5, [(acc3, f32)] * 2)(
        pick, acc_k, acc_v, back, from_prev, from_next
    )
    out_k, out_v = call(final_kernel, "final", 2, 3, [(acc3, f32)] * 2)(
        glob_blocks, me, acc_k, acc_v, gtotal
    )
    flat = (tokens, head_dim)
    return (
        attended.reshape(flat),
        token_loss,
        grad_q.reshape(flat),
        out_k.reshape(flat),
        out_v.reshape(flat),
    )


def solution(mesh):
    placed = (
        P("seq", "head"),
        P("seq", "head"),
        P("seq", "head"),
        P("seq", "head"),
        P("head"),
        P("seq"),
        P(),
        P(),
    )
    return jax.shard_map(
        body,
        mesh=mesh,
        in_specs=placed,
        out_specs=(
            P("seq", "head"),
            P("seq"),
            P("seq", "head"),
            P("seq", "head"),
            P("seq", "head"),
        ),
        check_vma=False,
    )
```

time: 169 us -> 146 us (0.86)
  blocking collectives: 66 us -> 25.5 us
  waiting for transfers between devices: 44.6 us -> 55.4 us
  starting transfers between devices: 34.3 us -> 41.8 us
  local copies, waits for them, and re-layouts: 5.32 us -> 2.17 us
    all_to_all x4 -> x1, blocking collectives: 66 us -> 25.5 us  [exchange(): return lax.all_to_all(x, axis, split_axis=0, concat_axis=0, tiled=True)]
    all_to_all x3 -> x4, waiting for transfers between devices: 16.5 us -> 55.4 us  [exchange(): return lax.all_to_all(x, axis, split_axis=0, concat_axis=0, tiled=True)]
    ppermute x1, waiting for transfers between devices: 14.1 us -> 0.01 us  [body(): from_prev = lax.ppermute(to_next, 'seq', ups)]
    ppermute x1, waiting for transfers between devices: 12.3 us -> 0.01 us  [body(): prev = lax.ppermute(last, 'seq', ups)]
    all_to_all x3 -> x4, starting transfers between devices: 22.6 us -> 30.1 us  [exchange(): return lax.all_to_all(x, axis, split_axis=0, concat_axis=0, tiled=True)]
    unnamed x21 -> x23, local copies, waits for them, and re-layouts: 4.55 us -> 0.14 us
    pallas_call x4 -> x6, Pallas kernels: 14.2 us -> 14.7 us  [the longest x1 5.24 us: body(): call(backward_kernel, 'backward', 1, 12, [(acc3, f32), (acc3, f32), (acc3...]
  transfers between devices with their start and end apart: 7 -> 8, of which waited for: 7 -> 4; matrix products, arithmetic and copies ran while one was open for 1% -> 2% of each run, Pallas kernels for 0% -> 3%
where the time goes in v4:
time: 146 us; the launch traced here: 145 us
  waiting for transfers between devices  55.4 us (38%)
  starting transfers between devices  41.8 us (29%)
  blocking collectives  25.5 us (17%)
  Pallas kernels  14.7 us (10%)
  between operations  3.47 us (2%)
  local copies, waits for them, and re-layouts  2.17 us (1%)
  other arithmetic  2.12 us (1%)
    all_to_all x4, waiting for transfers between devices, exchange(): return lax.all_to_all(x, axis, split_axis=0, concat_axis=0, tiled=True)  55.4 us
    all_to_all x4, starting transfers between devices, exchange(): return lax.all_to_all(x, axis, split_axis=0, concat_axis=0, tiled=True)  30.1 us
    all_to_all x1, blocking collectives, exchange(): return lax.all_to_all(x, axis, split_axis=0, concat_axis=0, tiled=True)  25.5 us
    pallas_call x1, Pallas kernels, body(): call(backward_kernel, 'backward', 1, 12, [(acc3, f32), (acc3, f32), (acc3...  5.24 us
    ppermute x1, starting transfers between devices, body(): prev = lax.ppermute(last, 'seq', ups)  3.38 us
    ppermute x1, starting transfers between devices, body(): from_prev = lax.ppermute(to_next, 'seq', ups)  3.38 us
  transfers between devices with their start and end apart: 8, of which 4 were waited for; matrix products, arithmetic and copies ran while one was open for 2% of the time, Pallas kernels for 3%

profile of v4, /device:TPU:8, one launch (start us, length us, event | category | flops | bytes accessed | tf_op | source)
XLA Modules:
  0.0 145.1 jit_solution(11638363773430142708)
XLA Ops:
  0.6 0.7 fusion.2
  1.4 0.6 reduce_max.19.pick
  2.1 2.1 %pack.1 = (bf16[32,136,128]{2,1,0:T(8,128)(2,1)}, bf16[128,128]{1,0:T(8,128)(2,1)}, bf16[128,128]{1,0:T(8,128)(2,1)}) custom-call(s32[32]{0:T(128)} %reduce_max.19.pick, s32[2]{0:T(128)} %glob.3, bf16[8,64,128]{2,1,0:T(8,128)(2,1)} %bitcast.16, bf16[8,64,128]{2,1,0:T(8,128)(2,1)} %bitcast.19), custom_call_target="tpu_custom_call" | custom-call | tf_op jit(solution)/shard_map/pack/pallas_call | solution.py:250
  4.2 13.2 %all-to-all-start = ((bf16[32,136,128]{2,1,0:T(8,128)(2,1)}), bf16[32,136,128]{2,1,0:T(8,128)(2,1)S(1)}, u32[]{:S(2)}, u32[]{:S(2)}) async-start(bf16[32,136,128]{2,1,0:T(8,128)(2,1)} %get-tuple-element.25), calls=%async_computation | async-start | bytes 2228224 | tf_op jit(solution)/shard_map/all_to_all | solution.py:221
  17.4 3.4 %collective-permute-start = (bf16[128,128]{1,0:T(8,128)(2,1)S(1)}, bf16[128,128]{1,0:T(8,128)(2,1)S(1)}, u32[]{:S(2)}, u32[]{:S(2)}) collective-permute-start(bf16[128,128]{1,0:T(8,128)(2,1)S(1)} %copy-done.10), channel_id=1, source_target_pairs={{0,24},{24,48},{48,72},{72,96},{96,120},{120,144},{144,168},{168,1... | collective-permute-start | bytes 98312 | tf_op jit(solution)/shard_map/ppermute | solution.py:256
  20.8 2.5 %collective-permute-start.1 = (bf16[128,128]{1,0:T(8,128)(2,1)S(1)}, bf16[128,128]{1,0:T(8,128)(2,1)S(1)}, u32[]{:S(2)}, u32[]{:S(2)}) collective-permute-start(bf16[128,128]{1,0:T(8,128)(2,1)S(1)} %copy-done.9), channel_id=1, source_target_pairs={{24,0},{48,24},{72,48},{96,72},{120,96},{144,120},{168,144},{192,1... | collective-permute-start | bytes 98312 | tf_op jit(solution)/shard_map/ppermute | solution.py:257
  26.5 18.2 %all-to-all-done.incoming = bf16[32,136,128]{2,1,0:T(8,128)(2,1)S(1)} async-done(((bf16[32,136,128]{2,1,0:T(8,128)(2,1)}), bf16[32,136,128]{2,1,0:T(8,128)(2,1)S(1)}, u32[]{:S(2)}, u32[]{:S(2)}) %all-to-all-start) | async-done | bytes 1114144 | tf_op jit(solution)/shard_map/all_to_all | solution.py:221
  44.8 0.6 broadcast_in_dim.16
  45.4 5.4 %all-to-all-start.1 = ((bf16[32,8,128]{2,1,0:T(8,128)(2,1)}), bf16[32,8,128]{2,1,0:T(8,128)(2,1)S(1)}, u32[]{:S(2)}, u32[]{:S(2)}) async-start(bf16[32,8,128]{2,1,0:T(8,128)(2,1)} %broadcast_in_dim.16), calls=%async_computation.1 | async-start | bytes 131072 | tf_op jit(solution)/shard_map/all_to_all | solution.py:221
  51.1 2.7 %near.1 = (f32[8,64,384]{2,1,0:T(8,128)S(1)}, f32[8,64,128]{2,1,0:T(8,128)S(1)}, f32[8,64,128]{2,1,0:T(8,128)S(1)}, f32[8,64,128]{2,1,0:T(8,128)S(1)}) custom-call(s32[8,3]{1,0:T(8,128)S(1)} %copy.15.rand, s32[2]{0:T(128)S(1)} %pad_add_fusion.me, bf16[8,64,128]{2,1,0:T(8,128)(2,1)S(1)} %bitcast.22, bf16[8,64,128]{2,1,0:T(8,128)(2,1)S(1)} %bitcast.17, ...), custom_call_target="tpu_custom_call" | custom-call | tf_op jit(solution)/shard_map/near/pallas_call | solution.py:264
  53.9 6.1 %all-to-all-done.1 = bf16[32,8,128]{2,1,0:T(8,128)(2,1)S(1)} async-done(((bf16[32,8,128]{2,1,0:T(8,128)(2,1)}), bf16[32,8,128]{2,1,0:T(8,128)(2,1)S(1)}, u32[]{:S(2)}, u32[]{:S(2)}) %all-to-all-start.1) | async-done | bytes 65568 | tf_op jit(solution)/shard_map/all_to_all | solution.py:221
  59.9 2.4 %forward.1 = (bf16[8,64,128]{2,1,0:T(8,128)(2,1)}, f32[8,64,512]{2,1,0:T(8,128)S(1)}, f32[24,1,512]{2,1,0:T(1,128)S(1)}) custom-call(bf16[8,64,128]{2,1,0:T(8,128)(2,1)S(1)} %bitcast.23, bf16[256,128]{1,0:T(8,128)(2,1)S(1)} %bitcast.25, bf16[1,128]{1,0:T(2,128)(2,1)S(1)} %bitcast.30, f32[8,64,384]{2,1,0:T(8,128)S(1)} %get-tuple-element.28.terms, ...), custom_call_target="tpu_custom_call" | custom-call | tf_op jit(solution)/shard_map/forward/pallas_call | solution.py:268
  62.3 25.5 %all_to_all.25.parts = f32[24,1,512]{2,1,0:T(1,128)S(1)} all-to-all(f32[24,1,512]{2,1,0:T(1,128)S(1)} %get-tuple-element.33), channel_id=1, replica_groups=mesh['seq'=32,'head'=24] {'head'}, dimensions={0} | all-to-all | bytes 98304 | tf_op jit(solution)/shard_map/all_to_all | solution.py:221
  87.8 5.2 %backward.1 = (f32[8,64,128]{2,1,0:T(8,128)}, f32[8,64,128]{2,1,0:T(8,128)S(1)}, f32[8,64,128]{2,1,0:T(8,128)S(1)}, bf16[32,136,128]{2,1,0:T(8,128)(2,1)}, bf16[...) custom-call(s32[8,3]{1,0:T(8,128)S(1)} %copy.15.rand, f32[24,1,512]{2,1,0:T(1,128)S(1)} %all_to_all.25.parts, ...), custom_call_target="tpu_custom_call" | custom-call | tf_op jit(solution)/shard_map/backward/pallas_call | solution.py:273
  93.0 4.9 %all-to-all-start.3 = ((bf16[32,136,128]{2,1,0:T(8,128)(2,1)}), bf16[32,136,128]{2,1,0:T(8,128)(2,1)S(1)}, u32[]{:S(2)}, u32[]{:S(2)}) async-start(bf16[32,136,128]{2,1,0:T(8,128)(2,1)} %get-tuple-element.38), calls=%async_computation.3 | async-start | bytes 2228224 | tf_op jit(solution)/shard_map/all_to_all | solution.py:221
  97.9 3.4 %collective-permute-start.2 = (bf16[128,128]{1,0:T(8,128)(2,1)S(1)}, bf16[128,128]{1,0:T(8,128)(2,1)S(1)}, u32[]{:S(2)}, u32[]{:S(2)}) collective-permute-start(bf16[128,128]{1,0:T(8,128)(2,1)S(1)} %get-tuple-element.39), channel_id=1, source_target_pairs={{0,24},{24,48},{48,72},{72,96},{96,120},{120,144},{144,168},{168,1... | collective-permute-start | bytes 98312 | tf_op jit(solution)/shard_map/ppermute | solution.py:281
  101.3 2.5 %collective-permute-start.3 = (bf16[128,128]{1,0:T(8,128)(2,1)S(1)}, bf16[128,128]{1,0:T(8,128)(2,1)S(1)}, u32[]{:S(2)}, u32[]{:S(2)}) collective-permute-start(bf16[128,128]{1,0:T(8,128)(2,1)S(1)} %get-tuple-element.40), channel_id=1, source_target_pairs={{24,0},{48,24},{72,48},{96,72},{120,96},{144,120},{168,144},{192,1... | collective-permute-start | bytes 98312 | tf_op jit(solution)/shard_map/ppermute | solution.py:282
  103.8 23.5 %all-to-all-done.3.back = bf16[32,136,128]{2,1,0:T(8,128)(2,1)S(1)} async-done(((bf16[32,136,128]{2,1,0:T(8,128)(2,1)}), bf16[32,136,128]{2,1,0:T(8,128)(2,1)S(1)}, u32[]{:S(2)}, u32[]{:S(2)}) %all-to-all-start.3) | async-done | bytes 1114144 | tf_op jit(solution)/shard_map/all_to_all | solution.py:221
  127.3 0.6 broadcast_in_dim.17
  128.0 6.6 %all-to-all-start.4 = ((bf16[32,8,128]{2,1,0:T(8,128)(2,1)}), bf16[32,8,128]{2,1,0:T(8,128)(2,1)S(1)}, u32[]{:S(2)}, u32[]{:S(2)}) async-start(bf16[32,8,128]{2,1,0:T(8,128)(2,1)} %broadcast_in_dim.17), calls=%async_computation.4 | async-start | bytes 131072 | tf_op jit(solution)/shard_map/all_to_all | solution.py:221
  134.6 0.6 fusion.4
  135.2 0.9 gather.1
  136.2 7.6 %all-to-all-done.4 = bf16[32,8,128]{2,1,0:T(8,128)(2,1)S(1)} async-done(((bf16[32,8,128]{2,1,0:T(8,128)(2,1)}), bf16[32,8,128]{2,1,0:T(8,128)(2,1)S(1)}, u32[]{:S(2)}, u32[]{:S(2)}) %all-to-all-start.4) | async-done | bytes 65568 | tf_op jit(solution)/shard_map/all_to_all | solution.py:221
  143.7 1.4 final.1
  (34 shorter events, 1.1 us)
Async XLA Ops:
  4.2 13.3 %copy-start.10 = (bf16[128,128]{1,0:T(8,128)(2,1)S(1)}, bf16[128,128]{1,0:T(8,128)(2,1)}, u32[]{:S(2)}) copy-start(bf16[128,128]{1,0:T(8,128)(2,1)} %get-tuple-element.26) | copy-start | bytes 98308
  4.2 16.7 %copy-start.9 = (bf16[128,128]{1,0:T(8,128)(2,1)S(1)}, bf16[128,128]{1,0:T(8,128)(2,1)}, u32[]{:S(2)}) copy-start(bf16[128,128]{1,0:T(8,128)(2,1)} %get-tuple-element.27) | copy-start | bytes 98308
  4.2 19.2 %copy-start.6 = (s32[2]{0:T(128)S(1)}, s32[2]{0:T(128)}, u32[]{:S(2)}) copy-start(s32[2]{0:T(128)} %glob.3) | copy-start | bytes 28
  4.2 46.6 %copy-start.8 = (s32[256,3]{0,1:T(4,128)S(1)}, s32[256,3]{0,1:T(4,128)}, u32[]{:S(2)}) copy-start(s32[256,3]{0,1:T(4,128)} %param.14) | copy-start | bytes 9220
  4.2 46.9 %copy-start = (bf16[512,128]{1,0:T(8,128)(2,1)S(1)}, bf16[512,128]{1,0:T(8,128)(2,1)}, u32[]{:S(2)}) copy-start(bf16[512,128]{1,0:T(8,128)(2,1)} %param.9) | copy-start | bytes 393220
  4.2 46.9 %copy-start.1 = (bf16[512,128]{1,0:T(8,128)(2,1)S(1)}, bf16[512,128]{1,0:T(8,128)(2,1)}, u32[]{:S(2)}) copy-start(bf16[512,128]{1,0:T(8,128)(2,1)} %param.10) | copy-start | bytes 393220
  4.2 46.9 %copy-start.2 = (bf16[512,128]{1,0:T(8,128)(2,1)S(1)}, bf16[512,128]{1,0:T(8,128)(2,1)}, u32[]{:S(2)}) copy-start(bf16[512,128]{1,0:T(8,128)(2,1)} %param.8) | copy-start | bytes 393220
  4.2 40.6 %all-to-all-start = ((bf16[32,136,128]{2,1,0:T(8,128)(2,1)}), bf16[32,136,128]{2,1,0:T(8,128)(2,1)S(1)}, u32[]{:S(2)}, u32[]{:S(2)}) async-start(bf16[32,136,128]{2,1,0:T(8,128)(2,1)} %get-tuple-element.25), calls=%async_computation | async-start | bytes 2228224 | tf_op jit(solution)/shard_map/all_to_all | solution.py:221
  17.4 42.5 %copy-start.7 = (bf16[128]{0:T(256)(128)(2,1)S(1)}, bf16[128]{0:T(256)(128)(2,1)}, u32[]{:S(2)}) copy-start(bf16[128]{0:T(256)(128)(2,1)} %param.12) | copy-start | bytes 772
  17.4 33.6 %collective-permute-start = (bf16[128,128]{1,0:T(8,128)(2,1)S(1)}, bf16[128,128]{1,0:T(8,128)(2,1)S(1)}, u32[]{:S(2)}, u32[]{:S(2)}) collective-permute-start(bf16[128,128]{1,0:T(8,128)(2,1)S(1)} %copy-done.10), channel_id=1, source_target_pairs={{0,24},{24,48},{48,72},{72,96},{96,120},{120,144},{144,168},{168,1... | collective-permute-start | bytes 98312 | tf_op jit(solution)/shard_map/ppermute | solution.py:256
  20.8 30.2 %collective-permute-start.1 = (bf16[128,128]{1,0:T(8,128)(2,1)S(1)}, bf16[128,128]{1,0:T(8,128)(2,1)S(1)}, u32[]{:S(2)}, u32[]{:S(2)}) collective-permute-start(bf16[128,128]{1,0:T(8,128)(2,1)S(1)} %copy-done.9), channel_id=1, source_target_pairs={{24,0},{48,24},{72,48},{96,72},{120,96},{144,120},{168,144},{192,1... | collective-permute-start | bytes 98312 | tf_op jit(solution)/shard_map/ppermute | solution.py:257
  45.4 14.5 %all-to-all-start.1 = ((bf16[32,8,128]{2,1,0:T(8,128)(2,1)}), bf16[32,8,128]{2,1,0:T(8,128)(2,1)S(1)}, u32[]{:S(2)}, u32[]{:S(2)}) async-start(bf16[32,8,128]{2,1,0:T(8,128)(2,1)} %broadcast_in_dim.16), calls=%async_computation.1 | async-start | bytes 131072 | tf_op jit(solution)/shard_map/all_to_all | solution.py:221
  53.8 33.9 %copy-start.3 = (bf16[512,128]{1,0:T(8,128)(2,1)S(1)}, bf16[512,128]{1,0:T(8,128)(2,1)}, u32[]{:S(2)}) copy-start(bf16[512,128]{1,0:T(8,128)(2,1)} %param.11) | copy-start | bytes 393220
  53.8 33.9 %copy-start.4 = (s32[512]{0:T(512)S(1)}, s32[512]{0:T(512)}, u32[]{:S(2)}) copy-start(s32[512]{0:T(512)} %param.13) | copy-start | bytes 6148
  93.0 42.2 %copy-start.5 = (s32[32]{0:T(128)S(1)}, s32[32]{0:T(128)}, u32[]{:S(2)}) copy-start(s32[32]{0:T(128)} %reduce_max.19.pick) | copy-start | bytes 388
  93.0 34.3 %all-to-all-start.3 = ((bf16[32,136,128]{2,1,0:T(8,128)(2,1)}), bf16[32,136,128]{2,1,0:T(8,128)(2,1)S(1)}, u32[]{:S(2)}, u32[]{:S(2)}) async-start(bf16[32,136,128]{2,1,0:T(8,128)(2,1)} %get-tuple-element.38), calls=%async_computation.3 | async-start | bytes 2228224 | tf_op jit(solution)/shard_map/all_to_all | solution.py:221
  97.9 37.4 %collective-permute-start.2 = (bf16[128,128]{1,0:T(8,128)(2,1)S(1)}, bf16[128,128]{1,0:T(8,128)(2,1)S(1)}, u32[]{:S(2)}, u32[]{:S(2)}) collective-permute-start(bf16[128,128]{1,0:T(8,128)(2,1)S(1)} %get-tuple-element.39), channel_id=1, source_target_pairs={{0,24},{24,48},{48,72},{72,96},{96,120},{120,144},{144,168},{168,1... | collective-permute-start | bytes 98312 | tf_op jit(solution)/shard_map/ppermute | solution.py:281
  101.3 34.0 %collective-permute-start.3 = (bf16[128,128]{1,0:T(8,128)(2,1)S(1)}, bf16[128,128]{1,0:T(8,128)(2,1)S(1)}, u32[]{:S(2)}, u32[]{:S(2)}) collective-permute-start(bf16[128,128]{1,0:T(8,128)(2,1)S(1)} %get-tuple-element.40), channel_id=1, source_target_pairs={{24,0},{48,24},{72,48},{96,72},{120,96},{144,120},{168,144},{192,1... | collective-permute-start | bytes 98312 | tf_op jit(solution)/shard_map/ppermute | solution.py:282
  128.0 15.7 %all-to-all-start.4 = ((bf16[32,8,128]{2,1,0:T(8,128)(2,1)}), bf16[32,8,128]{2,1,0:T(8,128)(2,1)S(1)}, u32[]{:S(2)}, u32[]{:S(2)}) async-start(bf16[32,8,128]{2,1,0:T(8,128)(2,1)} %broadcast_in_dim.17), calls=%async_computation.4 | async-start | bytes 131072 | tf_op jit(solution)/shard_map/all_to_all | solution.py:221

commit v5 on v4

--- a/solution.py
+++ b/solution.py
@@ -102,28 +102,25 @@
 
 
 def forward_kernel(q, shared, weight, terms, out, peak, total, attended, probs, part):
-    blocks = q.shape[0]
-    head_dim = q.shape[2]
-    near = (3 + RAND) * BLOCK
+    blocks, _, head_dim = q.shape
+    flat = (blocks * BLOCK, head_dim)
     inv_sqrt = 1.0 / math.sqrt(head_dim)
     w8 = jnp.broadcast_to(weight[...], (8, head_dim))
-    gk = global_slots(0, shared)
-    gv = global_slots(BLOCK, shared)
-    rows = []
-    for i in range(blocks):
-        s = mm(q[i], gk, NT) * inv_sqrt
-        old = peak[i][:, :1]
-        m = jnp.maximum(old, jnp.max(s, axis=1, keepdims=True))
-        e = jnp.exp(s - m)
-        shift = jnp.exp(old - m)
-        inv = 1.0 / (shift * total[i][:, :1] + jnp.sum(e, axis=1, keepdims=True))
-        probs[i, :, :near] = terms[i] * (shift * inv)
-        probs[i, :, near:] = e * inv
-        a = (out[i] * shift + mm(e.astype(jnp.bfloat16), gv, NN)) * inv
-        a = a.astype(jnp.bfloat16)
-        attended[i] = a
-        rows.append(mm(w8, a, NT)[:1])
-    row = jnp.concatenate(rows, axis=1)
+    s = mm(q[...].reshape(flat), global_slots(0, shared), NT) * inv_sqrt
+    old = peak[...].reshape(flat)
+    m = jnp.maximum(old, jnp.max(s, axis=1, keepdims=True))
+    e = jnp.exp(s - m)
+    shift = jnp.exp(old - m)
+    inv = 1.0 / (shift * total[...].reshape(flat) + jnp.sum(e, axis=1, keepdims=True))
+    scale = (shift * inv).reshape(blocks, BLOCK, head_dim)
+    near = (3 + RAND) * BLOCK
+    for lo in range(0, near, head_dim):
+        probs[:, :, lo : lo + head_dim] = terms[:, :, lo : lo + head_dim] * scale
+    probs[:, :, near:] = (e * inv).reshape(blocks, BLOCK, head_dim)
+    a = out[...].reshape(flat) * shift + mm(e.astype(jnp.bfloat16), global_slots(BLOCK, shared), NN)
+    a = (a * inv).astype(jnp.bfloat16)
+    attended[...] = a.reshape(blocks, BLOCK, head_dim)
+    row = mm(w8, a, NT)[:1]
     for r in range(part.shape[0]):
         part[r] = row
 
@@ -144,6 +141,7 @@
     gv = global_slots(BLOCK, shared)
     glob_k = jnp.zeros((GLOBAL * BLOCK, head_dim), jnp.float32)
     glob_v = jnp.zeros((GLOBAL * BLOCK, head_dim), jnp.float32)
+    none = jnp.zeros((BLOCK, head_dim), bf16)
     own = []
     for i in range(blocks):
         kk = near_slots(i, 0, k, prev, after, incoming, rand, blocks)
@@ -156,8 +154,13 @@
         dp = mm(g, vv, NT)
         ds = (p * (dp - jnp.sum(p * dp, axis=1, keepdims=True)) * inv_sqrt).astype(bf16)
         grad_q[i] = mm(ds, kk, NN)
-        dk = mm(ds, q[i], TN)
-        dv = mm(p.astype(bf16), g, TN)
+        left = jnp.concatenate([ds, p.astype(bf16)], axis=0)
+        right = jnp.concatenate(
+            [jnp.concatenate([q[i], none], axis=1), jnp.concatenate([none, g], axis=1)], axis=0
+        )
+        both = mm(left, right, TN)
+        dk = both[:, :head_dim]
+        dv = both[:, head_dim:]
         for j in range(RAND):
             lo = (3 + j) * BLOCK
             at = rand[i, j] // blocks

time: 146 us -> 144 us (0.986)
  Pallas kernels: 14.7 us -> 13 us
where the time goes in v5:
time: 144 us; the launch traced here: 143 us
  waiting for transfers between devices  55.4 us (38%)
  starting transfers between devices  41.8 us (29%)
  blocking collectives  25.5 us (18%)
  Pallas kernels  13 us (9%)
  between operations  3.47 us (2%)
  local copies, waits for them, and re-layouts  2.17 us (2%)
  other arithmetic  2.12 us (1%)
    all_to_all x4, waiting for transfers between devices, exchange(): return lax.all_to_all(x, axis, split_axis=0, concat_axis=0, tiled=True)  55.3 us
    all_to_all x4, starting transfers between devices, exchange(): return lax.all_to_all(x, axis, split_axis=0, concat_axis=0, tiled=True)  30.1 us
    all_to_all x1, blocking collectives, exchange(): return lax.all_to_all(x, axis, split_axis=0, concat_axis=0, tiled=True)  25.5 us
    pallas_call x1, Pallas kernels, body(): call(backward_kernel, 'backward', 1, 12, [(acc3, f32), (acc3, f32), (acc3...  4.75 us
    ppermute x1, starting transfers between devices, body(): prev = lax.ppermute(last, 'seq', ups)  3.38 us
    ppermute x1, starting transfers between devices, body(): from_prev = lax.ppermute(to_next, 'seq', ups)  3.38 us
  transfers between devices with their start and end apart: 8, of which 4 were waited for; matrix products, arithmetic and copies ran while one was open for 2% of the time, Pallas kernels for 3%

profile of v5, /device:TPU:8, one launch (start us, length us, event | category | flops | bytes accessed | tf_op | source)
XLA Modules:
  0.0 143.4 jit_solution(14904039755870457966)
XLA Ops:
  0.6 0.7 fusion.2
  1.4 0.6 reduce_max.19.pick
  2.1 2.1 %pack.1 = (bf16[32,136,128]{2,1,0:T(8,128)(2,1)}, bf16[128,128]{1,0:T(8,128)(2,1)}, bf16[128,128]{1,0:T(8,128)(2,1)}) custom-call(s32[32]{0:T(128)} %reduce_max.19.pick, s32[2]{0:T(128)} %glob.3, bf16[8,64,128]{2,1,0:T(8,128)(2,1)} %bitcast.16, bf16[8,64,128]{2,1,0:T(8,128)(2,1)} %bitcast.19), custom_call_target="tpu_custom_call" | custom-call | tf_op jit(solution)/shard_map/pack/pallas_call | solution.py:253
  4.2 13.2 %all-to-all-start = ((bf16[32,136,128]{2,1,0:T(8,128)(2,1)}), bf16[32,136,128]{2,1,0:T(8,128)(2,1)S(1)}, u32[]{:S(2)}, u32[]{:S(2)}) async-start(bf16[32,136,128]{2,1,0:T(8,128)(2,1)} %get-tuple-element.25), calls=%async_computation | async-start | bytes 2228224 | tf_op jit(solution)/shard_map/all_to_all | solution.py:224
  17.4 3.4 %collective-permute-start = (bf16[128,128]{1,0:T(8,128)(2,1)S(1)}, bf16[128,128]{1,0:T(8,128)(2,1)S(1)}, u32[]{:S(2)}, u32[]{:S(2)}) collective-permute-start(bf16[128,128]{1,0:T(8,128)(2,1)S(1)} %copy-done.10), channel_id=1, source_target_pairs={{0,24},{24,48},{48,72},{72,96},{96,120},{120,144},{144,168},{168,1... | collective-permute-start | bytes 98312 | tf_op jit(solution)/shard_map/ppermute | solution.py:259
  20.8 2.5 %collective-permute-start.1 = (bf16[128,128]{1,0:T(8,128)(2,1)S(1)}, bf16[128,128]{1,0:T(8,128)(2,1)S(1)}, u32[]{:S(2)}, u32[]{:S(2)}) collective-permute-start(bf16[128,128]{1,0:T(8,128)(2,1)S(1)} %copy-done.9), channel_id=1, source_target_pairs={{24,0},{48,24},{72,48},{96,72},{120,96},{144,120},{168,144},{192,1... | collective-permute-start | bytes 98312 | tf_op jit(solution)/shard_map/ppermute | solution.py:260
  26.5 18.2 %all-to-all-done.incoming = bf16[32,136,128]{2,1,0:T(8,128)(2,1)S(1)} async-done(((bf16[32,136,128]{2,1,0:T(8,128)(2,1)}), bf16[32,136,128]{2,1,0:T(8,128)(2,1)S(1)}, u32[]{:S(2)}, u32[]{:S(2)}) %all-to-all-start) | async-done | bytes 1114144 | tf_op jit(solution)/shard_map/all_to_all | solution.py:224
  44.8 0.6 broadcast_in_dim.16
  45.4 5.4 %all-to-all-start.1 = ((bf16[32,8,128]{2,1,0:T(8,128)(2,1)}), bf16[32,8,128]{2,1,0:T(8,128)(2,1)S(1)}, u32[]{:S(2)}, u32[]{:S(2)}) async-start(bf16[32,8,128]{2,1,0:T(8,128)(2,1)} %broadcast_in_dim.16), calls=%async_computation.1 | async-start | bytes 131072 | tf_op jit(solution)/shard_map/all_to_all | solution.py:224
  51.1 2.7 %near.1 = (f32[8,64,384]{2,1,0:T(8,128)S(1)}, f32[8,64,128]{2,1,0:T(8,128)S(1)}, f32[8,64,128]{2,1,0:T(8,128)S(1)}, f32[8,64,128]{2,1,0:T(8,128)S(1)}) custom-call(s32[8,3]{1,0:T(8,128)S(1)} %copy.15.rand, s32[2]{0:T(128)S(1)} %pad_add_fusion.me, bf16[8,64,128]{2,1,0:T(8,128)(2,1)S(1)} %bitcast.22, bf16[8,64,128]{2,1,0:T(8,128)(2,1)S(1)} %bitcast.17, ...), custom_call_target="tpu_custom_call" | custom-call | tf_op jit(solution)/shard_map/near/pallas_call | solution.py:267
  53.9 6.0 %all-to-all-done.1 = bf16[32,8,128]{2,1,0:T(8,128)(2,1)S(1)} async-done(((bf16[32,8,128]{2,1,0:T(8,128)(2,1)}), bf16[32,8,128]{2,1,0:T(8,128)(2,1)S(1)}, u32[]{:S(2)}, u32[]{:S(2)}) %all-to-all-start.1) | async-done | bytes 65568 | tf_op jit(solution)/shard_map/all_to_all | solution.py:224
  59.9 1.1 forward.1
  61.1 25.5 %all_to_all.25.parts = f32[24,1,512]{2,1,0:T(1,128)S(1)} all-to-all(f32[24,1,512]{2,1,0:T(1,128)S(1)} %get-tuple-element.33), channel_id=1, replica_groups=mesh['seq'=32,'head'=24] {'head'}, dimensions={0} | all-to-all | bytes 98304 | tf_op jit(solution)/shard_map/all_to_all | solution.py:224
  86.6 4.7 %backward.1 = (f32[8,64,128]{2,1,0:T(8,128)}, f32[8,64,128]{2,1,0:T(8,128)S(1)}, f32[8,64,128]{2,1,0:T(8,128)S(1)}, bf16[32,136,128]{2,1,0:T(8,128)(2,1)}, bf16[...) custom-call(s32[8,3]{1,0:T(8,128)S(1)} %copy.15.rand, f32[24,1,512]{2,1,0:T(1,128)S(1)} %all_to_all.25.parts, ...), custom_call_target="tpu_custom_call" | custom-call | tf_op jit(solution)/shard_map/backward/pallas_call | solution.py:276
  91.3 4.9 %all-to-all-start.3 = ((bf16[32,136,128]{2,1,0:T(8,128)(2,1)}), bf16[32,136,128]{2,1,0:T(8,128)(2,1)S(1)}, u32[]{:S(2)}, u32[]{:S(2)}) async-start(bf16[32,136,128]{2,1,0:T(8,128)(2,1)} %get-tuple-element.38), calls=%async_computation.3 | async-start | bytes 2228224 | tf_op jit(solution)/shard_map/all_to_all | solution.py:224
  96.2 3.4 %collective-permute-start.2 = (bf16[128,128]{1,0:T(8,128)(2,1)S(1)}, bf16[128,128]{1,0:T(8,128)(2,1)S(1)}, u32[]{:S(2)}, u32[]{:S(2)}) collective-permute-start(bf16[128,128]{1,0:T(8,128)(2,1)S(1)} %get-tuple-element.39), channel_id=1, source_target_pairs={{0,24},{24,48},{48,72},{72,96},{96,120},{120,144},{144,168},{168,1... | collective-permute-start | bytes 98312 | tf_op jit(solution)/shard_map/ppermute | solution.py:284
  99.6 2.5 %collective-permute-start.3 = (bf16[128,128]{1,0:T(8,128)(2,1)S(1)}, bf16[128,128]{1,0:T(8,128)(2,1)S(1)}, u32[]{:S(2)}, u32[]{:S(2)}) collective-permute-start(bf16[128,128]{1,0:T(8,128)(2,1)S(1)} %get-tuple-element.40), channel_id=1, source_target_pairs={{24,0},{48,24},{72,48},{96,72},{120,96},{144,120},{168,144},{192,1... | collective-permute-start | bytes 98312 | tf_op jit(solution)/shard_map/ppermute | solution.py:285
  102.1 23.5 %all-to-all-done.3.back = bf16[32,136,128]{2,1,0:T(8,128)(2,1)S(1)} async-done(((bf16[32,136,128]{2,1,0:T(8,128)(2,1)}), bf16[32,136,128]{2,1,0:T(8,128)(2,1)S(1)}, u32[]{:S(2)}, u32[]{:S(2)}) %all-to-all-start.3) | async-done | bytes 1114144 | tf_op jit(solution)/shard_map/all_to_all | solution.py:224
  125.6 0.6 broadcast_in_dim.17
  126.3 6.6 %all-to-all-start.4 = ((bf16[32,8,128]{2,1,0:T(8,128)(2,1)}), bf16[32,8,128]{2,1,0:T(8,128)(2,1)S(1)}, u32[]{:S(2)}, u32[]{:S(2)}) async-start(bf16[32,8,128]{2,1,0:T(8,128)(2,1)} %broadcast_in_dim.17), calls=%async_computation.4 | async-start | bytes 131072 | tf_op jit(solution)/shard_map/all_to_all | solution.py:224
  132.9 0.6 fusion.4
  133.5 0.9 gather.1
  134.5 7.5 %all-to-all-done.4 = bf16[32,8,128]{2,1,0:T(8,128)(2,1)S(1)} async-done(((bf16[32,8,128]{2,1,0:T(8,128)(2,1)}), bf16[32,8,128]{2,1,0:T(8,128)(2,1)S(1)}, u32[]{:S(2)}, u32[]{:S(2)}) %all-to-all-start.4) | async-done | bytes 65568 | tf_op jit(solution)/shard_map/all_to_all | solution.py:224
  142.0 1.4 final.1
  (34 shorter events, 1.1 us)
Async XLA Ops:
  4.2 13.3 %copy-start.10 = (bf16[128,128]{1,0:T(8,128)(2,1)S(1)}, bf16[128,128]{1,0:T(8,128)(2,1)}, u32[]{:S(2)}) copy-start(bf16[128,128]{1,0:T(8,128)(2,1)} %get-tuple-element.26) | copy-start | bytes 98308
  4.2 16.7 %copy-start.9 = (bf16[128,128]{1,0:T(8,128)(2,1)S(1)}, bf16[128,128]{1,0:T(8,128)(2,1)}, u32[]{:S(2)}) copy-start(bf16[128,128]{1,0:T(8,128)(2,1)} %get-tuple-element.27) | copy-start | bytes 98308
  4.2 19.2 %copy-start.6 = (s32[2]{0:T(128)S(1)}, s32[2]{0:T(128)}, u32[]{:S(2)}) copy-start(s32[2]{0:T(128)} %glob.3) | copy-start | bytes 28
  4.2 46.6 %copy-start.8 = (s32[256,3]{0,1:T(4,128)S(1)}, s32[256,3]{0,1:T(4,128)}, u32[]{:S(2)}) copy-start(s32[256,3]{0,1:T(4,128)} %param.14) | copy-start | bytes 9220
  4.2 46.9 %copy-start = (bf16[512,128]{1,0:T(8,128)(2,1)S(1)}, bf16[512,128]{1,0:T(8,128)(2,1)}, u32[]{:S(2)}) copy-start(bf16[512,128]{1,0:T(8,128)(2,1)} %param.9) | copy-start | bytes 393220
  4.2 46.9 %copy-start.1 = (bf16[512,128]{1,0:T(8,128)(2,1)S(1)}, bf16[512,128]{1,0:T(8,128)(2,1)}, u32[]{:S(2)}) copy-start(bf16[512,128]{1,0:T(8,128)(2,1)} %param.10) | copy-start | bytes 393220
  4.2 46.9 %copy-start.2 = (bf16[512,128]{1,0:T(8,128)(2,1)S(1)}, bf16[512,128]{1,0:T(8,128)(2,1)}, u32[]{:S(2)}) copy-start(bf16[512,128]{1,0:T(8,128)(2,1)} %param.8) | copy-start | bytes 393220
  4.2 40.6 %all-to-all-start = ((bf16[32,136,128]{2,1,0:T(8,128)(2,1)}), bf16[32,136,128]{2,1,0:T(8,128)(2,1)S(1)}, u32[]{:S(2)}, u32[]{:S(2)}) async-start(bf16[32,136,128]{2,1,0:T(8,128)(2,1)} %get-tuple-element.25), calls=%async_computation | async-start | bytes 2228224 | tf_op jit(solution)/shard_map/all_to_all | solution.py:224
  17.4 42.5 %copy-start.7 = (bf16[128]{0:T(256)(128)(2,1)S(1)}, bf16[128]{0:T(256)(128)(2,1)}, u32[]{:S(2)}) copy-start(bf16[128]{0:T(256)(128)(2,1)} %param.12) | copy-start | bytes 772
  17.4 33.6 %collective-permute-start = (bf16[128,128]{1,0:T(8,128)(2,1)S(1)}, bf16[128,128]{1,0:T(8,128)(2,1)S(1)}, u32[]{:S(2)}, u32[]{:S(2)}) collective-permute-start(bf16[128,128]{1,0:T(8,128)(2,1)S(1)} %copy-done.10), channel_id=1, source_target_pairs={{0,24},{24,48},{48,72},{72,96},{96,120},{120,144},{144,168},{168,1... | collective-permute-start | bytes 98312 | tf_op jit(solution)/shard_map/ppermute | solution.py:259
  20.8 30.2 %collective-permute-start.1 = (bf16[128,128]{1,0:T(8,128)(2,1)S(1)}, bf16[128,128]{1,0:T(8,128)(2,1)S(1)}, u32[]{:S(2)}, u32[]{:S(2)}) collective-permute-start(bf16[128,128]{1,0:T(8,128)(2,1)S(1)} %copy-done.9), channel_id=1, source_target_pairs={{24,0},{48,24},{72,48},{96,72},{120,96},{144,120},{168,144},{192,1... | collective-permute-start | bytes 98312 | tf_op jit(solution)/shard_map/ppermute | solution.py:260
  45.4 14.5 %all-to-all-start.1 = ((bf16[32,8,128]{2,1,0:T(8,128)(2,1)}), bf16[32,8,128]{2,1,0:T(8,128)(2,1)S(1)}, u32[]{:S(2)}, u32[]{:S(2)}) async-start(bf16[32,8,128]{2,1,0:T(8,128)(2,1)} %broadcast_in_dim.16), calls=%async_computation.1 | async-start | bytes 131072 | tf_op jit(solution)/shard_map/all_to_all | solution.py:224
  53.8 32.7 %copy-start.3 = (bf16[512,128]{1,0:T(8,128)(2,1)S(1)}, bf16[512,128]{1,0:T(8,128)(2,1)}, u32[]{:S(2)}) copy-start(bf16[512,128]{1,0:T(8,128)(2,1)} %param.11) | copy-start | bytes 393220
  53.9 32.7 %copy-start.4 = (s32[512]{0:T(512)S(1)}, s32[512]{0:T(512)}, u32[]{:S(2)}) copy-start(s32[512]{0:T(512)} %param.13) | copy-start | bytes 6148
  91.3 42.2 %copy-start.5 = (s32[32]{0:T(128)S(1)}, s32[32]{0:T(128)}, u32[]{:S(2)}) copy-start(s32[32]{0:T(128)} %reduce_max.19.pick) | copy-start | bytes 388
  91.3 34.3 %all-to-all-start.3 = ((bf16[32,136,128]{2,1,0:T(8,128)(2,1)}), bf16[32,136,128]{2,1,0:T(8,128)(2,1)S(1)}, u32[]{:S(2)}, u32[]{:S(2)}) async-start(bf16[32,136,128]{2,1,0:T(8,128)(2,1)} %get-tuple-element.38), calls=%async_computation.3 | async-start | bytes 2228224 | tf_op jit(solution)/shard_map/all_to_all | solution.py:224
  96.2 37.4 %collective-permute-start.2 = (bf16[128,128]{1,0:T(8,128)(2,1)S(1)}, bf16[128,128]{1,0:T(8,128)(2,1)S(1)}, u32[]{:S(2)}, u32[]{:S(2)}) collective-permute-start(bf16[128,128]{1,0:T(8,128)(2,1)S(1)} %get-tuple-element.39), channel_id=1, source_target_pairs={{0,24},{24,48},{48,72},{72,96},{96,120},{120,144},{144,168},{168,1... | collective-permute-start | bytes 98312 | tf_op jit(solution)/shard_map/ppermute | solution.py:284
  99.6 34.0 %collective-permute-start.3 = (bf16[128,128]{1,0:T(8,128)(2,1)S(1)}, bf16[128,128]{1,0:T(8,128)(2,1)S(1)}, u32[]{:S(2)}, u32[]{:S(2)}) collective-permute-start(bf16[128,128]{1,0:T(8,128)(2,1)S(1)} %get-tuple-element.40), channel_id=1, source_target_pairs={{24,0},{48,24},{72,48},{96,72},{120,96},{144,120},{168,144},{192,1... | collective-permute-start | bytes 98312 | tf_op jit(solution)/shard_map/ppermute | solution.py:285
  126.3 15.7 %all-to-all-start.4 = ((bf16[32,8,128]{2,1,0:T(8,128)(2,1)}), bf16[32,8,128]{2,1,0:T(8,128)(2,1)S(1)}, u32[]{:S(2)}, u32[]{:S(2)}) async-start(bf16[32,8,128]{2,1,0:T(8,128)(2,1)} %broadcast_in_dim.17), calls=%async_computation.4 | async-start | bytes 131072 | tf_op jit(solution)/shard_map/all_to_all | solution.py:224

commit v6 on v5

--- a/solution.py
+++ b/solution.py
@@ -187,7 +187,7 @@
         outgoing[n * per_block : (n + 1) * per_block, 2 * BLOCK :] = rows.reshape(per_block, CHUNK, head_dim)
 
 
-def gather_kernel(pick, acc_k, acc_v, back, from_prev, from_next, out_k, out_v):
+def gather_kernel(pick, glob, acc_k, acc_v, back, from_prev, from_next, out_k, out_v, held):
     blocks = acc_k.shape[0]
     f32 = jnp.float32
     out_k[...] = acc_k[...]
@@ -204,20 +204,29 @@
             out_k[at] = out_k[at] + back[r, :BLOCK].astype(f32)
             out_v[at] = out_v[at] + back[r, BLOCK : 2 * BLOCK].astype(f32)
 
-
-def final_kernel(glob, me, acc_k, acc_v, shared, out_k, out_v):
-    blocks = acc_k.shape[0]
-    f32 = jnp.float32
-    out_k[...] = acc_k[...]
-    out_v[...] = acc_v[...]
+    for g in range(GLOBAL):
+        at = glob[g] % blocks
+        held[2 * g] = out_k[at]
+        held[2 * g + 1] = out_v[at]
+
+
+def final_kernel(glob, me, held, shared, in_k, in_v, out_k, out_v, summed, sems):
+    del in_k, in_v
+    blocks = out_k.shape[0]
     for g in range(GLOBAL):
 
         @pl.when(glob[g] // blocks == me[0])
         def _():
-            at = glob[g] % blocks
-            lo = g * 2 * BLOCK
-            out_k[at] = out_k[at] + shared[lo : lo + BLOCK].astype(f32)
-            out_v[at] = out_v[at] + shared[lo + BLOCK : lo + 2 * BLOCK].astype(f32)
+            copies = []
+            for n, out in enumerate((out_k, out_v)):
+                slot = 2 * g + n
+                rows = shared[slot * BLOCK : (slot + 1) * BLOCK].astype(jnp.float32)
+                summed[slot] = held[slot] + rows
+                target = out.at[glob[g] % blocks]
+                copies.append(pltpu.make_async_copy(summed.at[slot], target, sems.at[slot]))
+                copies[-1].start()
+            for copy in copies:
+                copy.wait()
 
 
 def exchange(x, axis):
@@ -290,12 +299,21 @@
     logits = jnp.sum(parts, axis=(0, 1))
     token_loss = jax.nn.softplus(logits) - labels.astype(f32) * logits
 
-    acc_k, acc_v = call(gather_kernel, "gather", 1, 5, [(acc3, f32)] * 2)(
-        pick, acc_k, acc_v, back, from_prev, from_next
-    )
-    out_k, out_v = call(final_kernel, "final", 2, 3, [(acc3, f32)] * 2)(
-        glob_blocks, me, acc_k, acc_v, gtotal
-    )
+    anywhere = pl.BlockSpec(memory_space=pl.ANY)
+    held3 = (2 * GLOBAL, BLOCK, head_dim)
+    out_k, out_v, held = call(
+        gather_kernel, "gather", 2, 5, [(acc3, f32), (acc3, f32), (held3, f32)]
+    )(pick, glob_blocks, acc_k, acc_v, back, from_prev, from_next)
+    out_k, out_v = pl.pallas_call(
+        final_kernel,
+        name="final",
+        in_specs=smem(2) + vmem(2) + [anywhere] * 2,
+        out_specs=(anywhere,) * 2,
+        out_shape=(jax.ShapeDtypeStruct(acc3, f32),) * 2,
+        scratch_shapes=[pltpu.VMEM(held3, f32), pltpu.SemaphoreType.DMA((2 * GLOBAL,))],
+        input_output_aliases={4: 0, 5: 1},
+        compiler_params=pltpu.CompilerParams(vmem_limit_bytes=4 * 1024 * 1024),
+    )(glob_blocks, me, held, gtotal, out_k, out_v)
     flat = (tokens, head_dim)
     return (
         attended.reshape(flat),

time: 144 us -> 143 us (level)
  no operation moved by 1% of the time
where the time goes in v6:
time: 143 us
  waiting for transfers between devices  54.6 us (38%)
  starting transfers between devices  41.8 us (29%)
  blocking collectives  25.5 us (18%)
  Pallas kernels  13 us (9%)
  between operations  3.47 us (2%)
  local copies, waits for them, and re-layouts  2.17 us (2%)
  other arithmetic  2.12 us (1%)
    all_to_all x4, waiting for transfers between devices, exchange(): return lax.all_to_all(x, axis, split_axis=0, concat_axis=0, tiled=True)  54.6 us
    all_to_all x4, starting transfers between devices, exchange(): return lax.all_to_all(x, axis, split_axis=0, concat_axis=0, tiled=True)  30.1 us
    all_to_all x1, blocking collectives, exchange(): return lax.all_to_all(x, axis, split_axis=0, concat_axis=0, tiled=True)  25.5 us
    pallas_call x1, Pallas kernels, body(): call(backward_kernel, 'backward', 1, 12, [(acc3, f32), (acc3, f32), (acc3...  4.75 us
    ppermute x1, starting transfers between devices, body(): prev = lax.ppermute(last, 'seq', ups)  3.38 us
    ppermute x1, starting transfers between devices, body(): from_prev = lax.ppermute(to_next, 'seq', ups)  3.38 us
  transfers between devices with their start and end apart: 8, of which 4 were waited for; matrix products, arithmetic and copies ran while one was open for 2% of the time, Pallas kernels for 3%

profile of v6, /device:TPU:8, one launch (start us, length us, event | category | flops | bytes accessed | tf_op | source)
XLA Modules:
  0.0 142.6 jit_solution(7905074464847419364)
XLA Ops:
  0.6 0.7 fusion.2
  1.4 0.6 reduce_max.19.pick
  2.1 2.1 %pack.1 = (bf16[32,136,128]{2,1,0:T(8,128)(2,1)}, bf16[128,128]{1,0:T(8,128)(2,1)}, bf16[128,128]{1,0:T(8,128)(2,1)}) custom-call(s32[32]{0:T(128)} %reduce_max.19.pick, s32[2]{0:T(128)} %glob.5, bf16[8,64,128]{2,1,0:T(8,128)(2,1)} %bitcast.16, bf16[8,64,128]{2,1,0:T(8,128)(2,1)} %bitcast.19), custom_call_target="tpu_custom_call" | custom-call | tf_op jit(solution)/shard_map/pack/pallas_call | solution.py:262
  4.2 13.2 %all-to-all-start = ((bf16[32,136,128]{2,1,0:T(8,128)(2,1)}), bf16[32,136,128]{2,1,0:T(8,128)(2,1)S(1)}, u32[]{:S(2)}, u32[]{:S(2)}) async-start(bf16[32,136,128]{2,1,0:T(8,128)(2,1)} %get-tuple-element.26), calls=%async_computation | async-start | bytes 2228224 | tf_op jit(solution)/shard_map/all_to_all | solution.py:233
  17.4 3.4 %collective-permute-start = (bf16[128,128]{1,0:T(8,128)(2,1)S(1)}, bf16[128,128]{1,0:T(8,128)(2,1)S(1)}, u32[]{:S(2)}, u32[]{:S(2)}) collective-permute-start(bf16[128,128]{1,0:T(8,128)(2,1)S(1)} %copy-done.10), channel_id=1, source_target_pairs={{0,24},{24,48},{48,72},{72,96},{96,120},{120,144},{144,168},{168,1... | collective-permute-start | bytes 98312 | tf_op jit(solution)/shard_map/ppermute | solution.py:268
  20.8 2.5 %collective-permute-start.1 = (bf16[128,128]{1,0:T(8,128)(2,1)S(1)}, bf16[128,128]{1,0:T(8,128)(2,1)S(1)}, u32[]{:S(2)}, u32[]{:S(2)}) collective-permute-start(bf16[128,128]{1,0:T(8,128)(2,1)S(1)} %copy-done.9), channel_id=1, source_target_pairs={{24,0},{48,24},{72,48},{96,72},{120,96},{144,120},{168,144},{192,1... | collective-permute-start | bytes 98312 | tf_op jit(solution)/shard_map/ppermute | solution.py:269
  26.5 18.2 %all-to-all-done.incoming = bf16[32,136,128]{2,1,0:T(8,128)(2,1)S(1)} async-done(((bf16[32,136,128]{2,1,0:T(8,128)(2,1)}), bf16[32,136,128]{2,1,0:T(8,128)(2,1)S(1)}, u32[]{:S(2)}, u32[]{:S(2)}) %all-to-all-start) | async-done | bytes 1114144 | tf_op jit(solution)/shard_map/all_to_all | solution.py:233
  44.8 0.6 broadcast_in_dim.16
  45.4 5.4 %all-to-all-start.1 = ((bf16[32,8,128]{2,1,0:T(8,128)(2,1)}), bf16[32,8,128]{2,1,0:T(8,128)(2,1)S(1)}, u32[]{:S(2)}, u32[]{:S(2)}) async-start(bf16[32,8,128]{2,1,0:T(8,128)(2,1)} %broadcast_in_dim.16), calls=%async_computation.1 | async-start | bytes 131072 | tf_op jit(solution)/shard_map/all_to_all | solution.py:233
  51.1 2.7 %near.1 = (f32[8,64,384]{2,1,0:T(8,128)S(1)}, f32[8,64,128]{2,1,0:T(8,128)S(1)}, f32[8,64,128]{2,1,0:T(8,128)S(1)}, f32[8,64,128]{2,1,0:T(8,128)S(1)}) custom-call(s32[8,3]{1,0:T(8,128)S(1)} %copy.17.rand, s32[2]{0:T(128)S(1)} %pad_add_fusion.me, bf16[8,64,128]{2,1,0:T(8,128)(2,1)S(1)} %bitcast.22, bf16[8,64,128]{2,1,0:T(8,128)(2,1)S(1)} %bitcast.17, ...), custom_call_target="tpu_custom_call" | custom-call | tf_op jit(solution)/shard_map/near/pallas_call | solution.py:276
  53.9 6.0 %all-to-all-done.1 = bf16[32,8,128]{2,1,0:T(8,128)(2,1)S(1)} async-done(((bf16[32,8,128]{2,1,0:T(8,128)(2,1)}), bf16[32,8,128]{2,1,0:T(8,128)(2,1)S(1)}, u32[]{:S(2)}, u32[]{:S(2)}) %all-to-all-start.1) | async-done | bytes 65568 | tf_op jit(solution)/shard_map/all_to_all | solution.py:233
  59.9 1.1 forward.1
  61.1 25.5 %all_to_all.25.parts = f32[24,1,512]{2,1,0:T(1,128)S(1)} all-to-all(f32[24,1,512]{2,1,0:T(1,128)S(1)} %get-tuple-element.34), channel_id=1, replica_groups=mesh['seq'=32,'head'=24] {'head'}, dimensions={0} | all-to-all | bytes 98304 | tf_op jit(solution)/shard_map/all_to_all | solution.py:233
  86.6 4.8 %backward.1 = (f32[8,64,128]{2,1,0:T(8,128)}, f32[8,64,128]{2,1,0:T(8,128)S(1)}, f32[8,64,128]{2,1,0:T(8,128)S(1)}, bf16[32,136,128]{2,1,0:T(8,128)(2,1)}, bf16[...) custom-call(s32[8,3]{1,0:T(8,128)S(1)} %copy.17.rand, f32[24,1,512]{2,1,0:T(1,128)S(1)} %all_to_all.25.parts, ...), custom_call_target="tpu_custom_call" | custom-call | tf_op jit(solution)/shard_map/backward/pallas_call | solution.py:285
  91.3 4.9 %all-to-all-start.3 = ((bf16[32,136,128]{2,1,0:T(8,128)(2,1)}), bf16[32,136,128]{2,1,0:T(8,128)(2,1)S(1)}, u32[]{:S(2)}, u32[]{:S(2)}) async-start(bf16[32,136,128]{2,1,0:T(8,128)(2,1)} %get-tuple-element.39), calls=%async_computation.3 | async-start | bytes 2228224 | tf_op jit(solution)/shard_map/all_to_all | solution.py:233
  96.2 3.4 %collective-permute-start.2 = (bf16[128,128]{1,0:T(8,128)(2,1)S(1)}, bf16[128,128]{1,0:T(8,128)(2,1)S(1)}, u32[]{:S(2)}, u32[]{:S(2)}) collective-permute-start(bf16[128,128]{1,0:T(8,128)(2,1)S(1)} %get-tuple-element.40), channel_id=1, source_target_pairs={{0,24},{24,48},{48,72},{72,96},{96,120},{120,144},{144,168},{168,1... | collective-permute-start | bytes 98312 | tf_op jit(solution)/shard_map/ppermute | solution.py:293
  99.6 2.5 %collective-permute-start.3 = (bf16[128,128]{1,0:T(8,128)(2,1)S(1)}, bf16[128,128]{1,0:T(8,128)(2,1)S(1)}, u32[]{:S(2)}, u32[]{:S(2)}) collective-permute-start(bf16[128,128]{1,0:T(8,128)(2,1)S(1)} %get-tuple-element.41), channel_id=1, source_target_pairs={{24,0},{48,24},{72,48},{96,72},{120,96},{144,120},{168,144},{192,1... | collective-permute-start | bytes 98312 | tf_op jit(solution)/shard_map/ppermute | solution.py:294
  102.1 23.5 %all-to-all-done.3.back = bf16[32,136,128]{2,1,0:T(8,128)(2,1)S(1)} async-done(((bf16[32,136,128]{2,1,0:T(8,128)(2,1)}), bf16[32,136,128]{2,1,0:T(8,128)(2,1)S(1)}, u32[]{:S(2)}, u32[]{:S(2)}) %all-to-all-start.3) | async-done | bytes 1114144 | tf_op jit(solution)/shard_map/all_to_all | solution.py:233
  125.6 0.6 broadcast_in_dim.17
  126.3 6.6 %all-to-all-start.4 = ((bf16[32,8,128]{2,1,0:T(8,128)(2,1)}), bf16[32,8,128]{2,1,0:T(8,128)(2,1)S(1)}, u32[]{:S(2)}, u32[]{:S(2)}) async-start(bf16[32,8,128]{2,1,0:T(8,128)(2,1)} %broadcast_in_dim.17), calls=%async_computation.4 | async-start | bytes 131072 | tf_op jit(solution)/shard_map/all_to_all | solution.py:233
  132.9 0.6 fusion.4
  133.5 1.7 %gather.1 = (f32[8,64,128]{2,1,0:T(8,128)}, f32[8,64,128]{2,1,0:T(8,128)}, f32[4,64,128]{2,1,0:T(8,128)S(1)}) custom-call(s32[32]{0:T(128)S(1)} %copy-done.5, s32[2]{0:T(128)S(1)} %copy-done.6, f32[8,64,128]{2,1,0:T(8,128)S(1)} %get-tuple-element.37.acc_k, f32[8,64,128]{2,1,0:T(8,128)S(1)} %get-tuple-element.38.acc_v, ...), custom_call_target="tpu_custom_call" | custom-call | tf_op jit(solution)/shard_map/gather/pallas_call | solution.py:304
  135.2 6.8 %all-to-all-done.4 = bf16[32,8,128]{2,1,0:T(8,128)(2,1)S(1)} async-done(((bf16[32,8,128]{2,1,0:T(8,128)(2,1)}), bf16[32,8,128]{2,1,0:T(8,128)(2,1)S(1)}, u32[]{:S(2)}, u32[]{:S(2)}) %all-to-all-start.4) | async-done | bytes 65568 | tf_op jit(solution)/shard_map/all_to_all | solution.py:233
  142.0 0.6 final.1
  (34 shorter events, 1.1 us)
Async XLA Ops:
  4.2 13.3 %copy-start.10 = (bf16[128,128]{1,0:T(8,128)(2,1)S(1)}, bf16[128,128]{1,0:T(8,128)(2,1)}, u32[]{:S(2)}) copy-start(bf16[128,128]{1,0:T(8,128)(2,1)} %get-tuple-element.27) | copy-start | bytes 98308
  4.2 16.7 %copy-start.9 = (bf16[128,128]{1,0:T(8,128)(2,1)S(1)}, bf16[128,128]{1,0:T(8,128)(2,1)}, u32[]{:S(2)}) copy-start(bf16[128,128]{1,0:T(8,128)(2,1)} %get-tuple-element.28) | copy-start | bytes 98308
  4.2 19.2 %copy-start.6 = (s32[2]{0:T(128)S(1)}, s32[2]{0:T(128)}, u32[]{:S(2)}) copy-start(s32[2]{0:T(128)} %glob.5) | copy-start | bytes 28
  4.2 46.6 %copy-start.8 = (s32[256,3]{0,1:T(4,128)S(1)}, s32[256,3]{0,1:T(4,128)}, u32[]{:S(2)}) copy-start(s32[256,3]{0,1:T(4,128)} %param.14) | copy-start | bytes 9220
  4.2 46.9 %copy-start = (bf16[512,128]{1,0:T(8,128)(2,1)S(1)}, bf16[512,128]{1,0:T(8,128)(2,1)}, u32[]{:S(2)}) copy-start(bf16[512,128]{1,0:T(8,128)(2,1)} %param.9) | copy-start | bytes 393220
  4.2 46.9 %copy-start.1 = (bf16[512,128]{1,0:T(8,128)(2,1)S(1)}, bf16[512,128]{1,0:T(8,128)(2,1)}, u32[]{:S(2)}) copy-start(bf16[512,128]{1,0:T(8,128)(2,1)} %param.10) | copy-start | bytes 393220
  4.2 46.9 %copy-start.2 = (bf16[512,128]{1,0:T(8,128)(2,1)S(1)}, bf16[512,128]{1,0:T(8,128)(2,1)}, u32[]{:S(2)}) copy-start(bf16[512,128]{1,0:T(8,128)(2,1)} %param.8) | copy-start | bytes 393220
  4.2 40.6 %all-to-all-start = ((bf16[32,136,128]{2,1,0:T(8,128)(2,1)}), bf16[32,136,128]{2,1,0:T(8,128)(2,1)S(1)}, u32[]{:S(2)}, u32[]{:S(2)}) async-start(bf16[32,136,128]{2,1,0:T(8,128)(2,1)} %get-tuple-element.26), calls=%async_computation | async-start | bytes 2228224 | tf_op jit(solution)/shard_map/all_to_all | solution.py:233
  17.4 42.5 %copy-start.7 = (bf16[128]{0:T(256)(128)(2,1)S(1)}, bf16[128]{0:T(256)(128)(2,1)}, u32[]{:S(2)}) copy-start(bf16[128]{0:T(256)(128)(2,1)} %param.12) | copy-start | bytes 772
  17.4 33.6 %collective-permute-start = (bf16[128,128]{1,0:T(8,128)(2,1)S(1)}, bf16[128,128]{1,0:T(8,128)(2,1)S(1)}, u32[]{:S(2)}, u32[]{:S(2)}) collective-permute-start(bf16[128,128]{1,0:T(8,128)(2,1)S(1)} %copy-done.10), channel_id=1, source_target_pairs={{0,24},{24,48},{48,72},{72,96},{96,120},{120,144},{144,168},{168,1... | collective-permute-start | bytes 98312 | tf_op jit(solution)/shard_map/ppermute | solution.py:268
  20.8 30.2 %collective-permute-start.1 = (bf16[128,128]{1,0:T(8,128)(2,1)S(1)}, bf16[128,128]{1,0:T(8,128)(2,1)S(1)}, u32[]{:S(2)}, u32[]{:S(2)}) collective-permute-start(bf16[128,128]{1,0:T(8,128)(2,1)S(1)} %copy-done.9), channel_id=1, source_target_pairs={{24,0},{48,24},{72,48},{96,72},{120,96},{144,120},{168,144},{192,1... | collective-permute-start | bytes 98312 | tf_op jit(solution)/shard_map/ppermute | solution.py:269
  45.4 14.5 %all-to-all-start.1 = ((bf16[32,8,128]{2,1,0:T(8,128)(2,1)}), bf16[32,8,128]{2,1,0:T(8,128)(2,1)S(1)}, u32[]{:S(2)}, u32[]{:S(2)}) async-start(bf16[32,8,128]{2,1,0:T(8,128)(2,1)} %broadcast_in_dim.16), calls=%async_computation.1 | async-start | bytes 131072 | tf_op jit(solution)/shard_map/all_to_all | solution.py:233
  53.8 32.7 %copy-start.3 = (bf16[512,128]{1,0:T(8,128)(2,1)S(1)}, bf16[512,128]{1,0:T(8,128)(2,1)}, u32[]{:S(2)}) copy-start(bf16[512,128]{1,0:T(8,128)(2,1)} %param.11) | copy-start | bytes 393220
  53.9 32.7 %copy-start.4 = (s32[512]{0:T(512)S(1)}, s32[512]{0:T(512)}, u32[]{:S(2)}) copy-start(s32[512]{0:T(512)} %param.13) | copy-start | bytes 6148
  91.3 42.2 %copy-start.5 = (s32[32]{0:T(128)S(1)}, s32[32]{0:T(128)}, u32[]{:S(2)}) copy-start(s32[32]{0:T(128)} %reduce_max.19.pick) | copy-start | bytes 388
  91.3 34.3 %all-to-all-start.3 = ((bf16[32,136,128]{2,1,0:T(8,128)(2,1)}), bf16[32,136,128]{2,1,0:T(8,128)(2,1)S(1)}, u32[]{:S(2)}, u32[]{:S(2)}) async-start(bf16[32,136,128]{2,1,0:T(8,128)(2,1)} %get-tuple-element.39), calls=%async_computation.3 | async-start | bytes 2228224 | tf_op jit(solution)/shard_map/all_to_all | solution.py:233
  96.2 37.4 %collective-permute-start.2 = (bf16[128,128]{1,0:T(8,128)(2,1)S(1)}, bf16[128,128]{1,0:T(8,128)(2,1)S(1)}, u32[]{:S(2)}, u32[]{:S(2)}) collective-permute-start(bf16[128,128]{1,0:T(8,128)(2,1)S(1)} %get-tuple-element.40), channel_id=1, source_target_pairs={{0,24},{24,48},{48,72},{72,96},{96,120},{120,144},{144,168},{168,1... | collective-permute-start | bytes 98312 | tf_op jit(solution)/shard_map/ppermute | solution.py:293
  99.6 34.0 %collective-permute-start.3 = (bf16[128,128]{1,0:T(8,128)(2,1)S(1)}, bf16[128,128]{1,0:T(8,128)(2,1)S(1)}, u32[]{:S(2)}, u32[]{:S(2)}) collective-permute-start(bf16[128,128]{1,0:T(8,128)(2,1)S(1)} %get-tuple-element.41), channel_id=1, source_target_pairs={{24,0},{48,24},{72,48},{96,72},{120,96},{144,120},{168,144},{192,1... | collective-permute-start | bytes 98312 | tf_op jit(solution)/shard_map/ppermute | solution.py:294
  126.3 15.7 %all-to-all-start.4 = ((bf16[32,8,128]{2,1,0:T(8,128)(2,1)}), bf16[32,8,128]{2,1,0:T(8,128)(2,1)S(1)}, u32[]{:S(2)}, u32[]{:S(2)}) async-start(bf16[32,8,128]{2,1,0:T(8,128)(2,1)} %broadcast_in_dim.17), calls=%async_computation.4 | async-start | bytes 131072 | tf_op jit(solution)/shard_map/all_to_all | solution.py:233

commit v7 on v6

--- a/solution.py
+++ b/solution.py
@@ -101,7 +101,7 @@
         total[i] = jnp.broadcast_to(jnp.sum(e, axis=1, keepdims=True), (BLOCK, head_dim))
 
 
-def forward_kernel(q, shared, weight, terms, out, peak, total, attended, probs, part):
+def forward_kernel(q, shared, weight, terms, out, peak, total, attended, mean, probs, part):
     blocks, _, head_dim = q.shape
     flat = (blocks * BLOCK, head_dim)
     inv_sqrt = 1.0 / math.sqrt(head_dim)
@@ -118,7 +118,9 @@
         probs[:, :, lo : lo + head_dim] = terms[:, :, lo : lo + head_dim] * scale
     probs[:, :, near:] = (e * inv).reshape(blocks, BLOCK, head_dim)
     a = out[...].reshape(flat) * shift + mm(e.astype(jnp.bfloat16), global_slots(BLOCK, shared), NN)
-    a = (a * inv).astype(jnp.bfloat16)
+    a = a * inv
+    mean[...] = a.reshape(blocks, BLOCK, head_dim)
+    a = a.astype(jnp.bfloat16)
     attended[...] = a.reshape(blocks, BLOCK, head_dim)
     row = mm(w8, a, NT)[:1]
     for r in range(part.shape[0]):
@@ -126,7 +128,7 @@
 
 
 def backward_kernel(
-    rand, parts, labels, q, k, v, prev, after, incoming, shared, weight, upstream, probs,
+    rand, parts, labels, q, k, v, prev, after, incoming, shared, weight, upstream, mean, probs,
     grad_q, acc_k, acc_v, outgoing, to_prev, to_next,
 ):
     blocks = k.shape[0]
@@ -152,7 +154,8 @@
         vv = jnp.concatenate([vv, gv], axis=0)
         p = probs[i]
         dp = mm(g, vv, NT)
-        ds = (p * (dp - jnp.sum(p * dp, axis=1, keepdims=True)) * inv_sqrt).astype(bf16)
+        dot = jnp.sum(g.astype(jnp.float32) * mean[i], axis=1, keepdims=True)
+        ds = (p * (dp - dot) * inv_sqrt).astype(bf16)
         grad_q[i] = mm(ds, kk, NN)
         left = jnp.concatenate([ds, p.astype(bf16)], axis=0)
         right = jnp.concatenate(
@@ -277,17 +280,17 @@
         near_kernel, "near", 2, 6, [(near, f32), (acc3, f32), (acc3, f32), (acc3, f32)]
     )(rand, me, q, k, v, prev, after, incoming)
     full = (blocks, BLOCK, keys)
-    attended, probs, part = call(
-        forward_kernel, "forward", 0, 7, [(acc3, bf16), (full, f32), ((heads, 1, tokens), f32)]
+    attended, mean, probs, part = call(
+        forward_kernel, "forward", 0, 7, [(acc3, bf16), (acc3, f32), (full, f32), ((heads, 1, tokens), f32)]
     )(q, shared, weight, terms, out, peak, total)
     parts = exchange(part, "head")
 
     grad_q, acc_k, acc_v, outgoing, to_prev, to_next = call(
-        backward_kernel, "backward", 1, 12,
+        backward_kernel, "backward", 1, 13,
         [(acc3, f32), (acc3, f32), (acc3, f32), ((shards, slot_rows, head_dim), bf16),
          ((wide, head_dim), bf16), ((wide, head_dim), bf16)],
     )(
-        rand, parts, labels.reshape(1, tokens), q, k, v, prev, after, incoming, shared, weight, up, probs
+        rand, parts, labels.reshape(1, tokens), q, k, v, prev, after, incoming, shared, weight, up, mean, probs
     )
     back = exchange(outgoing, "seq")
     from_prev = lax.ppermute(to_next, "seq", ups)

time: 143 us -> 143 us (level)
  the two profiles are of different devices: /device:TPU:8 before, /device:TPU:2 now
where the time goes in v7:
time: 143 us; the launch traced here: 142 us
  starting transfers between devices  49.4 us (35%)
  waiting for transfers between devices  46.9 us (33%)
  blocking collectives  25.5 us (18%)
  Pallas kernels  12.1 us (8%)
  between operations  3.47 us (2%)
  local copies, waits for them, and re-layouts  2.17 us (2%)
  other arithmetic  2.12 us (1%)
    all_to_all x4, waiting for transfers between devices, exchange(): return lax.all_to_all(x, axis, split_axis=0, concat_axis=0, tiled=True)  46.8 us
    all_to_all x4, starting transfers between devices, exchange(): return lax.all_to_all(x, axis, split_axis=0, concat_axis=0, tiled=True)  33.5 us
    all_to_all x1, blocking collectives, exchange(): return lax.all_to_all(x, axis, split_axis=0, concat_axis=0, tiled=True)  25.5 us
    ppermute x1, starting transfers between devices, body(): after = lax.ppermute(first, 'seq', downs)  4.57 us
    ppermute x1, starting transfers between devices, body(): from_next = lax.ppermute(to_prev, 'seq', downs)  4.57 us
    pallas_call x1, Pallas kernels, body(): call(backward_kernel, 'backward', 1, 13, [(acc3, f32), (acc3, f32), (acc3...  3.86 us
    ppermute x1, starting transfers between devices, body(): prev = lax.ppermute(last, 'seq', ups)  3.38 us
    ppermute x1, starting transfers between devices, body(): from_prev = lax.ppermute(to_next, 'seq', ups)  3.38 us
  transfers between devices with their start and end apart: 8, of which 4 were waited for; matrix products, arithmetic and copies ran while one was open for 2% of the time, Pallas kernels for 3%

profile of v7, /device:TPU:2, one launch (start us, length us, event | category | flops | bytes accessed | tf_op | source)
XLA Modules:
  0.0 141.6 jit_solution(7314982984160452662)
XLA Ops:
  0.6 0.7 fusion.2
  1.4 0.6 reduce_max.19.pick
  2.1 2.1 %pack.1 = (bf16[32,136,128]{2,1,0:T(8,128)(2,1)}, bf16[128,128]{1,0:T(8,128)(2,1)}, bf16[128,128]{1,0:T(8,128)(2,1)}) custom-call(s32[32]{0:T(128)} %reduce_max.19.pick, s32[2]{0:T(128)} %glob.5, bf16[8,64,128]{2,1,0:T(8,128)(2,1)} %bitcast.16, bf16[8,64,128]{2,1,0:T(8,128)(2,1)} %bitcast.19), custom_call_target="tpu_custom_call" | custom-call | tf_op jit(solution)/shard_map/pack/pallas_call | solution.py:265
  4.2 13.3 %all-to-all-start = ((bf16[32,136,128]{2,1,0:T(8,128)(2,1)}), bf16[32,136,128]{2,1,0:T(8,128)(2,1)S(1)}, u32[]{:S(2)}, u32[]{:S(2)}) async-start(bf16[32,136,128]{2,1,0:T(8,128)(2,1)} %get-tuple-element.27), calls=%async_computation | async-start | bytes 2228224 | tf_op jit(solution)/shard_map/all_to_all | solution.py:236
  17.6 3.4 %collective-permute-start = (bf16[128,128]{1,0:T(8,128)(2,1)S(1)}, bf16[128,128]{1,0:T(8,128)(2,1)S(1)}, u32[]{:S(2)}, u32[]{:S(2)}) collective-permute-start(bf16[128,128]{1,0:T(8,128)(2,1)S(1)} %copy-done.10), channel_id=1, source_target_pairs={{0,24},{24,48},{48,72},{72,96},{96,120},{120,144},{144,168},{168,1... | collective-permute-start | bytes 98312 | tf_op jit(solution)/shard_map/ppermute | solution.py:271
  21.0 4.6 %collective-permute-start.1 = (bf16[128,128]{1,0:T(8,128)(2,1)S(1)}, bf16[128,128]{1,0:T(8,128)(2,1)S(1)}, u32[]{:S(2)}, u32[]{:S(2)}) collective-permute-start(bf16[128,128]{1,0:T(8,128)(2,1)S(1)} %copy-done.9), channel_id=1, source_target_pairs={{24,0},{48,24},{72,48},{96,72},{120,96},{144,120},{168,144},{192,1... | collective-permute-start | bytes 98312 | tf_op jit(solution)/shard_map/ppermute | solution.py:272
  28.8 13.7 %all-to-all-done.incoming = bf16[32,136,128]{2,1,0:T(8,128)(2,1)S(1)} async-done(((bf16[32,136,128]{2,1,0:T(8,128)(2,1)}), bf16[32,136,128]{2,1,0:T(8,128)(2,1)S(1)}, u32[]{:S(2)}, u32[]{:S(2)}) %all-to-all-start) | async-done | bytes 1114144 | tf_op jit(solution)/shard_map/all_to_all | solution.py:236
  42.5 0.6 broadcast_in_dim.16
  43.2 7.7 %all-to-all-start.1 = ((bf16[32,8,128]{2,1,0:T(8,128)(2,1)}), bf16[32,8,128]{2,1,0:T(8,128)(2,1)S(1)}, u32[]{:S(2)}, u32[]{:S(2)}) async-start(bf16[32,8,128]{2,1,0:T(8,128)(2,1)} %broadcast_in_dim.16), calls=%async_computation.1 | async-start | bytes 131072 | tf_op jit(solution)/shard_map/all_to_all | solution.py:236
  51.2 2.7 %near.1 = (f32[8,64,384]{2,1,0:T(8,128)S(1)}, f32[8,64,128]{2,1,0:T(8,128)S(1)}, f32[8,64,128]{2,1,0:T(8,128)S(1)}, f32[8,64,128]{2,1,0:T(8,128)S(1)}) custom-call(s32[8,3]{1,0:T(8,128)S(1)} %copy.17.rand, s32[2]{0:T(128)S(1)} %pad_add_fusion.me, bf16[8,64,128]{2,1,0:T(8,128)(2,1)S(1)} %bitcast.22, bf16[8,64,128]{2,1,0:T(8,128)(2,1)S(1)} %bitcast.17, ...), custom_call_target="tpu_custom_call" | custom-call | tf_op jit(solution)/shard_map/near/pallas_call | solution.py:279
  54.0 5.8 %all-to-all-done.1 = bf16[32,8,128]{2,1,0:T(8,128)(2,1)S(1)} async-done(((bf16[32,8,128]{2,1,0:T(8,128)(2,1)}), bf16[32,8,128]{2,1,0:T(8,128)(2,1)S(1)}, u32[]{:S(2)}, u32[]{:S(2)}) %all-to-all-start.1) | async-done | bytes 65568 | tf_op jit(solution)/shard_map/all_to_all | solution.py:236
  59.7 1.1 forward.1
  60.9 25.5 %all_to_all.25.parts = f32[24,1,512]{2,1,0:T(1,128)S(1)} all-to-all(f32[24,1,512]{2,1,0:T(1,128)S(1)} %get-tuple-element.35), channel_id=1, replica_groups=mesh['seq'=32,'head'=24] {'head'}, dimensions={0} | all-to-all | bytes 98304 | tf_op jit(solution)/shard_map/all_to_all | solution.py:236
  86.4 3.9 %backward.1 = (f32[8,64,128]{2,1,0:T(8,128)}, f32[8,64,128]{2,1,0:T(8,128)S(1)}, f32[8,64,128]{2,1,0:T(8,128)S(1)}, bf16[32,136,128]{2,1,0:T(8,128)(2,1)}, bf16[...) custom-call(s32[8,3]{1,0:T(8,128)S(1)} %copy.17.rand, f32[24,1,512]{2,1,0:T(1,128)S(1)} %all_to_all.25.parts, ...), custom_call_target="tpu_custom_call" | custom-call | tf_op jit(solution)/shard_map/backward/pallas_call | solution.py:288
  90.2 5.2 %all-to-all-start.3 = ((bf16[32,136,128]{2,1,0:T(8,128)(2,1)}), bf16[32,136,128]{2,1,0:T(8,128)(2,1)S(1)}, u32[]{:S(2)}, u32[]{:S(2)}) async-start(bf16[32,136,128]{2,1,0:T(8,128)(2,1)} %get-tuple-element.41), calls=%async_computation.3 | async-start | bytes 2228224 | tf_op jit(solution)/shard_map/all_to_all | solution.py:236
  95.4 3.4 %collective-permute-start.2 = (bf16[128,128]{1,0:T(8,128)(2,1)S(1)}, bf16[128,128]{1,0:T(8,128)(2,1)S(1)}, u32[]{:S(2)}, u32[]{:S(2)}) collective-permute-start(bf16[128,128]{1,0:T(8,128)(2,1)S(1)} %get-tuple-element.42), channel_id=1, source_target_pairs={{0,24},{24,48},{48,72},{72,96},{96,120},{120,144},{144,168},{168,1... | collective-permute-start | bytes 98312 | tf_op jit(solution)/shard_map/ppermute | solution.py:296
  98.8 4.6 %collective-permute-start.3 = (bf16[128,128]{1,0:T(8,128)(2,1)S(1)}, bf16[128,128]{1,0:T(8,128)(2,1)S(1)}, u32[]{:S(2)}, u32[]{:S(2)}) collective-permute-start(bf16[128,128]{1,0:T(8,128)(2,1)S(1)} %get-tuple-element.43), channel_id=1, source_target_pairs={{24,0},{48,24},{72,48},{96,72},{120,96},{144,120},{168,144},{192,1... | collective-permute-start | bytes 98312 | tf_op jit(solution)/shard_map/ppermute | solution.py:297
  103.5 20.8 %all-to-all-done.3.back = bf16[32,136,128]{2,1,0:T(8,128)(2,1)S(1)} async-done(((bf16[32,136,128]{2,1,0:T(8,128)(2,1)}), bf16[32,136,128]{2,1,0:T(8,128)(2,1)S(1)}, u32[]{:S(2)}, u32[]{:S(2)}) %all-to-all-start.3) | async-done | bytes 1114144 | tf_op jit(solution)/shard_map/all_to_all | solution.py:236
  124.3 0.6 broadcast_in_dim.17
  124.9 7.2 %all-to-all-start.4 = ((bf16[32,8,128]{2,1,0:T(8,128)(2,1)}), bf16[32,8,128]{2,1,0:T(8,128)(2,1)S(1)}, u32[]{:S(2)}, u32[]{:S(2)}) async-start(bf16[32,8,128]{2,1,0:T(8,128)(2,1)} %broadcast_in_dim.17), calls=%async_computation.4 | async-start | bytes 131072 | tf_op jit(solution)/shard_map/all_to_all | solution.py:236
  132.1 0.6 fusion.4
  132.7 1.7 %gather.1 = (f32[8,64,128]{2,1,0:T(8,128)}, f32[8,64,128]{2,1,0:T(8,128)}, f32[4,64,128]{2,1,0:T(8,128)S(1)}) custom-call(s32[32]{0:T(128)S(1)} %copy-done.5, s32[2]{0:T(128)S(1)} %copy-done.6, f32[8,64,128]{2,1,0:T(8,128)S(1)} %get-tuple-element.39.acc_k, f32[8,64,128]{2,1,0:T(8,128)S(1)} %get-tuple-element.40.acc_v, ...), custom_call_target="tpu_custom_call" | custom-call | tf_op jit(solution)/shard_map/gather/pallas_call | solution.py:307
  134.4 6.6 %all-to-all-done.4 = bf16[32,8,128]{2,1,0:T(8,128)(2,1)S(1)} async-done(((bf16[32,8,128]{2,1,0:T(8,128)(2,1)}), bf16[32,8,128]{2,1,0:T(8,128)(2,1)S(1)}, u32[]{:S(2)}, u32[]{:S(2)}) %all-to-all-start.4) | async-done | bytes 65568 | tf_op jit(solution)/shard_map/all_to_all | solution.py:236
  141.0 0.6 final.1
  (34 shorter events, 1.1 us)
Async XLA Ops:
  4.2 13.4 %copy-start.10 = (bf16[128,128]{1,0:T(8,128)(2,1)S(1)}, bf16[128,128]{1,0:T(8,128)(2,1)}, u32[]{:S(2)}) copy-start(bf16[128,128]{1,0:T(8,128)(2,1)} %get-tuple-element.28) | copy-start | bytes 98308
  4.2 16.8 %copy-start.9 = (bf16[128,128]{1,0:T(8,128)(2,1)S(1)}, bf16[128,128]{1,0:T(8,128)(2,1)}, u32[]{:S(2)}) copy-start(bf16[128,128]{1,0:T(8,128)(2,1)} %get-tuple-element.29) | copy-start | bytes 98308
  4.2 21.4 %copy-start.6 = (s32[2]{0:T(128)S(1)}, s32[2]{0:T(128)}, u32[]{:S(2)}) copy-start(s32[2]{0:T(128)} %glob.5) | copy-start | bytes 28
  4.2 46.7 %copy-start.8 = (s32[256,3]{0,1:T(4,128)S(1)}, s32[256,3]{0,1:T(4,128)}, u32[]{:S(2)}) copy-start(s32[256,3]{0,1:T(4,128)} %param.14) | copy-start | bytes 9220
  4.2 47.0 %copy-start = (bf16[512,128]{1,0:T(8,128)(2,1)S(1)}, bf16[512,128]{1,0:T(8,128)(2,1)}, u32[]{:S(2)}) copy-start(bf16[512,128]{1,0:T(8,128)(2,1)} %param.9) | copy-start | bytes 393220
  4.2 47.0 %copy-start.1 = (bf16[512,128]{1,0:T(8,128)(2,1)S(1)}, bf16[512,128]{1,0:T(8,128)(2,1)}, u32[]{:S(2)}) copy-start(bf16[512,128]{1,0:T(8,128)(2,1)} %param.10) | copy-start | bytes 393220
  4.2 47.0 %copy-start.2 = (bf16[512,128]{1,0:T(8,128)(2,1)S(1)}, bf16[512,128]{1,0:T(8,128)(2,1)}, u32[]{:S(2)}) copy-start(bf16[512,128]{1,0:T(8,128)(2,1)} %param.8) | copy-start | bytes 393220
  4.2 38.3 %all-to-all-start = ((bf16[32,136,128]{2,1,0:T(8,128)(2,1)}), bf16[32,136,128]{2,1,0:T(8,128)(2,1)S(1)}, u32[]{:S(2)}, u32[]{:S(2)}) async-start(bf16[32,136,128]{2,1,0:T(8,128)(2,1)} %get-tuple-element.27), calls=%async_computation | async-start | bytes 2228224 | tf_op jit(solution)/shard_map/all_to_all | solution.py:236
  17.6 42.2 %copy-start.7 = (bf16[128]{0:T(256)(128)(2,1)S(1)}, bf16[128]{0:T(256)(128)(2,1)}, u32[]{:S(2)}) copy-start(bf16[128]{0:T(256)(128)(2,1)} %param.12) | copy-start | bytes 772
  17.6 33.6 %collective-permute-start = (bf16[128,128]{1,0:T(8,128)(2,1)S(1)}, bf16[128,128]{1,0:T(8,128)(2,1)S(1)}, u32[]{:S(2)}, u32[]{:S(2)}) collective-permute-start(bf16[128,128]{1,0:T(8,128)(2,1)S(1)} %copy-done.10), channel_id=1, source_target_pairs={{0,24},{24,48},{48,72},{72,96},{96,120},{120,144},{144,168},{168,1... | collective-permute-start | bytes 98312 | tf_op jit(solution)/shard_map/ppermute | solution.py:271
  21.0 30.2 %collective-permute-start.1 = (bf16[128,128]{1,0:T(8,128)(2,1)S(1)}, bf16[128,128]{1,0:T(8,128)(2,1)S(1)}, u32[]{:S(2)}, u32[]{:S(2)}) collective-permute-start(bf16[128,128]{1,0:T(8,128)(2,1)S(1)} %copy-done.9), channel_id=1, source_target_pairs={{24,0},{48,24},{72,48},{96,72},{120,96},{144,120},{168,144},{192,1... | collective-permute-start | bytes 98312 | tf_op jit(solution)/shard_map/ppermute | solution.py:272
  43.2 16.6 %all-to-all-start.1 = ((bf16[32,8,128]{2,1,0:T(8,128)(2,1)}), bf16[32,8,128]{2,1,0:T(8,128)(2,1)S(1)}, u32[]{:S(2)}, u32[]{:S(2)}) async-start(bf16[32,8,128]{2,1,0:T(8,128)(2,1)} %broadcast_in_dim.16), calls=%async_computation.1 | async-start | bytes 131072 | tf_op jit(solution)/shard_map/all_to_all | solution.py:236
  53.9 32.5 %copy-start.3 = (bf16[512,128]{1,0:T(8,128)(2,1)S(1)}, bf16[512,128]{1,0:T(8,128)(2,1)}, u32[]{:S(2)}) copy-start(bf16[512,128]{1,0:T(8,128)(2,1)} %param.11) | copy-start | bytes 393220
  53.9 32.4 %copy-start.4 = (s32[512]{0:T(512)S(1)}, s32[512]{0:T(512)}, u32[]{:S(2)}) copy-start(s32[512]{0:T(512)} %param.13) | copy-start | bytes 6148
  90.2 42.5 %copy-start.5 = (s32[32]{0:T(128)S(1)}, s32[32]{0:T(128)}, u32[]{:S(2)}) copy-start(s32[32]{0:T(128)} %reduce_max.19.pick) | copy-start | bytes 388
  90.2 34.0 %all-to-all-start.3 = ((bf16[32,136,128]{2,1,0:T(8,128)(2,1)}), bf16[32,136,128]{2,1,0:T(8,128)(2,1)S(1)}, u32[]{:S(2)}, u32[]{:S(2)}) async-start(bf16[32,136,128]{2,1,0:T(8,128)(2,1)} %get-tuple-element.41), calls=%async_computation.3 | async-start | bytes 2228224 | tf_op jit(solution)/shard_map/all_to_all | solution.py:236
  95.4 37.3 %collective-permute-start.2 = (bf16[128,128]{1,0:T(8,128)(2,1)S(1)}, bf16[128,128]{1,0:T(8,128)(2,1)S(1)}, u32[]{:S(2)}, u32[]{:S(2)}) collective-permute-start(bf16[128,128]{1,0:T(8,128)(2,1)S(1)} %get-tuple-element.42), channel_id=1, source_target_pairs={{0,24},{24,48},{48,72},{72,96},{96,120},{120,144},{144,168},{168,1... | collective-permute-start | bytes 98312 | tf_op jit(solution)/shard_map/ppermute | solution.py:296
  98.8 33.9 %collective-permute-start.3 = (bf16[128,128]{1,0:T(8,128)(2,1)S(1)}, bf16[128,128]{1,0:T(8,128)(2,1)S(1)}, u32[]{:S(2)}, u32[]{:S(2)}) collective-permute-start(bf16[128,128]{1,0:T(8,128)(2,1)S(1)} %get-tuple-element.43), channel_id=1, source_target_pairs={{24,0},{48,24},{72,48},{96,72},{120,96},{144,120},{168,144},{192,1... | collective-permute-start | bytes 98312 | tf_op jit(solution)/shard_map/ppermute | solution.py:297
  124.9 16.1 %all-to-all-start.4 = ((bf16[32,8,128]{2,1,0:T(8,128)(2,1)}), bf16[32,8,128]{2,1,0:T(8,128)(2,1)S(1)}, u32[]{:S(2)}, u32[]{:S(2)}) async-start(bf16[32,8,128]{2,1,0:T(8,128)(2,1)} %broadcast_in_dim.17), calls=%async_computation.4 | async-start | bytes 131072 | tf_op jit(solution)/shard_map/all_to_all | solution.py:236

commit v8 on v7

--- a/solution.py
+++ b/solution.py
@@ -62,7 +62,7 @@
     last[BLOCK:] = v[blocks - 1]
 
 
-def near_slots(i, base, local, prev, after, incoming, rand, blocks):
+def near_slots(i, base, local, prev, after, incoming, rand, blocks, tail=()):
     parts = [
         local[i - 1] if i > 0 else prev[base : base + BLOCK],
         local[i],
@@ -70,7 +70,7 @@
     ]
     for j in range(RAND):
         parts.append(incoming[rand[i, j] // blocks, base : base + BLOCK])
-    return jnp.concatenate(parts, axis=0)
+    return jnp.concatenate(parts + list(tail), axis=0)
 
 
 def global_slots(base, shared):
@@ -123,6 +123,9 @@
     a = a.astype(jnp.bfloat16)
     attended[...] = a.reshape(blocks, BLOCK, head_dim)
     row = mm(w8, a, NT)[:1]
+    row = jnp.concatenate(
+        [row[:, lo : lo + head_dim] for lo in range(0, row.shape[1], head_dim)], axis=0
+    )
     for r in range(part.shape[0]):
         part[r] = row
 
@@ -136,6 +139,7 @@
     inv_sqrt = 1.0 / math.sqrt(head_dim)
     bf16 = jnp.bfloat16
     logits = jnp.sum(parts[...], axis=0)
+    logits = jnp.concatenate([logits[n : n + 1] for n in range(logits.shape[0])], axis=1)
     slope = lax.logistic(logits) - labels[...].astype(jnp.float32)
     column = jnp.transpose(jnp.broadcast_to(slope, (8, slope.shape[1])))[:, :1]
     w = weight[...].astype(jnp.float32)
@@ -146,12 +150,10 @@
     none = jnp.zeros((BLOCK, head_dim), bf16)
     own = []
     for i in range(blocks):
-        kk = near_slots(i, 0, k, prev, after, incoming, rand, blocks)
-        kk = jnp.concatenate([kk, gk], axis=0)
+        kk = near_slots(i, 0, k, prev, after, incoming, rand, blocks, [gk])
         d = column[i * BLOCK : (i + 1) * BLOCK]
         g = (upstream[i].astype(jnp.float32) + d * w).astype(bf16)
-        vv = near_slots(i, BLOCK, v, prev, after, incoming, rand, blocks)
-        vv = jnp.concatenate([vv, gv], axis=0)
+        vv = near_slots(i, BLOCK, v, prev, after, incoming, rand, blocks, [gv])
         p = probs[i]
         dp = mm(g, vv, NT)
         dot = jnp.sum(g.astype(jnp.float32) * mean[i], axis=1, keepdims=True)
@@ -281,7 +283,7 @@
     )(rand, me, q, k, v, prev, after, incoming)
     full = (blocks, BLOCK, keys)
     attended, mean, probs, part = call(
-        forward_kernel, "forward", 0, 7, [(acc3, bf16), (acc3, f32), (full, f32), ((heads, 1, tokens), f32)]
+        forward_kernel, "forward", 0, 7, [(acc3, bf16), (acc3, f32), (full, f32), ((heads, tokens // head_dim, head_dim), f32)]
     )(q, shared, weight, terms, out, peak, total)
     parts = exchange(part, "head")
 
@@ -299,7 +301,7 @@
     gtotal = exchange(jnp.broadcast_to(gsum, (shards, CHUNK, head_dim)), "seq")
     gtotal = gtotal.reshape(GLOBAL * wide, head_dim)
 
-    logits = jnp.sum(parts, axis=(0, 1))
+    logits = jnp.sum(parts, axis=0).reshape(tokens)
     token_loss = jax.nn.softplus(logits) - labels.astype(f32) * logits
 
     anywhere = pl.BlockSpec(memory_space=pl.ANY)

time: 143 us -> 142 us (level)
  the two profiles are of different devices: /device:TPU:2 before, /device:TPU:8 now
where the time goes in v8:
time: 142 us
  waiting for transfers between devices  54.6 us (38%)
  starting transfers between devices  41.8 us (29%)
  blocking collectives  25.5 us (18%)
  Pallas kernels  12.1 us (9%)
  between operations  3.47 us (2%)
  local copies, waits for them, and re-layouts  2.17 us (2%)
  other arithmetic  2.1 us (1%)
    all_to_all x4, waiting for transfers between devices, exchange(): return lax.all_to_all(x, axis, split_axis=0, concat_axis=0, tiled=True)  54.6 us
    all_to_all x4, starting transfers between devices, exchange(): return lax.all_to_all(x, axis, split_axis=0, concat_axis=0, tiled=True)  30.1 us
    all_to_all x1, blocking collectives, exchange(): return lax.all_to_all(x, axis, split_axis=0, concat_axis=0, tiled=True)  25.5 us
    pallas_call x1, Pallas kernels, body(): call(backward_kernel, 'backward', 1, 13, [(acc3, f32), (acc3, f32), (acc3...  3.85 us
    ppermute x1, starting transfers between devices, body(): prev = lax.ppermute(last, 'seq', ups)  3.38 us
    ppermute x1, starting transfers between devices, body(): from_prev = lax.ppermute(to_next, 'seq', ups)  3.38 us
  transfers between devices with their start and end apart: 8, of which 4 were waited for; matrix products, arithmetic and copies ran while one was open for 2% of the time, Pallas kernels for 3%

profile of v8, /device:TPU:8, one launch (start us, length us, event | category | flops | bytes accessed | tf_op | source)
XLA Modules:
  0.0 141.7 jit_solution(10748725103139684969)
XLA Ops:
  0.6 0.7 fusion.2
  1.4 0.6 reduce_max.19.pick
  2.1 2.1 %pack.1 = (bf16[32,136,128]{2,1,0:T(8,128)(2,1)}, bf16[128,128]{1,0:T(8,128)(2,1)}, bf16[128,128]{1,0:T(8,128)(2,1)}) custom-call(s32[32]{0:T(128)} %reduce_max.19.pick, s32[2]{0:T(128)} %glob.5, bf16[8,64,128]{2,1,0:T(8,128)(2,1)} %bitcast.35, bf16[8,64,128]{2,1,0:T(8,128)(2,1)} %bitcast.38), custom_call_target="tpu_custom_call" | custom-call | tf_op jit(solution)/shard_map/pack/pallas_call | solution.py:267
  4.2 13.2 %all-to-all-start = ((bf16[32,136,128]{2,1,0:T(8,128)(2,1)}), bf16[32,136,128]{2,1,0:T(8,128)(2,1)S(1)}, u32[]{:S(2)}, u32[]{:S(2)}) async-start(bf16[32,136,128]{2,1,0:T(8,128)(2,1)} %get-tuple-element.27), calls=%async_computation | async-start | bytes 2228224 | tf_op jit(solution)/shard_map/all_to_all | solution.py:238
  17.4 3.4 %collective-permute-start = (bf16[128,128]{1,0:T(8,128)(2,1)S(1)}, bf16[128,128]{1,0:T(8,128)(2,1)S(1)}, u32[]{:S(2)}, u32[]{:S(2)}) collective-permute-start(bf16[128,128]{1,0:T(8,128)(2,1)S(1)} %copy-done.10), channel_id=1, source_target_pairs={{0,24},{24,48},{48,72},{72,96},{96,120},{120,144},{144,168},{168,1... | collective-permute-start | bytes 98312 | tf_op jit(solution)/shard_map/ppermute | solution.py:273
  20.8 2.5 %collective-permute-start.1 = (bf16[128,128]{1,0:T(8,128)(2,1)S(1)}, bf16[128,128]{1,0:T(8,128)(2,1)S(1)}, u32[]{:S(2)}, u32[]{:S(2)}) collective-permute-start(bf16[128,128]{1,0:T(8,128)(2,1)S(1)} %copy-done.9), channel_id=1, source_target_pairs={{24,0},{48,24},{72,48},{96,72},{120,96},{144,120},{168,144},{192,1... | collective-permute-start | bytes 98312 | tf_op jit(solution)/shard_map/ppermute | solution.py:274
  26.5 18.2 %all-to-all-done.incoming = bf16[32,136,128]{2,1,0:T(8,128)(2,1)S(1)} async-done(((bf16[32,136,128]{2,1,0:T(8,128)(2,1)}), bf16[32,136,128]{2,1,0:T(8,128)(2,1)S(1)}, u32[]{:S(2)}, u32[]{:S(2)}) %all-to-all-start) | async-done | bytes 1114144 | tf_op jit(solution)/shard_map/all_to_all | solution.py:238
  44.8 0.6 broadcast_in_dim.16
  45.4 5.4 %all-to-all-start.1 = ((bf16[32,8,128]{2,1,0:T(8,128)(2,1)}), bf16[32,8,128]{2,1,0:T(8,128)(2,1)S(1)}, u32[]{:S(2)}, u32[]{:S(2)}) async-start(bf16[32,8,128]{2,1,0:T(8,128)(2,1)} %broadcast_in_dim.16), calls=%async_computation.1 | async-start | bytes 131072 | tf_op jit(solution)/shard_map/all_to_all | solution.py:238
  51.1 2.7 %near.1 = (f32[8,64,384]{2,1,0:T(8,128)S(1)}, f32[8,64,128]{2,1,0:T(8,128)S(1)}, f32[8,64,128]{2,1,0:T(8,128)S(1)}, f32[8,64,128]{2,1,0:T(8,128)S(1)}) custom-call(s32[8,3]{1,0:T(8,128)S(1)} %copy.17.rand, s32[2]{0:T(128)S(1)} %pad_add_fusion.me, bf16[8,64,128]{2,1,0:T(8,128)(2,1)S(1)} %bitcast.41, bf16[8,64,128]{2,1,0:T(8,128)(2,1)S(1)} %bitcast.36, ...), custom_call_target="tpu_custom_call" | custom-call | tf_op jit(solution)/shard_map/near/pallas_call | solution.py:281
  53.9 6.1 %all-to-all-done.1 = bf16[32,8,128]{2,1,0:T(8,128)(2,1)S(1)} async-done(((bf16[32,8,128]{2,1,0:T(8,128)(2,1)}), bf16[32,8,128]{2,1,0:T(8,128)(2,1)S(1)}, u32[]{:S(2)}, u32[]{:S(2)}) %all-to-all-start.1) | async-done | bytes 65568 | tf_op jit(solution)/shard_map/all_to_all | solution.py:238
  59.9 1.1 forward.1
  61.1 25.5 %all_to_all.25.parts = f32[24,4,128]{2,1,0:T(4,128)S(1)} all-to-all(f32[24,4,128]{2,1,0:T(4,128)S(1)} %get-tuple-element.35), channel_id=1, replica_groups=mesh['seq'=32,'head'=24] {'head'}, dimensions={0} | all-to-all | bytes 98304 | tf_op jit(solution)/shard_map/all_to_all | solution.py:238
  86.6 3.9 %backward.1 = (f32[8,64,128]{2,1,0:T(8,128)}, f32[8,64,128]{2,1,0:T(8,128)S(1)}, f32[8,64,128]{2,1,0:T(8,128)S(1)}, bf16[32,136,128]{2,1,0:T(8,128)(2,1)}, bf16[...) custom-call(s32[8,3]{1,0:T(8,128)S(1)} %copy.17.rand, f32[24,4,128]{2,1,0:T(4,128)S(1)} %all_to_all.25.parts, ...), custom_call_target="tpu_custom_call" | custom-call | tf_op jit(solution)/shard_map/backward/pallas_call | solution.py:290
  90.4 4.9 %all-to-all-start.3 = ((bf16[32,136,128]{2,1,0:T(8,128)(2,1)}), bf16[32,136,128]{2,1,0:T(8,128)(2,1)S(1)}, u32[]{:S(2)}, u32[]{:S(2)}) async-start(bf16[32,136,128]{2,1,0:T(8,128)(2,1)} %get-tuple-element.41), calls=%async_computation.3 | async-start | bytes 2228224 | tf_op jit(solution)/shard_map/all_to_all | solution.py:238
  95.3 3.4 %collective-permute-start.2 = (bf16[128,128]{1,0:T(8,128)(2,1)S(1)}, bf16[128,128]{1,0:T(8,128)(2,1)S(1)}, u32[]{:S(2)}, u32[]{:S(2)}) collective-permute-start(bf16[128,128]{1,0:T(8,128)(2,1)S(1)} %get-tuple-element.42), channel_id=1, source_target_pairs={{0,24},{24,48},{48,72},{72,96},{96,120},{120,144},{144,168},{168,1... | collective-permute-start | bytes 98312 | tf_op jit(solution)/shard_map/ppermute | solution.py:298
  98.7 2.5 %collective-permute-start.3 = (bf16[128,128]{1,0:T(8,128)(2,1)S(1)}, bf16[128,128]{1,0:T(8,128)(2,1)S(1)}, u32[]{:S(2)}, u32[]{:S(2)}) collective-permute-start(bf16[128,128]{1,0:T(8,128)(2,1)S(1)} %get-tuple-element.43), channel_id=1, source_target_pairs={{24,0},{48,24},{72,48},{96,72},{120,96},{144,120},{168,144},{192,1... | collective-permute-start | bytes 98312 | tf_op jit(solution)/shard_map/ppermute | solution.py:299
  101.2 23.5 %all-to-all-done.3.back = bf16[32,136,128]{2,1,0:T(8,128)(2,1)S(1)} async-done(((bf16[32,136,128]{2,1,0:T(8,128)(2,1)}), bf16[32,136,128]{2,1,0:T(8,128)(2,1)S(1)}, u32[]{:S(2)}, u32[]{:S(2)}) %all-to-all-start.3) | async-done | bytes 1114144 | tf_op jit(solution)/shard_map/all_to_all | solution.py:238
  124.8 0.6 broadcast_in_dim.17
  125.4 6.6 %all-to-all-start.4 = ((bf16[32,8,128]{2,1,0:T(8,128)(2,1)}), bf16[32,8,128]{2,1,0:T(8,128)(2,1)S(1)}, u32[]{:S(2)}, u32[]{:S(2)}) async-start(bf16[32,8,128]{2,1,0:T(8,128)(2,1)} %broadcast_in_dim.17), calls=%async_computation.4 | async-start | bytes 131072 | tf_op jit(solution)/shard_map/all_to_all | solution.py:238
  132.0 0.6 fusion.4
  132.6 1.7 %gather.1 = (f32[8,64,128]{2,1,0:T(8,128)}, f32[8,64,128]{2,1,0:T(8,128)}, f32[4,64,128]{2,1,0:T(8,128)S(1)}) custom-call(s32[32]{0:T(128)S(1)} %copy-done.5, s32[2]{0:T(128)S(1)} %copy-done.6, f32[8,64,128]{2,1,0:T(8,128)S(1)} %get-tuple-element.39.acc_k, f32[8,64,128]{2,1,0:T(8,128)S(1)} %get-tuple-element.40.acc_v, ...), custom_call_target="tpu_custom_call" | custom-call | tf_op jit(solution)/shard_map/gather/pallas_call | solution.py:309
  134.4 6.8 %all-to-all-done.4 = bf16[32,8,128]{2,1,0:T(8,128)(2,1)S(1)} async-done(((bf16[32,8,128]{2,1,0:T(8,128)(2,1)}), bf16[32,8,128]{2,1,0:T(8,128)(2,1)S(1)}, u32[]{:S(2)}, u32[]{:S(2)}) %all-to-all-start.4) | async-done | bytes 65568 | tf_op jit(solution)/shard_map/all_to_all | solution.py:238
  141.1 0.6 final.1
  (34 shorter events, 1.0 us)
Async XLA Ops:
  4.2 13.3 %copy-start.10 = (bf16[128,128]{1,0:T(8,128)(2,1)S(1)}, bf16[128,128]{1,0:T(8,128)(2,1)}, u32[]{:S(2)}) copy-start(bf16[128,128]{1,0:T(8,128)(2,1)} %get-tuple-element.28) | copy-start | bytes 98308
  4.2 16.7 %copy-start.9 = (bf16[128,128]{1,0:T(8,128)(2,1)S(1)}, bf16[128,128]{1,0:T(8,128)(2,1)}, u32[]{:S(2)}) copy-start(bf16[128,128]{1,0:T(8,128)(2,1)} %get-tuple-element.29) | copy-start | bytes 98308
  4.2 19.2 %copy-start.6 = (s32[2]{0:T(128)S(1)}, s32[2]{0:T(128)}, u32[]{:S(2)}) copy-start(s32[2]{0:T(128)} %glob.5) | copy-start | bytes 28
  4.2 46.6 %copy-start.8 = (s32[256,3]{0,1:T(4,128)S(1)}, s32[256,3]{0,1:T(4,128)}, u32[]{:S(2)}) copy-start(s32[256,3]{0,1:T(4,128)} %param.14) | copy-start | bytes 9220
  4.2 46.9 %copy-start = (bf16[512,128]{1,0:T(8,128)(2,1)S(1)}, bf16[512,128]{1,0:T(8,128)(2,1)}, u32[]{:S(2)}) copy-start(bf16[512,128]{1,0:T(8,128)(2,1)} %param.9) | copy-start | bytes 393220
  4.2 46.9 %copy-start.1 = (bf16[512,128]{1,0:T(8,128)(2,1)S(1)}, bf16[512,128]{1,0:T(8,128)(2,1)}, u32[]{:S(2)}) copy-start(bf16[512,128]{1,0:T(8,128)(2,1)} %param.10) | copy-start | bytes 393220
  4.2 46.9 %copy-start.2 = (bf16[512,128]{1,0:T(8,128)(2,1)S(1)}, bf16[512,128]{1,0:T(8,128)(2,1)}, u32[]{:S(2)}) copy-start(bf16[512,128]{1,0:T(8,128)(2,1)} %param.8) | copy-start | bytes 393220
  4.2 40.6 %all-to-all-start = ((bf16[32,136,128]{2,1,0:T(8,128)(2,1)}), bf16[32,136,128]{2,1,0:T(8,128)(2,1)S(1)}, u32[]{:S(2)}, u32[]{:S(2)}) async-start(bf16[32,136,128]{2,1,0:T(8,128)(2,1)} %get-tuple-element.27), calls=%async_computation | async-start | bytes 2228224 | tf_op jit(solution)/shard_map/all_to_all | solution.py:238
  17.4 42.5 %copy-start.7 = (bf16[128]{0:T(256)(128)(2,1)S(1)}, bf16[128]{0:T(256)(128)(2,1)}, u32[]{:S(2)}) copy-start(bf16[128]{0:T(256)(128)(2,1)} %param.12) | copy-start | bytes 772
  17.4 33.6 %collective-permute-start = (bf16[128,128]{1,0:T(8,128)(2,1)S(1)}, bf16[128,128]{1,0:T(8,128)(2,1)S(1)}, u32[]{:S(2)}, u32[]{:S(2)}) collective-permute-start(bf16[128,128]{1,0:T(8,128)(2,1)S(1)} %copy-done.10), channel_id=1, source_target_pairs={{0,24},{24,48},{48,72},{72,96},{96,120},{120,144},{144,168},{168,1... | collective-permute-start | bytes 98312 | tf_op jit(solution)/shard_map/ppermute | solution.py:273
  20.8 30.2 %collective-permute-start.1 = (bf16[128,128]{1,0:T(8,128)(2,1)S(1)}, bf16[128,128]{1,0:T(8,128)(2,1)S(1)}, u32[]{:S(2)}, u32[]{:S(2)}) collective-permute-start(bf16[128,128]{1,0:T(8,128)(2,1)S(1)} %copy-done.9), channel_id=1, source_target_pairs={{24,0},{48,24},{72,48},{96,72},{120,96},{144,120},{168,144},{192,1... | collective-permute-start | bytes 98312 | tf_op jit(solution)/shard_map/ppermute | solution.py:274
  45.4 14.5 %all-to-all-start.1 = ((bf16[32,8,128]{2,1,0:T(8,128)(2,1)}), bf16[32,8,128]{2,1,0:T(8,128)(2,1)S(1)}, u32[]{:S(2)}, u32[]{:S(2)}) async-start(bf16[32,8,128]{2,1,0:T(8,128)(2,1)} %broadcast_in_dim.16), calls=%async_computation.1 | async-start | bytes 131072 | tf_op jit(solution)/shard_map/all_to_all | solution.py:238
  53.8 32.7 %copy-start.3 = (bf16[512,128]{1,0:T(8,128)(2,1)S(1)}, bf16[512,128]{1,0:T(8,128)(2,1)}, u32[]{:S(2)}) copy-start(bf16[512,128]{1,0:T(8,128)(2,1)} %param.11) | copy-start | bytes 393220
  53.8 32.7 %copy-start.4 = (s32[512]{0:T(512)S(1)}, s32[512]{0:T(512)}, u32[]{:S(2)}) copy-start(s32[512]{0:T(512)} %param.13) | copy-start | bytes 6148
  90.4 42.2 %copy-start.5 = (s32[32]{0:T(128)S(1)}, s32[32]{0:T(128)}, u32[]{:S(2)}) copy-start(s32[32]{0:T(128)} %reduce_max.19.pick) | copy-start | bytes 388
  90.4 34.3 %all-to-all-start.3 = ((bf16[32,136,128]{2,1,0:T(8,128)(2,1)}), bf16[32,136,128]{2,1,0:T(8,128)(2,1)S(1)}, u32[]{:S(2)}, u32[]{:S(2)}) async-start(bf16[32,136,128]{2,1,0:T(8,128)(2,1)} %get-tuple-element.41), calls=%async_computation.3 | async-start | bytes 2228224 | tf_op jit(solution)/shard_map/all_to_all | solution.py:238
  95.3 37.3 %collective-permute-start.2 = (bf16[128,128]{1,0:T(8,128)(2,1)S(1)}, bf16[128,128]{1,0:T(8,128)(2,1)S(1)}, u32[]{:S(2)}, u32[]{:S(2)}) collective-permute-start(bf16[128,128]{1,0:T(8,128)(2,1)S(1)} %get-tuple-element.42), channel_id=1, source_target_pairs={{0,24},{24,48},{48,72},{72,96},{96,120},{120,144},{144,168},{168,1... | collective-permute-start | bytes 98312 | tf_op jit(solution)/shard_map/ppermute | solution.py:298
  98.7 34.0 %collective-permute-start.3 = (bf16[128,128]{1,0:T(8,128)(2,1)S(1)}, bf16[128,128]{1,0:T(8,128)(2,1)S(1)}, u32[]{:S(2)}, u32[]{:S(2)}) collective-permute-start(bf16[128,128]{1,0:T(8,128)(2,1)S(1)} %get-tuple-element.43), channel_id=1, source_target_pairs={{24,0},{48,24},{72,48},{96,72},{120,96},{144,120},{168,144},{192,1... | collective-permute-start | bytes 98312 | tf_op jit(solution)/shard_map/ppermute | solution.py:299
  125.4 15.7 %all-to-all-start.4 = ((bf16[32,8,128]{2,1,0:T(8,128)(2,1)}), bf16[32,8,128]{2,1,0:T(8,128)(2,1)S(1)}, u32[]{:S(2)}, u32[]{:S(2)}) async-start(bf16[32,8,128]{2,1,0:T(8,128)(2,1)} %broadcast_in_dim.17), calls=%async_computation.4 | async-start | bytes 131072 | tf_op jit(solution)/shard_map/all_to_all | solution.py:238
